TPU v7x, 32 devices: a whole 2x2x4 slice. The times are simulated.
32 devices in a mesh: seq: 16 (over z, y, x), dp: 2 (over core).
Axes of the slice: x: 2, y: 2, z: 4, core: 2. Of those that a mesh axis runs over, the one named last changes fastest.
Arguments:
- queries: bfloat16 [2, 4096, 1024], P('dp', 'seq'), may hold values from -8 to 8
- keys: bfloat16 [2, 4096, 1024], P('dp', 'seq'), may hold values from -8 to 8
- values: bfloat16 [2, 4096, 1024], P('dp', 'seq'), may hold values from -6 to 6
- out_grad: bfloat16 [2, 4096, 1024], P('dp', 'seq'), may hold values from -6 to 6
- out_weight: bfloat16 [1024, 1024], replicated, may hold values from -0.1875 to 0.1875
Outputs:
- q_grad: bfloat16 [2, 4096, 1024], P('dp', 'seq')
- k_grad: bfloat16 [2, 4096, 1024], P('dp', 'seq')
- v_grad: bfloat16 [2, 4096, 1024], P('dp', 'seq')
- wo_grad: float32 [1024, 1024], P('seq', 'dp')
All inputs are finite; a program needn't handle non-finite values.
Results may differ from a plain program's by a relative error of at most 0.017.
Values may be sent and summed in bfloat16 or wider, within the bound.
No kernel may reach another device: no remote copies, remote signals or barrier semaphores. Data moves between devices by JAX's collectives and lax.ppermute only.
A program may use at most 64 MiB of HBM per device.

v0:
```python
import jax
import jax.numpy as jnp
from jax import lax
from jax.experimental import pallas as pl
from jax.experimental.pallas import tpu as pltpu
from jax.sharding import PartitionSpec as P


HEAD_DIM = 64
HALF = 128
PAIR = 2 * HEAD_DIM
UNROLL = 4
masked_score = -1e30
f32 = jnp.float32
bf16 = jnp.bfloat16


NN = ((1,), (0,))
NT = ((1,), (1,))
TN = ((0,), (0,))

in_vmem = pl.BlockSpec(memory_space=pltpu.VMEM)
in_smem = pl.BlockSpec(memory_space=pltpu.SMEM)


def contract(a, b, dims):
    return lax.dot_general(a, b, (dims, ((), ())), preferred_element_type=f32)


def half_kernel(meta_ref, bias_ref, q_ref, da_ref, k_ref, v_ref, rim_ref, *rest):
    earlier, outs = rest[:-6], rest[-6:]
    keep_ref, send_ref, dq_ref, dk_ref, dv_ref, back_ref = outs
    side = meta_ref[0]
    y_digit = meta_ref[1]
    scale = HEAD_DIM ** -0.5
    first_head = lax.broadcasted_iota(jnp.int32, (HALF, PAIR), 1) < HEAD_DIM
    ahead = lax.broadcasted_iota(jnp.int32, (HALF, 2 * HALF), 0) - lax.broadcasted_iota(jnp.int32, (HALF, 2 * HALF), 1) % HALF
    in_rim = ahead * (1 - 2 * side) >= side
    near_rows = pl.ds(pl.multiple_of(side * HALF, HALF), HALF)
    far_rows = pl.ds(pl.multiple_of((1 - side) * HALF, HALF), HALF)
    if earlier:
        dq_ref[far_rows, :] = earlier[0][far_rows, :]

    def one(pair, place, at_ref):
        cols = pl.ds(pl.multiple_of(pair * PAIR, PAIR), PAIR)
        q_one = q_ref[near_rows, cols].astype(f32) * scale
        da_one = da_ref[near_rows, cols].astype(f32)
        q_two = jnp.concatenate([jnp.where(first_head, q_one, 0.0), jnp.where(first_head, 0.0, q_one)], axis=0).astype(bf16)
        da_two = jnp.concatenate([jnp.where(first_head, da_one, 0.0), jnp.where(first_head, 0.0, da_one)], axis=0).astype(bf16)
        keys = jnp.concatenate([rim_ref[0, :, cols], k_ref[near_rows, cols], k_ref[far_rows, cols]], axis=0)
        vals = jnp.concatenate([rim_ref[1, :, cols], v_ref[near_rows, cols], v_ref[far_rows, cols]], axis=0)
        score = contract(keys, q_two, NT)
        s_edge = jnp.where(in_rim, score[:HALF] + bias_ref[0], score[2 * HALF :])
        s_near = score[HALF : 2 * HALF]
        top = jnp.max(jnp.maximum(s_edge, s_near), axis=0, keepdims=True)
        e_edge = jnp.exp(s_edge - top)
        e_near = jnp.exp(s_near - top)
        inv = 1.0 / jnp.sum(e_edge + e_near, axis=0, keepdims=True)
        p_edge = e_edge * inv
        p_near = e_near * inv
        p_all = jnp.concatenate([jnp.where(in_rim, p_edge, 0.0).astype(bf16), p_near.astype(bf16),
                                 jnp.where(in_rim, 0.0, p_edge).astype(bf16)], axis=0)
        dp = contract(vals, da_two, NT)
        d_edge = jnp.where(in_rim, dp[:HALF], dp[2 * HALF :])
        d_near = dp[HALF : 2 * HALF]
        delta = jnp.sum(p_edge * d_edge + p_near * d_near, axis=0, keepdims=True)
        ds_edge = p_edge * (d_edge - delta)
        ds_near = p_near * (d_near - delta)
        ds_all = jnp.concatenate([jnp.where(in_rim, ds_edge, 0.0).astype(bf16), ds_near.astype(bf16),
                                  jnp.where(in_rim, 0.0, ds_edge).astype(bf16)], axis=0)
        at = contract(vals, p_all, TN)
        start = pl.multiple_of(place * PAIR, PAIR)
        at_ref[pl.ds(start, HEAD_DIM), :] = at[:HEAD_DIM, :HALF].astype(bf16)
        at_ref[pl.ds(start + HEAD_DIM, HEAD_DIM), :] = at[HEAD_DIM:, HALF:].astype(bf16)
        dqt = contract(keys, ds_all, TN)
        dqt = jnp.concatenate([dqt[:HEAD_DIM, :HALF], dqt[HEAD_DIM:, HALF:]], axis=0) * scale
        dq_ref[near_rows, cols] = dqt.T.astype(bf16)
        for which, (ref, left, right) in enumerate(((dk_ref, ds_all, q_two), (dv_ref, p_all, da_two))):
            part = contract(left, right, NN)
            back_ref[which, :, cols] = part[:HALF].astype(bf16)
            near, far = part[HALF : 2 * HALF], part[2 * HALF :]
            if earlier:
                near = near + earlier[1 + which][near_rows, cols]
                far = far + earlier[1 + which][far_rows, cols]
            ref[near_rows, cols] = near
            ref[far_rows, cols] = far

    def body(place, carry):
        one(2 * place + y_digit, place, keep_ref)
        one(2 * place + 1 - y_digit, place, send_ref)
        return carry

    lax.fori_loop(0, q_ref.shape[1] // (2 * PAIR), body, 0, unroll=UNROLL)


def half_attention(meta, bias, q, da, k, v, rim, earlier):
    rows, width = q.shape
    operands = [meta, bias, q, da, k, v, rim] + (list(earlier) if earlier else [])
    return pl.pallas_call(
        half_kernel,
        in_specs=[in_smem, in_smem] + [in_vmem] * (len(operands) - 2),
        out_specs=[in_vmem] * 6,
        out_shape=[
            jax.ShapeDtypeStruct((width // 2, HALF), bf16),
            jax.ShapeDtypeStruct((width // 2, HALF), bf16),
            jax.ShapeDtypeStruct((rows, width), bf16),
            jax.ShapeDtypeStruct((rows, width), f32),
            jax.ShapeDtypeStruct((rows, width), f32),
            jax.ShapeDtypeStruct((2, HALF, width), bf16),
        ],
        cost_estimate=pl.CostEstimate(flops=12 * HALF * 3 * HALF * width, bytes_accessed=16 * rows * width,
                                      transcendentals=HALF * 2 * HALF * width // HEAD_DIM),
        compiler_params=pltpu.CompilerParams(vmem_limit_bytes=24 << 20),
    )(*operands)


def rim_kernel(side_ref, k_ref, v_ref, out_ref):
    out_ref[0] = k_ref[...]
    out_ref[1] = v_ref[...]


def packed_rim(side, k, v):
    width = k.shape[1]
    block = pl.BlockSpec((HALF, width), lambda i, s: (s[0], 0))
    return pl.pallas_call(
        rim_kernel,
        grid_spec=pltpu.PrefetchScalarGridSpec(
            num_scalar_prefetch=1, grid=(1,), in_specs=[block, block],
            out_specs=pl.BlockSpec((2, HALF, width), lambda i, s: (0, 0, 0)),
        ),
        out_shape=jax.ShapeDtypeStruct((2, HALF, width), bf16),
    )(side, k, v)


def product_kernel(meta_ref, *refs):
    side, mine, z_digit = meta_ref[0], meta_ref[2], meta_ref[3]
    ats, (g_ref, g_dp_ref, g_y_ref, g_y_dp_ref), outs = refs[:8], refs[8:12], refs[12:]
    own = outs[0].shape[1]
    size = outs[0].shape[0]
    rights = []
    for row in (side, 1 - side):
        rows = pl.ds(pl.multiple_of(row * HALF, HALF), HALF)
        cols = pl.ds(pl.multiple_of(mine * own, own), own)
        rights += [g_ref[rows, cols], g_y_ref[rows, cols], g_dp_ref[rows, :], g_y_dp_ref[rows, :]]
    right = jnp.concatenate(rights, axis=0)
    for step, out_ref in enumerate(outs):
        rows = pl.ds(pl.multiple_of((z_digit ^ step) * size, size), size)
        left = jnp.concatenate([ref[rows, :] for ref in ats], axis=1)
        out_ref[...] = contract(left, right, NN).astype(out_ref.dtype)


def products(meta, ats, gs, radix, own):
    size = ats[0].shape[0] // radix
    return pl.pallas_call(
        product_kernel,
        in_specs=[in_smem] + [in_vmem] * 12,
        out_specs=[in_vmem] * radix,
        out_shape=[jax.ShapeDtypeStruct((size, own), f32)] + [jax.ShapeDtypeStruct((size, own), bf16)] * (radix - 1),
        compiler_params=pltpu.CompilerParams(vmem_limit_bytes=12 << 20),
        name="product",
    )(meta, *ats, *gs)


def sum_kernel(meta_ref, own_ref, *refs):
    pieces, (keep_ref, send_ref) = refs[:-2], refs[-2:]
    half = keep_ref.shape[0]
    for x_digit, ref in ((meta_ref[4], keep_ref), (1 - meta_ref[4], send_ref)):
        rows = pl.ds(pl.multiple_of(x_digit * half, half), half)
        total = own_ref[rows, :]
        for piece in pieces:
            total = total + piece[rows, :].astype(f32)
        ref[...] = total.astype(ref.dtype)


def summed(meta, own, pieces):
    half = own.shape[0] // 2
    return pl.pallas_call(
        sum_kernel,
        in_specs=[in_smem] + [in_vmem] * (1 + len(pieces)),
        out_specs=[in_vmem] * 2,
        out_shape=[jax.ShapeDtypeStruct((half, own.shape[1]), f32), jax.ShapeDtypeStruct((half, own.shape[1]), bf16)],
        compiler_params=pltpu.CompilerParams(vmem_limit_bytes=12 << 20),
        name="summed",
    )(meta, own, *pieces)


def join_kernel(meta_ref, dk_ref, dv_ref, long_ref, near_ref, dk_out, dv_out):
    side = meta_ref[0]
    for row, rim in ((side, long_ref), (1 - side, near_ref)):
        rows = pl.ds(pl.multiple_of(row * HALF, HALF), HALF)
        dk_out[rows, :] = (dk_ref[rows, :] + rim[0].astype(f32)).astype(bf16)
        dv_out[rows, :] = (dv_ref[rows, :] + rim[1].astype(f32)).astype(bf16)


def joined(meta, dk, dv, from_long, from_near):
    shape = jax.ShapeDtypeStruct(dk.shape, bf16)
    return pl.pallas_call(
        join_kernel,
        in_specs=[in_smem] + [in_vmem] * 4,
        out_specs=[in_vmem] * 2,
        out_shape=[shape, shape],
        compiler_params=pltpu.CompilerParams(vmem_limit_bytes=12 << 20),
        name="joined",
    )(meta, dk, dv, from_long, from_near)


def swapped(value, stride, count):
    return lax.ppermute(value, "seq", [(i, i ^ stride) for i in range(count)])


def turned(value, count):
    return [lax.ppermute(value, "dp", [(i, (i + step) % count) for i in range(count)]) for step in range(1, count)]


def upper_stages(count):
    found = []
    stride = 4
    while stride < count:
        radix = min(4, count // stride)
        found.append((stride, radix))
        stride *= radix
    return found


def scattered_sum(block, strides, stages, me, count):
    tail = list(block.shape[-2:])
    left = strides
    for number, (stride, radix) in enumerate(stages):
        axis = [place for place, (low, size) in enumerate(left) if low <= stride < low * size][0]
        base, total = left[axis]
        inner = stride // base
        outer = total // (inner * radix)
        dims = [size for _, size in left]
        block = block.reshape(dims[:axis] + [outer, radix, inner] + dims[axis + 1 :] + tail)
        digit = (me // stride) % radix
        received = []
        for step in range(1, radix):
            pairs = [(source, source ^ (step * stride)) for source in range(count)]
            sent = lax.dynamic_index_in_dim(block, digit ^ step, axis + 1, keepdims=False)
            received.append(lax.ppermute(sent, "seq", pairs))
        total_sum = lax.dynamic_index_in_dim(block, digit, axis + 1, keepdims=False).astype(f32)
        for piece in received:
            total_sum = total_sum + piece.astype(f32)
        block = total_sum if number == len(stages) - 1 else total_sum.astype(bf16)
        left = left[:axis] + [(stride * radix, outer), (base, inner)] + left[axis + 1 :]
        keep = [(low, size) for low, size in left if size > 1]
        block = block.reshape([size for _, size in keep] + tail)
        left = keep
    return block.reshape(tail)


def on_device(queries, keys, values, out_grad, out_weight):
    q, k, v, g = queries[0], keys[0], values[0], out_grad[0]
    rows, width = q.shape
    assert rows == 2 * HALF
    count = lax.axis_size("seq")
    dp_count = lax.axis_size("dp")
    assert count >= 8 and count & (count - 1) == 0
    place = lax.axis_index("seq")
    mine = lax.axis_index("dp")
    odd = place % 2
    y_digit = (place // 2) % 2
    sides = (odd, 1 - odd)
    long_pairs = [(i, i + 1 if i % 2 else i - 1) for i in range(1, count - 1)]
    near_pairs = [(i, i ^ 1) for i in range(count)]
    block = width // count
    own_width = width // dp_count
    stages = upper_stages(count)
    direct = 2 * block == PAIR and len(stages) == 1 and dp_count == 2
    metas = [jnp.stack([side, y_digit if direct else 0 * y_digit, mine, place // 4 % stages[0][1], odd]).astype(jnp.int32) for side in sides]
    alone = [jnp.where(side == 0, place == 0, place == count - 1) for side in sides]
    bias = [jnp.where(one, masked_score, 0.0).astype(f32).reshape(1) for one in alone]

    rim1 = packed_rim(metas[0][:1], k, v)
    first_rim = lax.ppermute(rim1, "seq", long_pairs)
    dattn = contract(g, out_weight, NT).astype(bf16)
    rim2 = packed_rim(metas[1][:1], k, v)
    rim2, dattn = lax.optimization_barrier((rim2, dattn))
    second_rim = lax.ppermute(rim2, "seq", near_pairs)

    def other_half(array):
        return lax.dynamic_slice_in_dim(array, (mine + 1) % dp_count * own_width, own_width, 1)

    if direct:
        g_y = swapped(g, 2, count)
        g_dp = turned(other_half(g), dp_count)[0]
        g_y_dp = turned(other_half(g_y), dp_count)[0]
        gs = [g, g_dp, g_y, g_y_dp]

    keep1, send1, dq, dk, dv, back1 = half_attention(metas[0], bias[0], q, dattn, k, v, first_rim, None)
    from_long = lax.ppermute(back1, "seq", long_pairs)
    if direct:
        at_y1 = swapped(send1, 2, count)
        at_dp1 = turned(keep1, dp_count)[0]
        at_y_dp1 = turned(at_y1, dp_count)[0]
    keep2, send2, dq, dk, dv, back2 = half_attention(metas[1], bias[1], q, dattn, k, v, second_rim, (dq, dk, dv))
    if direct:
        at_y2 = swapped(send2, 2, count)
        at_dp2 = turned(keep2, dp_count)[0]
        at_y_dp2 = turned(at_y2, dp_count)[0]
    from_near = lax.ppermute(back2, "seq", near_pairs)

    frames = rows * count * dp_count
    if direct:
        ats = [keep1, at_y1, at_dp1, at_y_dp1, keep2, at_y2, at_dp2, at_y_dp2]
        terms = products(metas[0], ats, gs, count // 4, own_width)
        pieces = []
        for step in range(1, count // 4):
            pieces.append(swapped(terms[step], 4 * step, count))
        kept, sent = summed(metas[0], terms[0], pieces)
        wo_grad = kept + swapped(sent, 1, count).astype(f32)
    else:
        wo_grad = general_sum((keep1, send1), (keep2, send2), g, sides, place, mine, y_digit, count, dp_count)
    dk, dv = joined(metas[0], dk, dv, from_long, from_near)
    return dq[None], dk[None], dv[None], wo_grad * frames ** -0.5


def general_sum(first, second, g, sides, place, mine, y_digit, count, dp_count):
    width = g.shape[1]
    block = width // count
    own_width = width // dp_count
    g_parts = [lax.dynamic_slice_in_dim(g, mine * own_width, own_width, 1)]
    for step in range(1, dp_count):
        sent = lax.dynamic_slice_in_dim(g, (mine + step) % dp_count * own_width, own_width, 1)
        g_parts.append(lax.ppermute(sent, "dp", [(i, (i + step) % dp_count) for i in range(dp_count)]))
    g_here = jnp.stack(g_parts)
    g_there = swapped(g_here, 2, count)
    term = None
    for side, (even, odd) in zip(sides, (first, second)):
        at = jnp.stack([even.reshape(-1, PAIR, HALF), odd.reshape(-1, PAIR, HALF)], axis=1)
        parts = at.reshape(count // 4, 2, 2 * block, HALF)
        kept = lax.dynamic_index_in_dim(parts, y_digit, 1, keepdims=False).reshape(width // 2, HALF)
        sent = lax.dynamic_index_in_dim(parts, 1 - y_digit, 1, keepdims=False).reshape(width // 2, HALF)
        pack = jnp.stack([kept, swapped(sent, 2, count)])
        for utt, part in enumerate([pack] + turned(pack, dp_count)):
            for row, source in ((0, g_here), (1, g_there)):
                piece = contract(part[row], lax.dynamic_slice_in_dim(source[utt], side * HALF, HALF, 0), NN)
                term = piece if term is None else term + piece
    term = term.astype(bf16).reshape(count // 4, 2, block, own_width)
    return scattered_sum(term, [(4, count // 4), (1, 2)], upper_stages(count) + [(1, 2)], place, count)


def solution(mesh):
    spread = P("dp", "seq", None)
    return jax.shard_map(
        on_device,
        mesh=mesh,
        in_specs=(spread, spread, spread, spread, P()),
        out_specs=(spread, spread, spread, P("seq", "dp")),
        check_vma=False,
    )
```

profile of v0, /device:TPU:0, one launch (start us, length us, event | category | flops | bytes accessed | tf_op | source)
XLA Modules:
  0.0 83.1 jit_solution(2494648241662351770)
XLA Ops:
  0.6 0.0 copy-start
  0.7 2.0 %shard_map.85 = bf16[2,128,1024]{2,1,0:T(8,128)(2,1)} custom-call(s32[1]{0:T(128)} %bitcast.4.side_ref, bf16[256,1024]{1,0:T(8,128)(2,1)} %bitcast.19, bf16[256,1024]{1,0:T(8,128)(2,1)} %bitcast.23), custom_call_target="tpu_custom_call" | custom-call | tf_op jit(solution)/shard_map/pallas_call | solution.py:125
  2.7 0.0 copy-start.1
  2.7 0.0 copy-start.2
  2.7 1.6 %collective-permute-start.1 = (bf16[2,128,1024]{2,1,0:T(8,128)(2,1)}, bf16[2,128,1024]{2,1,0:T(8,128)(2,1)}, u32[]{:S(2)}, u32[]{:S(2)}) collective-permute-start(bf16[2,128,1024]{2,1,0:T(8,128)(2,1)} %shard_map.85), channel_id=1, source_target_pairs={{2,4},{4,2},{6,8},{8,6},{10,12},{12,10},{14,16},{16,14},{18,20},{2... | collective-permute-start | bytes 1572872 | tf_op jit(solution)/shard_map/ppermute | solution.py:275
  4.2 0.0 copy-done
  4.3 2.6 %convolution_convert_fusion.da_ref = bf16[256,1024]{1,0:T(8,128)(2,1)} fusion(bf16[1024,1024]{1,0:T(8,128)(2,1)S(1)} %copy-done, bf16[1,256,1024]{2,1,0:T(8,128)(2,1)} %param.8), kind=kOutput, calls=%fused_computation | convolution fusion | flops 537133056 | bytes 3145728 | tf_op jit(solution)/shard_map/dot_general | solution.py:27
  6.8 1.9 %shard_map.84 = bf16[2,128,1024]{2,1,0:T(8,128)(2,1)} custom-call(s32[1]{0:T(128)} %bitcast.side_ref, bf16[256,1024]{1,0:T(8,128)(2,1)} %bitcast.20, bf16[256,1024]{1,0:T(8,128)(2,1)} %bitcast.24), custom_call_target="tpu_custom_call" | custom-call | tf_op jit(solution)/shard_map/pallas_call | solution.py:125
  8.7 4.9 %collective-permute-start = (bf16[2,128,1024]{2,1,0:T(8,128)(2,1)}, bf16[2,128,1024]{2,1,0:T(8,128)(2,1)}, u32[]{:S(2)}, u32[]{:S(2)}) collective-permute-start(bf16[2,128,1024]{2,1,0:T(8,128)(2,1)} %shard_map.84), channel_id=1, source_target_pairs={{0,2},{2,0},{4,6},{6,4},{8,10},{10,8},{12,14},{14,12},{16,18},{18,... | collective-permute-start | bytes 1572872 | tf_op jit(solution)/shard_map/ppermute | solution.py:279
  13.6 1.5 %collective-permute-start.11 = (bf16[256,1024]{1,0:T(8,128)(2,1)}, bf16[256,1024]{1,0:T(8,128)(2,1)}, u32[]{:S(2)}, u32[]{:S(2)}) collective-permute-start(bf16[256,1024]{1,0:T(8,128)(2,1)} %bitcast.29), channel_id=1, source_target_pairs={{0,4},{2,6},{4,0},{6,2},{8,12},{10,14},{12,8},{14,10},{16,20},{18,... | collective-permute-start | bytes 1572872 | tf_op jit(solution)/shard_map/ppermute | solution.py:208
  15.1 1.7 %dynamic-slice_bitcast_fusion = bf16[256,512]{1,0:T(8,128)(2,1)} fusion(bf16[1,256,1024]{2,1,0:T(8,128)(2,1)} %param.8, s32[]{:T(128)S(6)} %select_n.59), kind=kLoop, calls=%fused_computation.1 | loop fusion | bytes 524292 | tf_op jit(solution)/shard_map/dynamic_slice | solution.py:282
  16.9 0.0 collective-permute-start.10
  16.9 0.1 stack.32.meta_ref
  17.0 0.1 stack.31.meta_ref
  17.0 0.0 collective-permute-done.1.rim_ref
  17.0 0.0 copy-done.1
  17.0 0.0 copy-done.2
  17.1 0.0 copy-start.3
  17.1 1.0 %copy-done.3 = bf16[1,256,1024]{2,1,0:T(8,128)(2,1)S(1)} copy-done((bf16[1,256,1024]{2,1,0:T(8,128)(2,1)S(1)}, bf16[1,256,1024]{2,1,0:T(8,128)(2,1)}, u32[]{:S(2)}) %copy-start.3) | copy-done | bytes 524312
  18.1 0.0 copy-start.5
  18.1 1.0 %copy-done.5 = bf16[256,1024]{1,0:T(8,128)(2,1)S(1)} copy-done((bf16[256,1024]{1,0:T(8,128)(2,1)S(1)}, bf16[256,1024]{1,0:T(8,128)(2,1)}, u32[]{:S(2)}) %copy-start.5) | copy-done | bytes 524312
  19.1 0.0 copy-start.4
  19.1 5.6 %shard_map.86 = (bf16[512,128]{1,0:T(8,128)(2,1)S(1)}, bf16[512,128]{1,0:T(8,128)(2,1)S(1)}, bf16[256,1024]{1,0:T(8,128)(2,1)S(1)}, f32[256,1024]{1,0:T(8,128)S(...) custom-call(s32[5]{0:T(128)S(1)} %stack.32.meta_ref, f32[1]{0:T(128)} %bitcast.10.bias_ref, ...), custom_call_target="tpu_custom_call" | custom-call | flops 603979776 | bytes 4194304 | tf_op jit(solution)/shard_map/pallas_call | solution.py:99
  24.7 7.6 %collective-permute-done.rim_ref = bf16[2,128,1024]{2,1,0:T(8,128)(2,1)} collective-permute-done((bf16[2,128,1024]{2,1,0:T(8,128)(2,1)}, bf16[2,128,1024]{2,1,0:T(8,128)(2,1)}, u32[]{:S(2)}, u32[]{:S(2)}) %collective-permute-start) | collective-permute-done | bytes 524320 | tf_op jit(solution)/shard_map/ppermute | solution.py:279
  32.4 0.0 copy-done.4
  32.4 0.0 copy-start.6
  32.4 6.4 %shard_map.87 = (bf16[512,128]{1,0:T(8,128)(2,1)S(1)}, bf16[512,128]{1,0:T(8,128)(2,1)S(1)}, bf16[256,1024]{1,0:T(8,128)(2,1)}, f32[256,1024]{1,0:T(8,128)S(1)},...) custom-call(s32[5]{0:T(128)S(1)} %stack.31.meta_ref, f32[1]{0:T(128)} %bitcast.5.bias_ref, ...), custom_call_target="tpu_custom_call" | custom-call | flops 603979776 | bytes 4194304 | tf_op jit(solution)/shard_map/pallas_call | solution.py:99
  38.8 0.0 collective-permute-start.7
  38.8 0.0 collective-permute-done.11.refs_10_
  38.8 1.0 %constant_dynamic-slice_fusion = bf16[256,512]{1,0:T(8,128)(2,1)S(1)} fusion(bf16[256,1024]{1,0:T(8,128)(2,1)} %collective-permute-done.11.refs_10_, s32[]{:T(128)S(6)} %select_n.59), kind=kLoop, calls=%fused_computation.3 | loop fusion | bytes 524292 | tf_op jit(solution)/shard_map/dynamic_slice | solution.py:282
  39.7 0.1 collective-permute-start.12
  39.8 2.1 %collective-permute-start.4 = (bf16[512,128]{1,0:T(8,128)(2,1)S(1)}, bf16[512,128]{1,0:T(8,128)(2,1)S(1)}, u32[]{:S(2)}, u32[]{:S(2)}) collective-permute-start(bf16[512,128]{1,0:T(8,128)(2,1)S(1)} %get-tuple-element.39), channel_id=1, source_target_pairs={{0,4},{2,6},{4,0},{6,2},{8,12},{10,14},{12,8},{14,10},{16,20},{18,... | collective-permute-start | bytes 393224 | tf_op jit(solution)/shard_map/ppermute | solution.py:208
  41.9 0.2 collective-permute-start.8
  42.1 0.0 collective-permute-done.10.refs_9_
  42.1 0.4 collective-permute-start.5
  42.4 2.5 %collective-permute-done.7.refs_5_ = bf16[512,128]{1,0:T(8,128)(2,1)S(1)} collective-permute-done((bf16[512,128]{1,0:T(8,128)(2,1)S(1)}, bf16[512,128]{1,0:T(8,128)(2,1)S(1)}, u32[]{:S(2)}, u32[]{:S(2)}) %collective-permute-start.7) | collective-permute-done | bytes 131104 | tf_op jit(solution)/shard_map/ppermute | solution.py:208
  44.9 0.0 collective-permute-start.9
  44.9 2.0 %collective-permute-done.4.refs_1_ = bf16[512,128]{1,0:T(8,128)(2,1)S(1)} collective-permute-done((bf16[512,128]{1,0:T(8,128)(2,1)S(1)}, bf16[512,128]{1,0:T(8,128)(2,1)S(1)}, u32[]{:S(2)}, u32[]{:S(2)}) %collective-permute-start.4) | collective-permute-done | bytes 131104 | tf_op jit(solution)/shard_map/ppermute | solution.py:208
  46.9 0.0 collective-permute-start.6
  46.9 0.0 collective-permute-done.8.refs_6_
  46.9 2.5 %collective-permute-start.3 = (bf16[2,128,1024]{2,1,0:T(8,128)(2,1)S(1)}, bf16[2,128,1024]{2,1,0:T(8,128)(2,1)S(1)}, u32[]{:S(2)}, u32[]{:S(2)}) collective-permute-start(bf16[2,128,1024]{2,1,0:T(8,128)(2,1)S(1)} %get-tuple-element.35), channel_id=1, source_target_pairs={{0,2},{2,0},{4,6},{6,4},{8,10},{10,8},{12,14},{14,12},{16,18},{18,... | collective-permute-start | bytes 1572872 | tf_op jit(solution)/shard_map/ppermute | solution.py:301
  49.3 0.0 collective-permute-done.5.refs_2_
  49.3 0.7 collective-permute-start.2
  50.0 0.0 collective-permute-done.12.refs_11_
  50.0 0.0 collective-permute-done.9.refs_7_
  50.1 0.0 collective-permute-done.6.refs_3_
  50.1 0.0 copy-done.6
  50.1 1.8 %product.1 = (f32[128,512]{1,0:T(8,128)S(1)}, bf16[128,512]{1,0:T(8,128)(2,1)S(1)}, bf16[128,512]{1,0:T(8,128)(2,1)S(1)}, bf16[128,512]{1,0:T(8,128)(2,1)S(1)}) custom-call(s32[5]{0:T(128)S(1)} %stack.32.meta_ref, bf16[512,128]{1,0:T(8,128)(2,1)S(1)} %get-tuple-element.38.refs_0_, bf16[512,128]{1,0:T(8,128)(2,1)S(1)} %collective-permute-done.4.refs_1_, ...), custom_call_target="tpu_custom_call" | custom-call | tf_op jit(solution)/shard_map/product/pallas_call | solution.py:154
  51.9 3.0 %collective-permute-start.13 = (bf16[128,512]{1,0:T(8,128)(2,1)S(1)}, bf16[128,512]{1,0:T(8,128)(2,1)S(1)}, u32[]{:S(2)}, u32[]{:S(2)}) collective-permute-start(bf16[128,512]{1,0:T(8,128)(2,1)S(1)} %get-tuple-element.43), channel_id=1, source_target_pairs={{0,8},{2,10},{4,12},{6,14},{8,0},{10,2},{12,4},{14,6},{16,24},{18,... | collective-permute-start | bytes 393224 | tf_op jit(solution)/shard_map/ppermute | solution.py:208
  54.8 2.9 %collective-permute-start.14 = (bf16[128,512]{1,0:T(8,128)(2,1)S(1)}, bf16[128,512]{1,0:T(8,128)(2,1)S(1)}, u32[]{:S(2)}, u32[]{:S(2)}) collective-permute-start(bf16[128,512]{1,0:T(8,128)(2,1)S(1)} %get-tuple-element.44), channel_id=1, source_target_pairs={{0,16},{2,18},{4,20},{6,22},{8,24},{10,26},{12,28},{14,30},{16,0},... | collective-permute-start | bytes 393224 | tf_op jit(solution)/shard_map/ppermute | solution.py:208
  57.7 0.0 collective-permute-start.15
  57.7 13.2 %collective-permute-done.13.refs_0_ = bf16[128,512]{1,0:T(8,128)(2,1)S(1)} collective-permute-done((bf16[128,512]{1,0:T(8,128)(2,1)S(1)}, bf16[128,512]{1,0:T(8,128)(2,1)S(1)}, u32[]{:S(2)}, u32[]{:S(2)}) %collective-permute-start.13) | collective-permute-done | bytes 131104 | tf_op jit(solution)/shard_map/ppermute | solution.py:208
  70.9 0.0 collective-permute-done.14.refs_1_
  70.9 4.9 %collective-permute-done.15.refs_2_ = bf16[128,512]{1,0:T(8,128)(2,1)S(1)} collective-permute-done((bf16[128,512]{1,0:T(8,128)(2,1)S(1)}, bf16[128,512]{1,0:T(8,128)(2,1)S(1)}, u32[]{:S(2)}, u32[]{:S(2)}) %collective-permute-start.15) | collective-permute-done | bytes 131104 | tf_op jit(solution)/shard_map/ppermute | solution.py:208
  75.8 0.6 summed.1
  76.4 0.1 collective-permute-start.16
  76.5 4.3 %collective-permute-done.16 = bf16[64,512]{1,0:T(8,128)(2,1)S(1)} collective-permute-done((bf16[64,512]{1,0:T(8,128)(2,1)S(1)}, bf16[64,512]{1,0:T(8,128)(2,1)S(1)}, u32[]{:S(2)}, u32[]{:S(2)}) %collective-permute-start.16) | collective-permute-done | bytes 65568 | tf_op jit(solution)/shard_map/ppermute | solution.py:208
  80.7 0.7 add_multiply_fusion
  81.4 0.0 collective-permute-done.3.near_ref
  81.4 0.0 collective-permute-done.2.long_ref
  81.4 1.6 %joined.1 = (bf16[256,1024]{1,0:T(8,128)(2,1)}, bf16[256,1024]{1,0:T(8,128)(2,1)}) custom-call(s32[5]{0:T(128)S(1)} %stack.32.meta_ref, f32[256,1024]{1,0:T(8,128)S(1)} %get-tuple-element.32.dk_ref, f32[256,1024]{1,0:T(8,128)S(1)} %get-tuple-element.33.dv_ref, bf16[2,128,1024]{2,1,0:T(8,128)(2,1)S(1)} %collective-permute-done.2.long_ref, ...), custom_call_target="tpu_custom_call" | custom-call | tf_op jit(solution)/shard_map/joined/pallas_call | solution.py:197
Async XLA Ops:
  0.6 3.6 %copy-start = (bf16[1024,1024]{1,0:T(8,128)(2,1)S(1)}, bf16[1024,1024]{1,0:T(8,128)(2,1)}, u32[]{:S(2)}) copy-start(bf16[1024,1024]{1,0:T(8,128)(2,1)} %param.9) | copy-start | bytes 6291460
  2.7 14.4 %copy-start.1 = (bf16[1,256,1024]{2,1,0:T(8,128)(2,1)S(1)}, bf16[1,256,1024]{2,1,0:T(8,128)(2,1)}, u32[]{:S(2)}) copy-start(bf16[1,256,1024]{2,1,0:T(8,128)(2,1)} %param.6) | copy-start | bytes 1572868
  2.7 14.4 %copy-start.2 = (bf16[1,256,1024]{2,1,0:T(8,128)(2,1)S(1)}, bf16[1,256,1024]{2,1,0:T(8,128)(2,1)}, u32[]{:S(2)}) copy-start(bf16[1,256,1024]{2,1,0:T(8,128)(2,1)} %param.7) | copy-start | bytes 1572868
  2.7 14.4 %collective-permute-start.1 = (bf16[2,128,1024]{2,1,0:T(8,128)(2,1)}, bf16[2,128,1024]{2,1,0:T(8,128)(2,1)}, u32[]{:S(2)}, u32[]{:S(2)}) collective-permute-start(bf16[2,128,1024]{2,1,0:T(8,128)(2,1)} %shard_map.85), channel_id=1, source_target_pairs={{2,4},{4,2},{6,8},{8,6},{10,12},{12,10},{14,16},{16,14},{18,20},{2... | collective-permute-start | bytes 1572872 | tf_op jit(solution)/shard_map/ppermute | solution.py:275
  8.7 23.7 %collective-permute-start = (bf16[2,128,1024]{2,1,0:T(8,128)(2,1)}, bf16[2,128,1024]{2,1,0:T(8,128)(2,1)}, u32[]{:S(2)}, u32[]{:S(2)}) collective-permute-start(bf16[2,128,1024]{2,1,0:T(8,128)(2,1)} %shard_map.84), channel_id=1, source_target_pairs={{0,2},{2,0},{4,6},{6,4},{8,10},{10,8},{12,14},{14,12},{16,18},{18,... | collective-permute-start | bytes 1572872 | tf_op jit(solution)/shard_map/ppermute | solution.py:279
  13.6 25.2 %collective-permute-start.11 = (bf16[256,1024]{1,0:T(8,128)(2,1)}, bf16[256,1024]{1,0:T(8,128)(2,1)}, u32[]{:S(2)}, u32[]{:S(2)}) collective-permute-start(bf16[256,1024]{1,0:T(8,128)(2,1)} %bitcast.29), channel_id=1, source_target_pairs={{0,4},{2,6},{4,0},{6,2},{8,12},{10,14},{12,8},{14,10},{16,20},{18,... | collective-permute-start | bytes 1572872 | tf_op jit(solution)/shard_map/ppermute | solution.py:208
  16.9 25.2 %collective-permute-start.10 = (bf16[256,512]{1,0:T(8,128)(2,1)}, bf16[256,512]{1,0:T(8,128)(2,1)S(1)}, u32[]{:S(2)}, u32[]{:S(2)}) collective-permute-start(bf16[256,512]{1,0:T(8,128)(2,1)} %dynamic-slice_bitcast_fusion), channel_id=1, source_target_pairs={{0,1},{1,0},{2,3},{3,2},{4,5},{5,4},{6,7},{7,6},{8,9},{9,8},{10,11... | collective-permute-start | bytes 786440 | tf_op jit(solution)/shard_map/ppermute | solution.py:212
  17.1 1.0 %copy-start.3 = (bf16[1,256,1024]{2,1,0:T(8,128)(2,1)S(1)}, bf16[1,256,1024]{2,1,0:T(8,128)(2,1)}, u32[]{:S(2)}) copy-start(bf16[1,256,1024]{2,1,0:T(8,128)(2,1)} %param.5) | copy-start | bytes 1572868
  18.1 1.0 %copy-start.5 = (bf16[256,1024]{1,0:T(8,128)(2,1)S(1)}, bf16[256,1024]{1,0:T(8,128)(2,1)}, u32[]{:S(2)}) copy-start(bf16[256,1024]{1,0:T(8,128)(2,1)} %convolution_convert_fusion.da_ref) | copy-start | bytes 1572868
  19.1 13.2 %copy-start.4 = (bf16[1,256,1024]{2,1,0:T(8,128)(2,1)S(1)}, bf16[1,256,1024]{2,1,0:T(8,128)(2,1)}, u32[]{:S(2)}) copy-start(bf16[1,256,1024]{2,1,0:T(8,128)(2,1)} %param.5) | copy-start | bytes 1572868
  32.4 17.7 %copy-start.6 = (bf16[1,256,1024]{2,1,0:T(8,128)(2,1)S(1)}, bf16[1,256,1024]{2,1,0:T(8,128)(2,1)}, u32[]{:S(2)}) copy-start(bf16[1,256,1024]{2,1,0:T(8,128)(2,1)} %param.8) | copy-start | bytes 1572868
  38.8 6.1 %collective-permute-start.7 = (bf16[512,128]{1,0:T(8,128)(2,1)S(1)}, bf16[512,128]{1,0:T(8,128)(2,1)S(1)}, u32[]{:S(2)}, u32[]{:S(2)}) collective-permute-start(bf16[512,128]{1,0:T(8,128)(2,1)S(1)} %get-tuple-element.41), channel_id=1, source_target_pairs={{0,4},{2,6},{4,0},{6,2},{8,12},{10,14},{12,8},{14,10},{16,20},{18,... | collective-permute-start | bytes 393224 | tf_op jit(solution)/shard_map/ppermute | solution.py:208
  39.7 10.3 %collective-permute-start.12 = (bf16[256,512]{1,0:T(8,128)(2,1)S(1)}, bf16[256,512]{1,0:T(8,128)(2,1)S(1)}, u32[]{:S(2)}, u32[]{:S(2)}) collective-permute-start(bf16[256,512]{1,0:T(8,128)(2,1)S(1)} %constant_dynamic-slice_fusion), channel_id=1, source_target_pairs={{0,1},{1,0},{2,3},{3,2},{4,5},{5,4},{6,7},{7,6},{8,9},{9,8},{10,11... | collective-permute-start | bytes 786440 | tf_op jit(solution)/shard_map/ppermute | solution.py:212
  39.8 7.0 %collective-permute-start.4 = (bf16[512,128]{1,0:T(8,128)(2,1)S(1)}, bf16[512,128]{1,0:T(8,128)(2,1)S(1)}, u32[]{:S(2)}, u32[]{:S(2)}) collective-permute-start(bf16[512,128]{1,0:T(8,128)(2,1)S(1)} %get-tuple-element.39), channel_id=1, source_target_pairs={{0,4},{2,6},{4,0},{6,2},{8,12},{10,14},{12,8},{14,10},{16,20},{18,... | collective-permute-start | bytes 393224 | tf_op jit(solution)/shard_map/ppermute | solution.py:208
  41.9 4.9 %collective-permute-start.8 = (bf16[512,128]{1,0:T(8,128)(2,1)S(1)}, bf16[512,128]{1,0:T(8,128)(2,1)S(1)}, u32[]{:S(2)}, u32[]{:S(2)}) collective-permute-start(bf16[512,128]{1,0:T(8,128)(2,1)S(1)} %get-tuple-element.40.refs_4_), channel_id=1, source_target_pairs={{0,1},{1,0},{2,3},{3,2},{4,5},{5,4},{6,7},{7,6},{8,9},{9,8},{10,11... | collective-permute-start | bytes 393224 | tf_op jit(solution)/shard_map/ppermute | solution.py:212
  42.1 7.3 %collective-permute-start.5 = (bf16[512,128]{1,0:T(8,128)(2,1)S(1)}, bf16[512,128]{1,0:T(8,128)(2,1)S(1)}, u32[]{:S(2)}, u32[]{:S(2)}) collective-permute-start(bf16[512,128]{1,0:T(8,128)(2,1)S(1)} %get-tuple-element.38.refs_0_), channel_id=1, source_target_pairs={{0,1},{1,0},{2,3},{3,2},{4,5},{5,4},{6,7},{7,6},{8,9},{9,8},{10,11... | collective-permute-start | bytes 393224 | tf_op jit(solution)/shard_map/ppermute | solution.py:212
  44.9 5.2 %collective-permute-start.9 = (bf16[512,128]{1,0:T(8,128)(2,1)S(1)}, bf16[512,128]{1,0:T(8,128)(2,1)S(1)}, u32[]{:S(2)}, u32[]{:S(2)}) collective-permute-start(bf16[512,128]{1,0:T(8,128)(2,1)S(1)} %collective-permute-done.7.refs_5_), channel_id=1, source_target_pairs={{0,1},{1,0},{2,3},{3,2},{4,5},{5,4},{6,7},{7,6},{8,9},{9,8},{10,11... | collective-permute-start | bytes 393224 | tf_op jit(solution)/shard_map/ppermute | solution.py:212
  46.9 3.2 %collective-permute-start.6 = (bf16[512,128]{1,0:T(8,128)(2,1)S(1)}, bf16[512,128]{1,0:T(8,128)(2,1)S(1)}, u32[]{:S(2)}, u32[]{:S(2)}) collective-permute-start(bf16[512,128]{1,0:T(8,128)(2,1)S(1)} %collective-permute-done.4.refs_1_), channel_id=1, source_target_pairs={{0,1},{1,0},{2,3},{3,2},{4,5},{5,4},{6,7},{7,6},{8,9},{9,8},{10,11... | collective-permute-start | bytes 393224 | tf_op jit(solution)/shard_map/ppermute | solution.py:212
  46.9 34.6 %collective-permute-start.3 = (bf16[2,128,1024]{2,1,0:T(8,128)(2,1)S(1)}, bf16[2,128,1024]{2,1,0:T(8,128)(2,1)S(1)}, u32[]{:S(2)}, u32[]{:S(2)}) collective-permute-start(bf16[2,128,1024]{2,1,0:T(8,128)(2,1)S(1)} %get-tuple-element.35), channel_id=1, source_target_pairs={{0,2},{2,0},{4,6},{6,4},{8,10},{10,8},{12,14},{14,12},{16,18},{18,... | collective-permute-start | bytes 1572872 | tf_op jit(solution)/shard_map/ppermute | solution.py:301
  49.3 32.1 %collective-permute-start.2 = (bf16[2,128,1024]{2,1,0:T(8,128)(2,1)S(1)}, bf16[2,128,1024]{2,1,0:T(8,128)(2,1)S(1)}, u32[]{:S(2)}, u32[]{:S(2)}) collective-permute-start(bf16[2,128,1024]{2,1,0:T(8,128)(2,1)S(1)} %get-tuple-element.34), channel_id=1, source_target_pairs={{2,4},{4,2},{6,8},{8,6},{10,12},{12,10},{14,16},{16,14},{18,20},{2... | collective-permute-start | bytes 1572872 | tf_op jit(solution)/shard_map/ppermute | solution.py:291
  51.9 19.0 %collective-permute-start.13 = (bf16[128,512]{1,0:T(8,128)(2,1)S(1)}, bf16[128,512]{1,0:T(8,128)(2,1)S(1)}, u32[]{:S(2)}, u32[]{:S(2)}) collective-permute-start(bf16[128,512]{1,0:T(8,128)(2,1)S(1)} %get-tuple-element.43), channel_id=1, source_target_pairs={{0,8},{2,10},{4,12},{6,14},{8,0},{10,2},{12,4},{14,6},{16,24},{18,... | collective-permute-start | bytes 393224 | tf_op jit(solution)/shard_map/ppermute | solution.py:208
  54.8 16.0 %collective-permute-start.14 = (bf16[128,512]{1,0:T(8,128)(2,1)S(1)}, bf16[128,512]{1,0:T(8,128)(2,1)S(1)}, u32[]{:S(2)}, u32[]{:S(2)}) collective-permute-start(bf16[128,512]{1,0:T(8,128)(2,1)S(1)} %get-tuple-element.44), channel_id=1, source_target_pairs={{0,16},{2,18},{4,20},{6,22},{8,24},{10,26},{12,28},{14,30},{16,0},... | collective-permute-start | bytes 393224 | tf_op jit(solution)/shard_map/ppermute | solution.py:208
  57.7 18.1 %collective-permute-start.15 = (bf16[128,512]{1,0:T(8,128)(2,1)S(1)}, bf16[128,512]{1,0:T(8,128)(2,1)S(1)}, u32[]{:S(2)}, u32[]{:S(2)}) collective-permute-start(bf16[128,512]{1,0:T(8,128)(2,1)S(1)} %get-tuple-element.45), channel_id=1, source_target_pairs={{0,24},{2,26},{4,28},{6,30},{8,16},{10,18},{12,20},{14,22},{16,8},... | collective-permute-start | bytes 393224 | tf_op jit(solution)/shard_map/ppermute | solution.py:208
  76.4 4.3 %collective-permute-start.16 = (bf16[64,512]{1,0:T(8,128)(2,1)S(1)}, bf16[64,512]{1,0:T(8,128)(2,1)S(1)}, u32[]{:S(2)}, u32[]{:S(2)}) collective-permute-start(bf16[64,512]{1,0:T(8,128)(2,1)S(1)} %get-tuple-element.47), channel_id=1, source_target_pairs={{0,2},{2,0},{4,6},{6,4},{8,10},{10,8},{12,14},{14,12},{16,18},{18,... | collective-permute-start | bytes 196616 | tf_op jit(solution)/shard_map/ppermute | solution.py:208
where the time goes:
time: 83.5 us; the launch traced here: 83.1 us
  waiting for transfers between devices  34.5 us (41%)
  Pallas kernels  19.9 us (24%)
  starting transfers between devices  19.8 us (24%)
  local copies, waits for them, and re-layouts  4.97 us (6%)
  matrix products  2.58 us (3%)
    ppermute x7, waiting for transfers between devices, swapped(): return lax.ppermute(value, 'seq', [(i, i ^ stride) for i in range(count)])  26.8 us
    pallas_call x2, Pallas kernels, half_attention(): pl.pallas_call(half_kernel, in_specs=[in_smem, in_smem] + [in_vmem] * (le...  12 us
    ppermute x7, starting transfers between devices, swapped(): return lax.ppermute(value, 'seq', [(i, i ^ stride) for i in range(count)])  9.5 us
    ppermute x1, waiting for transfers between devices, on_device(): second_rim = lax.ppermute(rim2, 'seq', near_pairs)  7.65 us
    ppermute x1, starting transfers between devices, on_device(): second_rim = lax.ppermute(rim2, 'seq', near_pairs)  4.92 us
    pallas_call x2, Pallas kernels, packed_rim(): pl.pallas_call(rim_kernel, grid_spec=pltpu.PrefetchScalarGridSpec(num_sca...  3.86 us
    dynamic_slice x2, local copies, waits for them, and re-layouts, other_half(): lax.dynamic_slice_in_dim(array, (mine + 1) % dp_count * own_width, own_wi...  2.7 us
    dot_general x1, matrix products, contract(): return lax.dot_general(a, b, (dims, ((), ())), preferred_element_type=f32)  2.58 us
  transfers between devices with their start and end apart: 17, of which 6 were waited for; matrix products, arithmetic and copies ran while one was open for 7% of the time, Pallas kernels for 20%

commit v1 on v0

--- a/solution.py
+++ b/solution.py
@@ -9,7 +9,6 @@
 HEAD_DIM = 64
 HALF = 128
 PAIR = 2 * HEAD_DIM
-UNROLL = 4
 masked_score = -1e30
 f32 = jnp.float32
 bf16 = jnp.bfloat16
@@ -27,91 +26,132 @@
     return lax.dot_general(a, b, (dims, ((), ())), preferred_element_type=f32)
 
 
-def half_kernel(meta_ref, bias_ref, q_ref, da_ref, k_ref, v_ref, rim_ref, *rest):
-    earlier, outs = rest[:-6], rest[-6:]
-    keep_ref, send_ref, dq_ref, dk_ref, dv_ref, back_ref = outs
+def half_kernel(meta_ref, bias_ref, q_hbm, da_hbm, k_hbm, v_hbm, rim_hbm, keep_ref, send_ref, back_ref, dq_hbm, dk_hbm, dv_hbm,
+                one_ref, wide_ref, two_ref, score_ref, dp_ref, p_ref, ds_ref, dq_ref, own_ref, in_sem, out_sem):
     side = meta_ref[0]
     y_digit = meta_ref[1]
     scale = HEAD_DIM ** -0.5
-    first_head = lax.broadcasted_iota(jnp.int32, (HALF, PAIR), 1) < HEAD_DIM
-    ahead = lax.broadcasted_iota(jnp.int32, (HALF, 2 * HALF), 0) - lax.broadcasted_iota(jnp.int32, (HALF, 2 * HALF), 1) % HALF
-    in_rim = ahead * (1 - 2 * side) >= side
     near_rows = pl.ds(pl.multiple_of(side * HALF, HALF), HALF)
     far_rows = pl.ds(pl.multiple_of((1 - side) * HALF, HALF), HALF)
-    if earlier:
-        dq_ref[far_rows, :] = earlier[0][far_rows, :]
-
-    def one(pair, place, at_ref):
-        cols = pl.ds(pl.multiple_of(pair * PAIR, PAIR), PAIR)
-        q_one = q_ref[near_rows, cols].astype(f32) * scale
-        da_one = da_ref[near_rows, cols].astype(f32)
-        q_two = jnp.concatenate([jnp.where(first_head, q_one, 0.0), jnp.where(first_head, 0.0, q_one)], axis=0).astype(bf16)
-        da_two = jnp.concatenate([jnp.where(first_head, da_one, 0.0), jnp.where(first_head, 0.0, da_one)], axis=0).astype(bf16)
-        keys = jnp.concatenate([rim_ref[0, :, cols], k_ref[near_rows, cols], k_ref[far_rows, cols]], axis=0)
-        vals = jnp.concatenate([rim_ref[1, :, cols], v_ref[near_rows, cols], v_ref[far_rows, cols]], axis=0)
-        score = contract(keys, q_two, NT)
-        s_edge = jnp.where(in_rim, score[:HALF] + bias_ref[0], score[2 * HALF :])
-        s_near = score[HALF : 2 * HALF]
+    pairs = one_ref.shape[0]
+
+    def columns(number):
+        pair = 2 * (number // 2) + (y_digit if number % 2 == 0 else 1 - y_digit)
+        return pl.ds(pl.multiple_of(pair * PAIR, PAIR), PAIR)
+
+    def fetches(number):
+        cols = columns(number)
+        found = []
+        for which, (thin, thick) in enumerate(((q_hbm, k_hbm), (da_hbm, v_hbm))):
+            found.append((thin.at[near_rows, cols], one_ref.at[number, which]))
+            found.append((rim_hbm.at[which, :, cols], wide_ref.at[number, which, pl.ds(0, HALF)]))
+            found.append((thick.at[near_rows, cols], wide_ref.at[number, which, pl.ds(HALF, HALF)]))
+            found.append((thick.at[far_rows, cols], wide_ref.at[number, which, pl.ds(2 * HALF, HALF)]))
+        return [pltpu.make_async_copy(a, b, in_sem.at[number, place]) for place, (a, b) in enumerate(found)]
+
+    def stores(number):
+        cols = columns(number)
+        found = [(dq_ref.at[number], dq_hbm.at[:, cols]), (own_ref.at[number, 0], dk_hbm.at[:, cols]), (own_ref.at[number, 1], dv_hbm.at[:, cols])]
+        return [pltpu.make_async_copy(a, b, out_sem.at[number, place]) for place, (a, b) in enumerate(found)]
+
+    def multiply(number):
+        for copy in fetches(number):
+            copy.wait()
+        slot = number % 3
+        first_head = lax.broadcasted_iota(jnp.int32, (HALF, PAIR), 1) < HEAD_DIM
+        for which, (factor, out) in enumerate(((scale, score_ref), (1.0, dp_ref))):
+            one = one_ref[number, which].astype(f32) * factor
+            two_ref[slot, which, :HALF] = jnp.where(first_head, one, 0.0).astype(bf16)
+            two_ref[slot, which, HALF:] = jnp.where(first_head, 0.0, one).astype(bf16)
+            out[number % 2] = contract(wide_ref[number, which], two_ref[slot, which], NT)
+
+    def weigh(number):
+        slot = number % 2
+        ahead = lax.broadcasted_iota(jnp.int32, (HALF, 2 * HALF), 0) - lax.broadcasted_iota(jnp.int32, (HALF, 2 * HALF), 1) % HALF
+        in_rim = ahead * (1 - 2 * side) >= side
+        s_edge = jnp.where(in_rim, score_ref[slot, :HALF] + bias_ref[0], score_ref[slot, 2 * HALF :])
+        s_near = score_ref[slot, HALF : 2 * HALF]
         top = jnp.max(jnp.maximum(s_edge, s_near), axis=0, keepdims=True)
         e_edge = jnp.exp(s_edge - top)
         e_near = jnp.exp(s_near - top)
         inv = 1.0 / jnp.sum(e_edge + e_near, axis=0, keepdims=True)
         p_edge = e_edge * inv
         p_near = e_near * inv
-        p_all = jnp.concatenate([jnp.where(in_rim, p_edge, 0.0).astype(bf16), p_near.astype(bf16),
-                                 jnp.where(in_rim, 0.0, p_edge).astype(bf16)], axis=0)
-        dp = contract(vals, da_two, NT)
-        d_edge = jnp.where(in_rim, dp[:HALF], dp[2 * HALF :])
-        d_near = dp[HALF : 2 * HALF]
+        d_edge = jnp.where(in_rim, dp_ref[slot, :HALF], dp_ref[slot, 2 * HALF :])
+        d_near = dp_ref[slot, HALF : 2 * HALF]
         delta = jnp.sum(p_edge * d_edge + p_near * d_near, axis=0, keepdims=True)
-        ds_edge = p_edge * (d_edge - delta)
-        ds_near = p_near * (d_near - delta)
-        ds_all = jnp.concatenate([jnp.where(in_rim, ds_edge, 0.0).astype(bf16), ds_near.astype(bf16),
-                                  jnp.where(in_rim, 0.0, ds_edge).astype(bf16)], axis=0)
-        at = contract(vals, p_all, TN)
-        start = pl.multiple_of(place * PAIR, PAIR)
-        at_ref[pl.ds(start, HEAD_DIM), :] = at[:HEAD_DIM, :HALF].astype(bf16)
-        at_ref[pl.ds(start + HEAD_DIM, HEAD_DIM), :] = at[HEAD_DIM:, HALF:].astype(bf16)
-        dqt = contract(keys, ds_all, TN)
+        for ref, edge, near in ((p_ref, p_edge, p_near), (ds_ref, p_edge * (d_edge - delta), p_near * (d_near - delta))):
+            ref[slot, :HALF] = jnp.where(in_rim, edge, 0.0).astype(bf16)
+            ref[slot, HALF : 2 * HALF] = near.astype(bf16)
+            ref[slot, 2 * HALF :] = jnp.where(in_rim, 0.0, edge).astype(bf16)
+
+    def spread(number):
+        slot = number % 2
+        at_ref = send_ref if number % 2 else keep_ref
+        start = number // 2 * PAIR
+        at = contract(wide_ref[number, 1], p_ref[slot], TN)
+        at_ref[start : start + HEAD_DIM, :] = at[:HEAD_DIM, :HALF].astype(bf16)
+        at_ref[start + HEAD_DIM : start + PAIR, :] = at[HEAD_DIM:, HALF:].astype(bf16)
+        for which, left in enumerate((ds_ref, p_ref)):
+            part = contract(left[slot], two_ref[number % 3, which], NN)
+            back_ref[which, :, columns(number)] = part[:HALF].astype(bf16)
+            own_ref[number, which, near_rows, :] = part[HALF : 2 * HALF].astype(bf16)
+            own_ref[number, which, far_rows, :] = part[2 * HALF :].astype(bf16)
+        dqt = contract(wide_ref[number, 0], ds_ref[slot], TN)
         dqt = jnp.concatenate([dqt[:HEAD_DIM, :HALF], dqt[HEAD_DIM:, HALF:]], axis=0) * scale
-        dq_ref[near_rows, cols] = dqt.T.astype(bf16)
-        for which, (ref, left, right) in enumerate(((dk_ref, ds_all, q_two), (dv_ref, p_all, da_two))):
-            part = contract(left, right, NN)
-            back_ref[which, :, cols] = part[:HALF].astype(bf16)
-            near, far = part[HALF : 2 * HALF], part[2 * HALF :]
-            if earlier:
-                near = near + earlier[1 + which][near_rows, cols]
-                far = far + earlier[1 + which][far_rows, cols]
-            ref[near_rows, cols] = near
-            ref[far_rows, cols] = far
-
-    def body(place, carry):
-        one(2 * place + y_digit, place, keep_ref)
-        one(2 * place + 1 - y_digit, place, send_ref)
-        return carry
-
-    lax.fori_loop(0, q_ref.shape[1] // (2 * PAIR), body, 0, unroll=UNROLL)
-
-
-def half_attention(meta, bias, q, da, k, v, rim, earlier):
+        dq_ref[number] = dqt.T.astype(bf16)
+        for copy in stores(number):
+            copy.start()
+
+    for number in range(pairs):
+        for copy in fetches(number):
+            copy.start()
+    for step in range(pairs + 2):
+        if step < pairs:
+            multiply(step)
+        if 0 <= step - 2:
+            spread(step - 2)
+        if 0 <= step - 1 < pairs:
+            weigh(step - 1)
+    for number in range(pairs):
+        for copy in stores(number):
+            copy.wait()
+
+
+def half_attention(meta, bias, q, da, k, v, rim):
     rows, width = q.shape
-    operands = [meta, bias, q, da, k, v, rim] + (list(earlier) if earlier else [])
+    pairs = width // PAIR
+    in_hbm = pl.BlockSpec(memory_space=pltpu.HBM)
+    held = [pltpu.with_memory_space_constraint(array, pltpu.HBM) for array in (q, da, k, v)]
     return pl.pallas_call(
         half_kernel,
-        in_specs=[in_smem, in_smem] + [in_vmem] * (len(operands) - 2),
-        out_specs=[in_vmem] * 6,
+        in_specs=[in_smem, in_smem] + [in_hbm] * 4 + [pl.BlockSpec(memory_space=pl.ANY)],
+        out_specs=[in_vmem] * 3 + [in_hbm] * 3,
         out_shape=[
             jax.ShapeDtypeStruct((width // 2, HALF), bf16),
             jax.ShapeDtypeStruct((width // 2, HALF), bf16),
-            jax.ShapeDtypeStruct((rows, width), bf16),
-            jax.ShapeDtypeStruct((rows, width), f32),
-            jax.ShapeDtypeStruct((rows, width), f32),
             jax.ShapeDtypeStruct((2, HALF, width), bf16),
+            pltpu.HBM((HALF, width), bf16),
+            pltpu.HBM((rows, width), bf16),
+            pltpu.HBM((rows, width), bf16),
+        ],
+        scratch_shapes=[
+            pltpu.VMEM((pairs, 2, HALF, PAIR), bf16),
+            pltpu.VMEM((pairs, 2, 3 * HALF, PAIR), bf16),
+            pltpu.VMEM((3, 2, 2 * HALF, PAIR), bf16),
+            pltpu.VMEM((2, 3 * HALF, 2 * HALF), f32),
+            pltpu.VMEM((2, 3 * HALF, 2 * HALF), f32),
+            pltpu.VMEM((2, 3 * HALF, 2 * HALF), bf16),
+            pltpu.VMEM((2, 3 * HALF, 2 * HALF), bf16),
+            pltpu.VMEM((pairs, HALF, PAIR), bf16),
+            pltpu.VMEM((pairs, 2, rows, PAIR), bf16),
+            pltpu.SemaphoreType.DMA((pairs, 8)),
+            pltpu.SemaphoreType.DMA((pairs, 3)),
         ],
         cost_estimate=pl.CostEstimate(flops=12 * HALF * 3 * HALF * width, bytes_accessed=16 * rows * width,
                                       transcendentals=HALF * 2 * HALF * width // HEAD_DIM),
         compiler_params=pltpu.CompilerParams(vmem_limit_bytes=24 << 20),
-    )(*operands)
+    )(meta, bias, *held, rim)
 
 
 def rim_kernel(side_ref, k_ref, v_ref, out_ref):
@@ -141,7 +181,7 @@
     for row in (side, 1 - side):
         rows = pl.ds(pl.multiple_of(row * HALF, HALF), HALF)
         cols = pl.ds(pl.multiple_of(mine * own, own), own)
-        rights += [g_ref[rows, cols], g_y_ref[rows, cols], g_dp_ref[rows, :], g_y_dp_ref[rows, :]]
+        rights += [ref[rows, cols] for ref in (g_ref, g_y_ref, g_dp_ref, g_y_dp_ref)]
     right = jnp.concatenate(rights, axis=0)
     for step, out_ref in enumerate(outs):
         rows = pl.ds(pl.multiple_of((z_digit ^ step) * size, size), size)
@@ -184,24 +224,26 @@
     )(meta, own, *pieces)
 
 
-def join_kernel(meta_ref, dk_ref, dv_ref, long_ref, near_ref, dk_out, dv_out):
+def join_kernel(meta_ref, dq1_ref, dk1_ref, dv1_ref, dq2_ref, dk2_ref, dv2_ref, long_ref, near_ref, dq_out, dk_out, dv_out):
     side = meta_ref[0]
-    for row, rim in ((side, long_ref), (1 - side, near_ref)):
+    for row, rim, dq_ref in ((side, long_ref, dq1_ref), (1 - side, near_ref, dq2_ref)):
         rows = pl.ds(pl.multiple_of(row * HALF, HALF), HALF)
-        dk_out[rows, :] = (dk_ref[rows, :] + rim[0].astype(f32)).astype(bf16)
-        dv_out[rows, :] = (dv_ref[rows, :] + rim[1].astype(f32)).astype(bf16)
-
-
-def joined(meta, dk, dv, from_long, from_near):
-    shape = jax.ShapeDtypeStruct(dk.shape, bf16)
+        dq_out[rows, :] = dq_ref[...]
+        for which, (one, two, out) in enumerate(((dk1_ref, dk2_ref, dk_out), (dv1_ref, dv2_ref, dv_out))):
+            total = one[rows, :].astype(f32) + two[rows, :].astype(f32) + rim[which].astype(f32)
+            out[rows, :] = total.astype(bf16)
+
+
+def joined(meta, own1, own2, from_long, from_near):
+    shape = jax.ShapeDtypeStruct(own1[1].shape, bf16)
     return pl.pallas_call(
         join_kernel,
-        in_specs=[in_smem] + [in_vmem] * 4,
-        out_specs=[in_vmem] * 2,
-        out_shape=[shape, shape],
+        in_specs=[in_smem] + [in_vmem] * 8,
+        out_specs=[in_vmem] * 3,
+        out_shape=[shape] * 3,
         compiler_params=pltpu.CompilerParams(vmem_limit_bytes=12 << 20),
         name="joined",
-    )(meta, dk, dv, from_long, from_near)
+    )(meta, *own1, *own2, from_long, from_near)
 
 
 def swapped(value, stride, count):
@@ -278,22 +320,19 @@
     rim2, dattn = lax.optimization_barrier((rim2, dattn))
     second_rim = lax.ppermute(rim2, "seq", near_pairs)
 
-    def other_half(array):
-        return lax.dynamic_slice_in_dim(array, (mine + 1) % dp_count * own_width, own_width, 1)
-
     if direct:
         g_y = swapped(g, 2, count)
-        g_dp = turned(other_half(g), dp_count)[0]
-        g_y_dp = turned(other_half(g_y), dp_count)[0]
+        g_dp = turned(g, dp_count)[0]
+        g_y_dp = turned(g_y, dp_count)[0]
         gs = [g, g_dp, g_y, g_y_dp]
 
-    keep1, send1, dq, dk, dv, back1 = half_attention(metas[0], bias[0], q, dattn, k, v, first_rim, None)
+    keep1, send1, back1, *own1 = half_attention(metas[0], bias[0], q, dattn, k, v, first_rim)
     from_long = lax.ppermute(back1, "seq", long_pairs)
     if direct:
         at_y1 = swapped(send1, 2, count)
         at_dp1 = turned(keep1, dp_count)[0]
         at_y_dp1 = turned(at_y1, dp_count)[0]
-    keep2, send2, dq, dk, dv, back2 = half_attention(metas[1], bias[1], q, dattn, k, v, second_rim, (dq, dk, dv))
+    keep2, send2, back2, *own2 = half_attention(metas[1], bias[1], q, dattn, k, v, second_rim)
     if direct:
         at_y2 = swapped(send2, 2, count)
         at_dp2 = turned(keep2, dp_count)[0]
@@ -311,7 +350,7 @@
         wo_grad = kept + swapped(sent, 1, count).astype(f32)
     else:
         wo_grad = general_sum((keep1, send1), (keep2, send2), g, sides, place, mine, y_digit, count, dp_count)
-    dk, dv = joined(metas[0], dk, dv, from_long, from_near)
+    dq, dk, dv = joined(metas[0], own1, own2, from_long, from_near)
     return dq[None], dk[None], dv[None], wo_grad * frames ** -0.5
 
 

time: 83.5 us -> 87.3 us (1.046)
  starting transfers between devices: 19.8 us -> 26.3 us
  local copies, waits for them, and re-layouts: 4.97 us -> 0.22 us
  Pallas kernels: 19.9 us -> 24 us
  waiting for transfers between devices: 34.5 us -> 32.3 us
    ppermute x7, starting transfers between devices: 9.5 us -> 18.7 us  [swapped(): return lax.ppermute(value, 'seq', [(i, i ^ stride) for i in range(count)])]
    ppermute x1, waiting for transfers between devices: 7.65 us -> 0.01 us  [on_device(): second_rim = lax.ppermute(rim2, 'seq', near_pairs)]
    ppermute x7, waiting for transfers between devices: 26.8 us -> 31.3 us  [swapped(): return lax.ppermute(value, 'seq', [(i, i ^ stride) for i in range(count)])]
    pallas_call x3, Pallas kernels: 13.6 us -> 17.4 us  [the longest x2 15.4 us: half_attention(): pl.pallas_call(half_kernel, in_specs=[in_smem, in_smem] + [in_hbm] * 4 +...]
    ppermute x1, starting transfers between devices: 4.92 us -> 1.55 us  [on_device(): second_rim = lax.ppermute(rim2, 'seq', near_pairs)]
    dynamic_slice x2 -> x0, local copies, waits for them, and re-layouts: 2.7 us -> none  [other_half(): lax.dynamic_slice_in_dim(array, (mine + 1) % dp_count * own_width, own_wi...]
    unnamed x14 -> x18, local copies, waits for them, and re-layouts: 2.1 us -> 0.05 us
    ppermute x1, starting transfers between devices: 2.48 us -> 3.74 us  [on_device(): from_near = lax.ppermute(back2, 'seq', near_pairs)]
  transfers between devices with their start and end apart: 17 -> 17, of which waited for: 6 -> 7; matrix products, arithmetic and copies ran while one was open for 7% -> 3% of each run, Pallas kernels for 20% -> 25%
where the time goes in v1:
time: 87.3 us; the launch traced here: 86.9 us
  waiting for transfers between devices  32.3 us (37%)
  starting transfers between devices  26.3 us (30%)
  Pallas kernels  24 us (27%)
  matrix products  2.61 us (3%)
    ppermute x7, waiting for transfers between devices, swapped(): return lax.ppermute(value, 'seq', [(i, i ^ stride) for i in range(count)])  31.3 us
    ppermute x7, starting transfers between devices, swapped(): return lax.ppermute(value, 'seq', [(i, i ^ stride) for i in range(count)])  18.7 us
    pallas_call x2, Pallas kernels, half_attention(): pl.pallas_call(half_kernel, in_specs=[in_smem, in_smem] + [in_hbm] * 4 +...  15.4 us
    pallas_call x2, Pallas kernels, packed_rim(): pl.pallas_call(rim_kernel, grid_spec=pltpu.PrefetchScalarGridSpec(num_sca...  3.86 us
    ppermute x1, starting transfers between devices, on_device(): from_near = lax.ppermute(back2, 'seq', near_pairs)  3.74 us
    dot_general x1, matrix products, contract(): return lax.dot_general(a, b, (dims, ((), ())), preferred_element_type=f32)  2.61 us
    pallas_call x1, Pallas kernels, products(): pl.pallas_call(product_kernel, in_specs=[in_smem] + [in_vmem] * 12, out_s...  2.09 us
    pallas_call x1, Pallas kernels, joined(): pl.pallas_call(join_kernel, in_specs=[in_smem] + [in_vmem] * 8, out_specs...  2.01 us
  transfers between devices with their start and end apart: 17, of which 7 were waited for; matrix products, arithmetic and copies ran while one was open for 3% of the time, Pallas kernels for 25%

profile of v1, /device:TPU:0, one launch (start us, length us, event | category | flops | bytes accessed | tf_op | source)
XLA Modules:
  0.0 86.9 jit_solution(503175617778906696)
XLA Ops:
  0.6 0.0 copy-start
  0.7 2.0 %shard_map.85 = bf16[2,128,1024]{2,1,0:T(8,128)(2,1)} custom-call(s32[1]{0:T(128)} %bitcast.side_ref, bf16[256,1024]{1,0:T(8,128)(2,1)} %bitcast.20, bf16[256,1024]{1,0:T(8,128)(2,1)} %bitcast.24), custom_call_target="tpu_custom_call" | custom-call | tf_op jit(solution)/shard_map/pallas_call | solution.py:165
  2.7 0.7 collective-permute-start
  3.4 5.7 %collective-permute-start.11 = (bf16[256,1024]{1,0:T(8,128)(2,1)}, bf16[256,1024]{1,0:T(8,128)(2,1)}, u32[]{:S(2)}, u32[]{:S(2)}) collective-permute-start(bf16[256,1024]{1,0:T(8,128)(2,1)} %bitcast.17), channel_id=1, source_target_pairs={{0,4},{2,6},{4,0},{6,2},{8,12},{10,14},{12,8},{14,10},{16,20},{18,... | collective-permute-start | bytes 1572872 | tf_op jit(solution)/shard_map/ppermute | solution.py:250
  9.1 0.0 copy-done
  9.1 2.6 %convolution_convert_fusion.da_hbm = bf16[256,1024]{1,0:T(8,128)(2,1)} fusion(bf16[1024,1024]{1,0:T(8,128)(2,1)S(1)} %copy-done, bf16[1,256,1024]{2,1,0:T(8,128)(2,1)} %param.8), kind=kOutput, calls=%fused_computation | convolution fusion | flops 537133056 | bytes 3145728 | tf_op jit(solution)/shard_map/dot_general | solution.py:26
  11.7 1.9 %shard_map.84 = bf16[2,128,1024]{2,1,0:T(8,128)(2,1)} custom-call(s32[1]{0:T(128)} %bitcast.6.side_ref, bf16[256,1024]{1,0:T(8,128)(2,1)} %bitcast.21, bf16[256,1024]{1,0:T(8,128)(2,1)} %bitcast.25), custom_call_target="tpu_custom_call" | custom-call | tf_op jit(solution)/shard_map/pallas_call | solution.py:165
  13.5 1.5 %collective-permute-start.1 = (bf16[2,128,1024]{2,1,0:T(8,128)(2,1)}, bf16[2,128,1024]{2,1,0:T(8,128)(2,1)S(1)}, u32[]{:S(2)}, u32[]{:S(2)}) collective-permute-start(bf16[2,128,1024]{2,1,0:T(8,128)(2,1)} %shard_map.84), channel_id=1, source_target_pairs={{0,2},{2,0},{4,6},{6,4},{8,10},{10,8},{12,14},{14,12},{16,18},{18,... | collective-permute-start | bytes 1572872 | tf_op jit(solution)/shard_map/ppermute | solution.py:321
  15.1 0.0 collective-permute-start.10
  15.1 16.1 %collective-permute-done.11.refs_10_ = bf16[256,1024]{1,0:T(8,128)(2,1)} collective-permute-done((bf16[256,1024]{1,0:T(8,128)(2,1)}, bf16[256,1024]{1,0:T(8,128)(2,1)}, u32[]{:S(2)}, u32[]{:S(2)}) %collective-permute-start.11) | collective-permute-done | bytes 524320 | tf_op jit(solution)/shard_map/ppermute | solution.py:250
  31.2 0.0 collective-permute-start.12
  31.2 0.1 stack.30.meta_ref
  31.3 0.0 collective-permute-done.rim_hbm
  31.3 8.0 %shard_map.86 = (bf16[512,128]{1,0:T(8,128)(2,1)S(1)}, bf16[512,128]{1,0:T(8,128)(2,1)}, bf16[2,128,1024]{2,1,0:T(8,128)(2,1)S(1)}, bf16[128,1024]{1,0:T(8,128)(...) custom-call(s32[5]{0:T(128)S(1)} %stack.30.meta_ref, f32[1]{0:T(128)} %bitcast.4.bias_ref, ...), custom_call_target="tpu_custom_call" | custom-call | flops 603979776 | bytes 4194304 | tf_op jit(solution)/shard_map/pallas_call | solution.py:126
  39.3 0.0 copy-start.8
  39.3 0.0 copy-start.1
  39.3 2.5 %collective-permute-start.4 = (bf16[512,128]{1,0:T(8,128)(2,1)}, bf16[512,128]{1,0:T(8,128)(2,1)S(1)}, u32[]{:S(2)}, u32[]{:S(2)}) collective-permute-start(bf16[512,128]{1,0:T(8,128)(2,1)} %get-tuple-element.41), channel_id=1, source_target_pairs={{0,4},{2,6},{4,0},{6,2},{8,12},{10,14},{12,8},{14,10},{16,20},{18,... | collective-permute-start | bytes 393224 | tf_op jit(solution)/shard_map/ppermute | solution.py:250
  41.9 0.0 copy-done.8
  41.9 0.2 collective-permute-start.5
  42.1 0.1 stack.32.meta_ref
  42.2 0.0 collective-permute-done.1.rim_hbm
  42.2 0.9 collective-permute-start.2
  43.0 7.4 %shard_map.87 = (bf16[512,128]{1,0:T(8,128)(2,1)S(1)}, bf16[512,128]{1,0:T(8,128)(2,1)S(1)}, bf16[2,128,1024]{2,1,0:T(8,128)(2,1)S(1)}, bf16[128,1024]{1,0:T(8,1...) custom-call(s32[5]{0:T(128)S(1)} %stack.32.meta_ref, f32[1]{0:T(128)} %bitcast.10.bias_ref, ...), custom_call_target="tpu_custom_call" | custom-call | flops 603979776 | bytes 4194304 | tf_op jit(solution)/shard_map/pallas_call | solution.py:126
  50.5 0.0 copy-start.2
  50.5 0.0 copy-start.3
  50.5 0.0 copy-start.4
  50.5 0.0 copy-start.5
  50.5 0.0 copy-start.6
  50.5 0.0 copy-start.7
  50.5 0.0 collective-permute-done.10.refs_9_
  50.5 3.7 %collective-permute-start.3 = (bf16[2,128,1024]{2,1,0:T(8,128)(2,1)S(1)}, bf16[2,128,1024]{2,1,0:T(8,128)(2,1)S(1)}, u32[]{:S(2)}, u32[]{:S(2)}) collective-permute-start(bf16[2,128,1024]{2,1,0:T(8,128)(2,1)S(1)} %get-tuple-element.36), channel_id=1, source_target_pairs={{0,2},{2,0},{4,6},{6,4},{8,10},{10,8},{12,14},{14,12},{16,18},{18,... | collective-permute-start | bytes 1572872 | tf_op jit(solution)/shard_map/ppermute | solution.py:340
  54.3 0.0 collective-permute-done.4.refs_1_
  54.3 2.4 %collective-permute-start.7 = (bf16[512,128]{1,0:T(8,128)(2,1)S(1)}, bf16[512,128]{1,0:T(8,128)(2,1)S(1)}, u32[]{:S(2)}, u32[]{:S(2)}) collective-permute-start(bf16[512,128]{1,0:T(8,128)(2,1)S(1)} %get-tuple-element.43), channel_id=1, source_target_pairs={{0,4},{2,6},{4,0},{6,2},{8,12},{10,14},{12,8},{14,10},{16,20},{18,... | collective-permute-start | bytes 393224 | tf_op jit(solution)/shard_map/ppermute | solution.py:250
  56.7 0.0 collective-permute-done.5.refs_2_
  56.7 0.0 collective-permute-start.8
  56.7 3.6 %collective-permute-done.7.refs_5_ = bf16[512,128]{1,0:T(8,128)(2,1)S(1)} collective-permute-done((bf16[512,128]{1,0:T(8,128)(2,1)S(1)}, bf16[512,128]{1,0:T(8,128)(2,1)S(1)}, u32[]{:S(2)}, u32[]{:S(2)}) %collective-permute-start.7) | collective-permute-done | bytes 131104 | tf_op jit(solution)/shard_map/ppermute | solution.py:250
  60.3 0.0 collective-permute-start.6
  60.4 0.0 collective-permute-done.8.refs_6_
  60.4 0.5 collective-permute-start.9
  60.9 0.8 collective-permute-done.6.refs_3_
  61.7 0.2 collective-permute-done.9.refs_7_
  61.9 0.0 collective-permute-done.12.refs_11_
  61.9 0.0 copy-done.1
  61.9 2.1 %product.1 = (f32[128,512]{1,0:T(8,128)S(1)}, bf16[128,512]{1,0:T(8,128)(2,1)S(1)}, bf16[128,512]{1,0:T(8,128)(2,1)S(1)}, bf16[128,512]{1,0:T(8,128)(2,1)S(1)}) custom-call(s32[5]{0:T(128)S(1)} %stack.30.meta_ref, bf16[512,128]{1,0:T(8,128)(2,1)S(1)} %get-tuple-element.40.refs_0_, bf16[512,128]{1,0:T(8,128)(2,1)S(1)} %collective-permute-done.4.refs_1_, ...), custom_call_target="tpu_custom_call" | custom-call | tf_op jit(solution)/shard_map/product/pallas_call | solution.py:194
  64.0 4.4 %collective-permute-start.13 = (bf16[128,512]{1,0:T(8,128)(2,1)S(1)}, bf16[128,512]{1,0:T(8,128)(2,1)S(1)}, u32[]{:S(2)}, u32[]{:S(2)}) collective-permute-start(bf16[128,512]{1,0:T(8,128)(2,1)S(1)} %get-tuple-element.45), channel_id=1, source_target_pairs={{0,8},{2,10},{4,12},{6,14},{8,0},{10,2},{12,4},{14,6},{16,24},{18,... | collective-permute-start | bytes 393224 | tf_op jit(solution)/shard_map/ppermute | solution.py:250
  68.4 2.7 %collective-permute-start.14 = (bf16[128,512]{1,0:T(8,128)(2,1)S(1)}, bf16[128,512]{1,0:T(8,128)(2,1)S(1)}, u32[]{:S(2)}, u32[]{:S(2)}) collective-permute-start(bf16[128,512]{1,0:T(8,128)(2,1)S(1)} %get-tuple-element.46), channel_id=1, source_target_pairs={{0,16},{2,18},{4,20},{6,22},{8,24},{10,26},{12,28},{14,30},{16,0},... | collective-permute-start | bytes 393224 | tf_op jit(solution)/shard_map/ppermute | solution.py:250
  71.1 0.0 collective-permute-start.15
  71.1 3.3 %collective-permute-done.13.refs_0_ = bf16[128,512]{1,0:T(8,128)(2,1)S(1)} collective-permute-done((bf16[128,512]{1,0:T(8,128)(2,1)S(1)}, bf16[128,512]{1,0:T(8,128)(2,1)S(1)}, u32[]{:S(2)}, u32[]{:S(2)}) %collective-permute-start.13) | collective-permute-done | bytes 131104 | tf_op jit(solution)/shard_map/ppermute | solution.py:250
  74.4 6.9 %collective-permute-done.14.refs_1_ = bf16[128,512]{1,0:T(8,128)(2,1)S(1)} collective-permute-done((bf16[128,512]{1,0:T(8,128)(2,1)S(1)}, bf16[128,512]{1,0:T(8,128)(2,1)S(1)}, u32[]{:S(2)}, u32[]{:S(2)}) %collective-permute-start.14) | collective-permute-done | bytes 131104 | tf_op jit(solution)/shard_map/ppermute | solution.py:250
  81.3 0.0 collective-permute-done.15.refs_2_
  81.3 0.6 summed.1
  81.9 0.9 %collective-permute-start.16 = (bf16[64,512]{1,0:T(8,128)(2,1)S(1)}, bf16[64,512]{1,0:T(8,128)(2,1)S(1)}, u32[]{:S(2)}, u32[]{:S(2)}) collective-permute-start(bf16[64,512]{1,0:T(8,128)(2,1)S(1)} %get-tuple-element.49), channel_id=1, source_target_pairs={{0,2},{2,0},{4,6},{6,4},{8,10},{10,8},{12,14},{14,12},{16,18},{18,... | collective-permute-start | bytes 196616 | tf_op jit(solution)/shard_map/ppermute | solution.py:250
  82.9 0.0 collective-permute-done.2.long_ref
  82.9 0.0 collective-permute-done.3.near_ref
  82.9 0.0 copy-done.2
  82.9 0.0 copy-done.3
  82.9 0.0 copy-done.4
  82.9 0.0 copy-done.5
  82.9 0.0 copy-done.6
  82.9 0.0 copy-done.7
  82.9 2.0 %joined.1 = (bf16[256,1024]{1,0:T(8,128)(2,1)}, bf16[256,1024]{1,0:T(8,128)(2,1)}, bf16[256,1024]{1,0:T(8,128)(2,1)}) custom-call(s32[5]{0:T(128)S(1)} %stack.30.meta_ref, bf16[128,1024]{1,0:T(8,128)(2,1)S(1)} %copy-done.6, bf16[256,1024]{1,0:T(8,128)(2,1)S(1)} %copy-done.2, bf16[256,1024]{1,0:T(8,128)(2,1)S(1)} %copy-done.3, ...), custom_call_target="tpu_custom_call" | custom-call | tf_op jit(solution)/shard_map/joined/pallas_call | solution.py:239
  85.0 1.3 %collective-permute-done.16 = bf16[64,512]{1,0:T(8,128)(2,1)S(1)} collective-permute-done((bf16[64,512]{1,0:T(8,128)(2,1)S(1)}, bf16[64,512]{1,0:T(8,128)(2,1)S(1)}, u32[]{:S(2)}, u32[]{:S(2)}) %collective-permute-start.16) | collective-permute-done | bytes 65568 | tf_op jit(solution)/shard_map/ppermute | solution.py:250
  86.3 0.7 add_multiply_fusion
Async XLA Ops:
  0.6 8.4 %copy-start = (bf16[1024,1024]{1,0:T(8,128)(2,1)S(1)}, bf16[1024,1024]{1,0:T(8,128)(2,1)}, u32[]{:S(2)}) copy-start(bf16[1024,1024]{1,0:T(8,128)(2,1)} %param.9) | copy-start | bytes 6291460
  2.7 28.6 %collective-permute-start = (bf16[2,128,1024]{2,1,0:T(8,128)(2,1)}, bf16[2,128,1024]{2,1,0:T(8,128)(2,1)S(1)}, u32[]{:S(2)}, u32[]{:S(2)}) collective-permute-start(bf16[2,128,1024]{2,1,0:T(8,128)(2,1)} %shard_map.85), channel_id=1, source_target_pairs={{2,4},{4,2},{6,8},{8,6},{10,12},{12,10},{14,16},{16,14},{18,20},{2... | collective-permute-start | bytes 1572872 | tf_op jit(solution)/shard_map/ppermute | solution.py:317
  3.4 27.8 %collective-permute-start.11 = (bf16[256,1024]{1,0:T(8,128)(2,1)}, bf16[256,1024]{1,0:T(8,128)(2,1)}, u32[]{:S(2)}, u32[]{:S(2)}) collective-permute-start(bf16[256,1024]{1,0:T(8,128)(2,1)} %bitcast.17), channel_id=1, source_target_pairs={{0,4},{2,6},{4,0},{6,2},{8,12},{10,14},{12,8},{14,10},{16,20},{18,... | collective-permute-start | bytes 1572872 | tf_op jit(solution)/shard_map/ppermute | solution.py:250
  13.5 28.6 %collective-permute-start.1 = (bf16[2,128,1024]{2,1,0:T(8,128)(2,1)}, bf16[2,128,1024]{2,1,0:T(8,128)(2,1)S(1)}, u32[]{:S(2)}, u32[]{:S(2)}) collective-permute-start(bf16[2,128,1024]{2,1,0:T(8,128)(2,1)} %shard_map.84), channel_id=1, source_target_pairs={{0,2},{2,0},{4,6},{6,4},{8,10},{10,8},{12,14},{14,12},{16,18},{18,... | collective-permute-start | bytes 1572872 | tf_op jit(solution)/shard_map/ppermute | solution.py:321
  15.1 35.4 %collective-permute-start.10 = (bf16[256,1024]{1,0:T(8,128)(2,1)}, bf16[256,1024]{1,0:T(8,128)(2,1)}, u32[]{:S(2)}, u32[]{:S(2)}) collective-permute-start(bf16[256,1024]{1,0:T(8,128)(2,1)} %bitcast.18), channel_id=1, source_target_pairs={{0,1},{1,0},{2,3},{3,2},{4,5},{5,4},{6,7},{7,6},{8,9},{9,8},{10,11... | collective-permute-start | bytes 1572872 | tf_op jit(solution)/shard_map/ppermute | solution.py:254
  31.2 30.7 %collective-permute-start.12 = (bf16[256,1024]{1,0:T(8,128)(2,1)}, bf16[256,1024]{1,0:T(8,128)(2,1)}, u32[]{:S(2)}, u32[]{:S(2)}) collective-permute-start(bf16[256,1024]{1,0:T(8,128)(2,1)} %collective-permute-done.11.refs_10_), channel_id=1, source_target_pairs={{0,1},{1,0},{2,3},{3,2},{4,5},{5,4},{6,7},{7,6},{8,9},{9,8},{10,11... | collective-permute-start | bytes 1572872 | tf_op jit(solution)/shard_map/ppermute | solution.py:254
  39.3 2.6 %copy-start.8 = (bf16[2,128,1024]{2,1,0:T(8,128)(2,1)}, bf16[2,128,1024]{2,1,0:T(8,128)(2,1)S(1)}, u32[]{:S(2)}) copy-start(bf16[2,128,1024]{2,1,0:T(8,128)(2,1)S(1)} %get-tuple-element.35) | copy-start | bytes 1572868
  39.3 22.6 %copy-start.1 = (bf16[1,256,1024]{2,1,0:T(8,128)(2,1)S(1)}, bf16[1,256,1024]{2,1,0:T(8,128)(2,1)}, u32[]{:S(2)}) copy-start(bf16[1,256,1024]{2,1,0:T(8,128)(2,1)} %param.8) | copy-start | bytes 1572868
  39.3 14.9 %collective-permute-start.4 = (bf16[512,128]{1,0:T(8,128)(2,1)}, bf16[512,128]{1,0:T(8,128)(2,1)S(1)}, u32[]{:S(2)}, u32[]{:S(2)}) collective-permute-start(bf16[512,128]{1,0:T(8,128)(2,1)} %get-tuple-element.41), channel_id=1, source_target_pairs={{0,4},{2,6},{4,0},{6,2},{8,12},{10,14},{12,8},{14,10},{16,20},{18,... | collective-permute-start | bytes 393224 | tf_op jit(solution)/shard_map/ppermute | solution.py:250
  41.9 14.8 %collective-permute-start.5 = (bf16[512,128]{1,0:T(8,128)(2,1)S(1)}, bf16[512,128]{1,0:T(8,128)(2,1)S(1)}, u32[]{:S(2)}, u32[]{:S(2)}) collective-permute-start(bf16[512,128]{1,0:T(8,128)(2,1)S(1)} %get-tuple-element.40.refs_0_), channel_id=1, source_target_pairs={{0,1},{1,0},{2,3},{3,2},{4,5},{5,4},{6,7},{7,6},{8,9},{9,8},{10,11... | collective-permute-start | bytes 393224 | tf_op jit(solution)/shard_map/ppermute | solution.py:254
  42.2 40.7 %collective-permute-start.2 = (bf16[2,128,1024]{2,1,0:T(8,128)(2,1)}, bf16[2,128,1024]{2,1,0:T(8,128)(2,1)S(1)}, u32[]{:S(2)}, u32[]{:S(2)}) collective-permute-start(bf16[2,128,1024]{2,1,0:T(8,128)(2,1)} %copy-done.8), channel_id=1, source_target_pairs={{2,4},{4,2},{6,8},{8,6},{10,12},{12,10},{14,16},{16,14},{18,20},{2... | collective-permute-start | bytes 1572872 | tf_op jit(solution)/shard_map/ppermute | solution.py:330
  50.5 32.4 %copy-start.2 = (bf16[256,1024]{1,0:T(8,128)(2,1)S(1)}, bf16[256,1024]{1,0:T(8,128)(2,1)}, u32[]{:S(2)}) copy-start(bf16[256,1024]{1,0:T(8,128)(2,1)} %get-tuple-element.29.dk1_ref) | copy-start | bytes 1572868
  50.5 32.4 %copy-start.3 = (bf16[256,1024]{1,0:T(8,128)(2,1)S(1)}, bf16[256,1024]{1,0:T(8,128)(2,1)}, u32[]{:S(2)}) copy-start(bf16[256,1024]{1,0:T(8,128)(2,1)} %get-tuple-element.30.dv1_ref) | copy-start | bytes 1572868
  50.5 32.4 %copy-start.4 = (bf16[256,1024]{1,0:T(8,128)(2,1)S(1)}, bf16[256,1024]{1,0:T(8,128)(2,1)}, u32[]{:S(2)}) copy-start(bf16[256,1024]{1,0:T(8,128)(2,1)} %get-tuple-element.33.dk2_ref) | copy-start | bytes 1572868
  50.5 32.4 %copy-start.5 = (bf16[256,1024]{1,0:T(8,128)(2,1)S(1)}, bf16[256,1024]{1,0:T(8,128)(2,1)}, u32[]{:S(2)}) copy-start(bf16[256,1024]{1,0:T(8,128)(2,1)} %get-tuple-element.34.dv2_ref) | copy-start | bytes 1572868
  50.5 32.4 %copy-start.6 = (bf16[128,1024]{1,0:T(8,128)(2,1)S(1)}, bf16[128,1024]{1,0:T(8,128)(2,1)}, u32[]{:S(2)}) copy-start(bf16[128,1024]{1,0:T(8,128)(2,1)} %get-tuple-element.28.dq1_ref) | copy-start | bytes 786436
  50.5 32.4 %copy-start.7 = (bf16[128,1024]{1,0:T(8,128)(2,1)S(1)}, bf16[128,1024]{1,0:T(8,128)(2,1)}, u32[]{:S(2)}) copy-start(bf16[128,1024]{1,0:T(8,128)(2,1)} %get-tuple-element.32.dq2_ref) | copy-start | bytes 786436
  50.5 32.3 %collective-permute-start.3 = (bf16[2,128,1024]{2,1,0:T(8,128)(2,1)S(1)}, bf16[2,128,1024]{2,1,0:T(8,128)(2,1)S(1)}, u32[]{:S(2)}, u32[]{:S(2)}) collective-permute-start(bf16[2,128,1024]{2,1,0:T(8,128)(2,1)S(1)} %get-tuple-element.36), channel_id=1, source_target_pairs={{0,2},{2,0},{4,6},{6,4},{8,10},{10,8},{12,14},{14,12},{16,18},{18,... | collective-permute-start | bytes 1572872 | tf_op jit(solution)/shard_map/ppermute | solution.py:340
  54.3 6.1 %collective-permute-start.7 = (bf16[512,128]{1,0:T(8,128)(2,1)S(1)}, bf16[512,128]{1,0:T(8,128)(2,1)S(1)}, u32[]{:S(2)}, u32[]{:S(2)}) collective-permute-start(bf16[512,128]{1,0:T(8,128)(2,1)S(1)} %get-tuple-element.43), channel_id=1, source_target_pairs={{0,4},{2,6},{4,0},{6,2},{8,12},{10,14},{12,8},{14,10},{16,20},{18,... | collective-permute-start | bytes 393224 | tf_op jit(solution)/shard_map/ppermute | solution.py:250
  56.7 3.7 %collective-permute-start.8 = (bf16[512,128]{1,0:T(8,128)(2,1)S(1)}, bf16[512,128]{1,0:T(8,128)(2,1)S(1)}, u32[]{:S(2)}, u32[]{:S(2)}) collective-permute-start(bf16[512,128]{1,0:T(8,128)(2,1)S(1)} %get-tuple-element.42.refs_4_), channel_id=1, source_target_pairs={{0,1},{1,0},{2,3},{3,2},{4,5},{5,4},{6,7},{7,6},{8,9},{9,8},{10,11... | collective-permute-start | bytes 393224 | tf_op jit(solution)/shard_map/ppermute | solution.py:254
  60.3 1.3 %collective-permute-start.6 = (bf16[512,128]{1,0:T(8,128)(2,1)S(1)}, bf16[512,128]{1,0:T(8,128)(2,1)S(1)}, u32[]{:S(2)}, u32[]{:S(2)}) collective-permute-start(bf16[512,128]{1,0:T(8,128)(2,1)S(1)} %collective-permute-done.4.refs_1_), channel_id=1, source_target_pairs={{0,1},{1,0},{2,3},{3,2},{4,5},{5,4},{6,7},{7,6},{8,9},{9,8},{10,11... | collective-permute-start | bytes 393224 | tf_op jit(solution)/shard_map/ppermute | solution.py:254
  60.4 1.5 %collective-permute-start.9 = (bf16[512,128]{1,0:T(8,128)(2,1)S(1)}, bf16[512,128]{1,0:T(8,128)(2,1)S(1)}, u32[]{:S(2)}, u32[]{:S(2)}) collective-permute-start(bf16[512,128]{1,0:T(8,128)(2,1)S(1)} %collective-permute-done.7.refs_5_), channel_id=1, source_target_pairs={{0,1},{1,0},{2,3},{3,2},{4,5},{5,4},{6,7},{7,6},{8,9},{9,8},{10,11... | collective-permute-start | bytes 393224 | tf_op jit(solution)/shard_map/ppermute | solution.py:254
  64.0 10.4 %collective-permute-start.13 = (bf16[128,512]{1,0:T(8,128)(2,1)S(1)}, bf16[128,512]{1,0:T(8,128)(2,1)S(1)}, u32[]{:S(2)}, u32[]{:S(2)}) collective-permute-start(bf16[128,512]{1,0:T(8,128)(2,1)S(1)} %get-tuple-element.45), channel_id=1, source_target_pairs={{0,8},{2,10},{4,12},{6,14},{8,0},{10,2},{12,4},{14,6},{16,24},{18,... | collective-permute-start | bytes 393224 | tf_op jit(solution)/shard_map/ppermute | solution.py:250
  68.4 12.9 %collective-permute-start.14 = (bf16[128,512]{1,0:T(8,128)(2,1)S(1)}, bf16[128,512]{1,0:T(8,128)(2,1)S(1)}, u32[]{:S(2)}, u32[]{:S(2)}) collective-permute-start(bf16[128,512]{1,0:T(8,128)(2,1)S(1)} %get-tuple-element.46), channel_id=1, source_target_pairs={{0,16},{2,18},{4,20},{6,22},{8,24},{10,26},{12,28},{14,30},{16,0},... | collective-permute-start | bytes 393224 | tf_op jit(solution)/shard_map/ppermute | solution.py:250
  71.1 10.2 %collective-permute-start.15 = (bf16[128,512]{1,0:T(8,128)(2,1)S(1)}, bf16[128,512]{1,0:T(8,128)(2,1)S(1)}, u32[]{:S(2)}, u32[]{:S(2)}) collective-permute-start(bf16[128,512]{1,0:T(8,128)(2,1)S(1)} %get-tuple-element.47), channel_id=1, source_target_pairs={{0,24},{2,26},{4,28},{6,30},{8,16},{10,18},{12,20},{14,22},{16,8},... | collective-permute-start | bytes 393224 | tf_op jit(solution)/shard_map/ppermute | solution.py:250
  81.9 4.3 %collective-permute-start.16 = (bf16[64,512]{1,0:T(8,128)(2,1)S(1)}, bf16[64,512]{1,0:T(8,128)(2,1)S(1)}, u32[]{:S(2)}, u32[]{:S(2)}) collective-permute-start(bf16[64,512]{1,0:T(8,128)(2,1)S(1)} %get-tuple-element.49), channel_id=1, source_target_pairs={{0,2},{2,0},{4,6},{6,4},{8,10},{10,8},{12,14},{14,12},{16,18},{18,... | collective-permute-start | bytes 196616 | tf_op jit(solution)/shard_map/ppermute | solution.py:250

commit v2 on v1

--- a/solution.py
+++ b/solution.py
@@ -26,7 +26,7 @@
     return lax.dot_general(a, b, (dims, ((), ())), preferred_element_type=f32)
 
 
-def half_kernel(meta_ref, bias_ref, q_hbm, da_hbm, k_hbm, v_hbm, rim_hbm, keep_ref, send_ref, back_ref, dq_hbm, dk_hbm, dv_hbm,
+def half_kernel(meta_ref, bias_ref, thin_hbm, thick_hbm, rim_hbm, keep_ref, send_ref, back_ref, dq_hbm, own_hbm,
                 one_ref, wide_ref, two_ref, score_ref, dp_ref, p_ref, ds_ref, dq_ref, own_ref, in_sem, out_sem):
     side = meta_ref[0]
     y_digit = meta_ref[1]
@@ -35,23 +35,19 @@
     far_rows = pl.ds(pl.multiple_of((1 - side) * HALF, HALF), HALF)
     pairs = one_ref.shape[0]
 
-    def columns(number):
-        pair = 2 * (number // 2) + (y_digit if number % 2 == 0 else 1 - y_digit)
-        return pl.ds(pl.multiple_of(pair * PAIR, PAIR), PAIR)
+    def pair_of(number):
+        return 2 * (number // 2) + (y_digit if number % 2 == 0 else 1 - y_digit)
 
     def fetches(number):
-        cols = columns(number)
-        found = []
-        for which, (thin, thick) in enumerate(((q_hbm, k_hbm), (da_hbm, v_hbm))):
-            found.append((thin.at[near_rows, cols], one_ref.at[number, which]))
-            found.append((rim_hbm.at[which, :, cols], wide_ref.at[number, which, pl.ds(0, HALF)]))
-            found.append((thick.at[near_rows, cols], wide_ref.at[number, which, pl.ds(HALF, HALF)]))
-            found.append((thick.at[far_rows, cols], wide_ref.at[number, which, pl.ds(2 * HALF, HALF)]))
+        pair = pair_of(number)
+        found = [(thin_hbm.at[pair, :, side], one_ref.at[number])]
+        for place, source in enumerate((rim_hbm.at[pair], thick_hbm.at[pair, :, side], thick_hbm.at[pair, :, 1 - side])):
+            found.append((source, wide_ref.at[number, :, pl.ds(place * HALF, HALF)]))
         return [pltpu.make_async_copy(a, b, in_sem.at[number, place]) for place, (a, b) in enumerate(found)]
 
     def stores(number):
-        cols = columns(number)
-        found = [(dq_ref.at[number], dq_hbm.at[:, cols]), (own_ref.at[number, 0], dk_hbm.at[:, cols]), (own_ref.at[number, 1], dv_hbm.at[:, cols])]
+        pair = pair_of(number)
+        found = [(dq_ref.at[number], dq_hbm.at[pair]), (own_ref.at[number], own_hbm.at[pair])]
         return [pltpu.make_async_copy(a, b, out_sem.at[number, place]) for place, (a, b) in enumerate(found)]
 
     def multiply(number):
@@ -94,7 +90,7 @@
         at_ref[start + HEAD_DIM : start + PAIR, :] = at[HEAD_DIM:, HALF:].astype(bf16)
         for which, left in enumerate((ds_ref, p_ref)):
             part = contract(left[slot], two_ref[number % 3, which], NN)
-            back_ref[which, :, columns(number)] = part[:HALF].astype(bf16)
+            back_ref[pair_of(number), which] = part[:HALF].astype(bf16)
             own_ref[number, which, near_rows, :] = part[HALF : 2 * HALF].astype(bf16)
             own_ref[number, which, far_rows, :] = part[2 * HALF :].astype(bf16)
         dqt = contract(wide_ref[number, 0], ds_ref[slot], TN)
@@ -118,22 +114,22 @@
             copy.wait()
 
 
-def half_attention(meta, bias, q, da, k, v, rim):
-    rows, width = q.shape
-    pairs = width // PAIR
+def half_attention(meta, bias, thin, thick, rim):
+    pairs, _, blocks, _, _ = thick.shape
+    rows = blocks * HALF
+    width = pairs * PAIR
     in_hbm = pl.BlockSpec(memory_space=pltpu.HBM)
-    held = [pltpu.with_memory_space_constraint(array, pltpu.HBM) for array in (q, da, k, v)]
+    held = [pltpu.with_memory_space_constraint(array, pltpu.HBM) for array in (thin, thick)]
     return pl.pallas_call(
         half_kernel,
-        in_specs=[in_smem, in_smem] + [in_hbm] * 4 + [pl.BlockSpec(memory_space=pl.ANY)],
-        out_specs=[in_vmem] * 3 + [in_hbm] * 3,
+        in_specs=[in_smem, in_smem, in_hbm, in_hbm, pl.BlockSpec(memory_space=pl.ANY)],
+        out_specs=[in_vmem] * 3 + [in_hbm] * 2,
         out_shape=[
             jax.ShapeDtypeStruct((width // 2, HALF), bf16),
             jax.ShapeDtypeStruct((width // 2, HALF), bf16),
-            jax.ShapeDtypeStruct((2, HALF, width), bf16),
-            pltpu.HBM((HALF, width), bf16),
-            pltpu.HBM((rows, width), bf16),
-            pltpu.HBM((rows, width), bf16),
+            jax.ShapeDtypeStruct((pairs, 2, HALF, PAIR), bf16),
+            pltpu.HBM((pairs, HALF, PAIR), bf16),
+            pltpu.HBM((pairs, 2, rows, PAIR), bf16),
         ],
         scratch_shapes=[
             pltpu.VMEM((pairs, 2, HALF, PAIR), bf16),
@@ -145,8 +141,8 @@
             pltpu.VMEM((2, 3 * HALF, 2 * HALF), bf16),
             pltpu.VMEM((pairs, HALF, PAIR), bf16),
             pltpu.VMEM((pairs, 2, rows, PAIR), bf16),
-            pltpu.SemaphoreType.DMA((pairs, 8)),
-            pltpu.SemaphoreType.DMA((pairs, 3)),
+            pltpu.SemaphoreType.DMA((pairs, 4)),
+            pltpu.SemaphoreType.DMA((pairs, 2)),
         ],
         cost_estimate=pl.CostEstimate(flops=12 * HALF * 3 * HALF * width, bytes_accessed=16 * rows * width,
                                       transcendentals=HALF * 2 * HALF * width // HEAD_DIM),
@@ -155,21 +151,58 @@
 
 
 def rim_kernel(side_ref, k_ref, v_ref, out_ref):
-    out_ref[0] = k_ref[...]
-    out_ref[1] = v_ref[...]
+    for pair in range(out_ref.shape[0]):
+        cols = slice(pair * PAIR, (pair + 1) * PAIR)
+        out_ref[pair, 0] = k_ref[:, cols]
+        out_ref[pair, 1] = v_ref[:, cols]
 
 
 def packed_rim(side, k, v):
     width = k.shape[1]
     block = pl.BlockSpec((HALF, width), lambda i, s: (s[0], 0))
+    shape = (width // PAIR, 2, HALF, PAIR)
     return pl.pallas_call(
         rim_kernel,
         grid_spec=pltpu.PrefetchScalarGridSpec(
             num_scalar_prefetch=1, grid=(1,), in_specs=[block, block],
-            out_specs=pl.BlockSpec((2, HALF, width), lambda i, s: (0, 0, 0)),
+            out_specs=pl.BlockSpec(shape, lambda i, s: (0, 0, 0, 0)),
         ),
-        out_shape=jax.ShapeDtypeStruct((2, HALF, width), bf16),
+        out_shape=jax.ShapeDtypeStruct(shape, bf16),
     )(side, k, v)
+
+
+def prepare_kernel(meta_ref, q_ref, k_ref, v_ref, g_ref, w_ref, thin_ref, thick_ref, rim_ref):
+    pairs, _, blocks, _, _ = thin_ref.shape
+    for pair in range(pairs):
+        cols = slice(pair * PAIR, (pair + 1) * PAIR)
+        for block in range(blocks):
+            rows = slice(block * HALF, (block + 1) * HALF)
+            thin_ref[pair, 0, block] = q_ref[rows, cols]
+            thick_ref[pair, 0, block] = k_ref[rows, cols]
+            thick_ref[pair, 1, block] = v_ref[rows, cols]
+        rim_rows = pl.ds(pl.multiple_of((1 - meta_ref[0]) * HALF, HALF), HALF)
+        rim_ref[pair, 0] = k_ref[rim_rows, cols]
+        rim_ref[pair, 1] = v_ref[rim_rows, cols]
+    step = 2 * PAIR
+    for col in range(0, w_ref.shape[0], step):
+        part = contract(g_ref[...], w_ref[col : col + step, :], NT).astype(bf16)
+        for pair in range(2):
+            for block in range(blocks):
+                thin_ref[col // PAIR + pair, 1, block] = part[block * HALF : (block + 1) * HALF, pair * PAIR : (pair + 1) * PAIR]
+
+
+def prepared(meta, q, k, v, g, w):
+    rows, width = q.shape
+    pairs, blocks = width // PAIR, rows // HALF
+    whole = jax.ShapeDtypeStruct((pairs, 2, blocks, HALF, PAIR), bf16)
+    return pl.pallas_call(
+        prepare_kernel,
+        in_specs=[in_smem] + [in_vmem] * 5,
+        out_specs=[in_vmem] * 3,
+        out_shape=[whole, whole, jax.ShapeDtypeStruct((pairs, 2, HALF, PAIR), bf16)],
+        cost_estimate=pl.CostEstimate(flops=2 * rows * width * width, bytes_accessed=14 * rows * width + 2 * width * width, transcendentals=0),
+        name="prepared",
+    )(meta, q, k, v, g, w)
 
 
 def product_kernel(meta_ref, *refs):
@@ -224,23 +257,25 @@
     )(meta, own, *pieces)
 
 
-def join_kernel(meta_ref, dq1_ref, dk1_ref, dv1_ref, dq2_ref, dk2_ref, dv2_ref, long_ref, near_ref, dq_out, dk_out, dv_out):
+def join_kernel(meta_ref, dq1_ref, own1_ref, dq2_ref, own2_ref, long_ref, near_ref, dq_out, dk_out, dv_out):
     side = meta_ref[0]
     for row, rim, dq_ref in ((side, long_ref, dq1_ref), (1 - side, near_ref, dq2_ref)):
         rows = pl.ds(pl.multiple_of(row * HALF, HALF), HALF)
-        dq_out[rows, :] = dq_ref[...]
-        for which, (one, two, out) in enumerate(((dk1_ref, dk2_ref, dk_out), (dv1_ref, dv2_ref, dv_out))):
-            total = one[rows, :].astype(f32) + two[rows, :].astype(f32) + rim[which].astype(f32)
-            out[rows, :] = total.astype(bf16)
-
-
-def joined(meta, own1, own2, from_long, from_near):
-    shape = jax.ShapeDtypeStruct(own1[1].shape, bf16)
+        for pair in range(dq1_ref.shape[0]):
+            cols = slice(pair * PAIR, (pair + 1) * PAIR)
+            dq_out[rows, cols] = dq_ref[pair]
+            for which, out in enumerate((dk_out, dv_out)):
+                total = own1_ref[pair, which, rows].astype(f32) + own2_ref[pair, which, rows].astype(f32)
+                out[rows, cols] = (total + rim[pair, which].astype(f32)).astype(bf16)
+
+
+def joined(meta, own1, own2, from_long, from_near, shape):
+    out = jax.ShapeDtypeStruct(shape, bf16)
     return pl.pallas_call(
         join_kernel,
-        in_specs=[in_smem] + [in_vmem] * 8,
+        in_specs=[in_smem] + [in_vmem] * 6,
         out_specs=[in_vmem] * 3,
-        out_shape=[shape] * 3,
+        out_shape=[out] * 3,
         compiler_params=pltpu.CompilerParams(vmem_limit_bytes=12 << 20),
         name="joined",
     )(meta, *own1, *own2, from_long, from_near)
@@ -315,9 +350,7 @@
 
     rim1 = packed_rim(metas[0][:1], k, v)
     first_rim = lax.ppermute(rim1, "seq", long_pairs)
-    dattn = contract(g, out_weight, NT).astype(bf16)
-    rim2 = packed_rim(metas[1][:1], k, v)
-    rim2, dattn = lax.optimization_barrier((rim2, dattn))
+    thin, thick, rim2 = prepared(metas[0], q, k, v, g, out_weight)
     second_rim = lax.ppermute(rim2, "seq", near_pairs)
 
     if direct:
@@ -326,13 +359,13 @@
         g_y_dp = turned(g_y, dp_count)[0]
         gs = [g, g_dp, g_y, g_y_dp]
 
-    keep1, send1, back1, *own1 = half_attention(metas[0], bias[0], q, dattn, k, v, first_rim)
+    keep1, send1, back1, *own1 = half_attention(metas[0], bias[0], thin, thick, first_rim)
     from_long = lax.ppermute(back1, "seq", long_pairs)
     if direct:
         at_y1 = swapped(send1, 2, count)
         at_dp1 = turned(keep1, dp_count)[0]
         at_y_dp1 = turned(at_y1, dp_count)[0]
-    keep2, send2, back2, *own2 = half_attention(metas[1], bias[1], q, dattn, k, v, second_rim)
+    keep2, send2, back2, *own2 = half_attention(metas[1], bias[1], thin, thick, second_rim)
     if direct:
         at_y2 = swapped(send2, 2, count)
         at_dp2 = turned(keep2, dp_count)[0]
@@ -350,7 +383,7 @@
         wo_grad = kept + swapped(sent, 1, count).astype(f32)
     else:
         wo_grad = general_sum((keep1, send1), (keep2, send2), g, sides, place, mine, y_digit, count, dp_count)
-    dq, dk, dv = joined(metas[0], own1, own2, from_long, from_near)
+    dq, dk, dv = joined(metas[0], own1, own2, from_long, from_near, q.shape)
     return dq[None], dk[None], dv[None], wo_grad * frames ** -0.5
 
 

time: 87.3 us -> 81.9 us (0.938)
  waiting for transfers between devices: 32.3 us -> 28.8 us
  matrix products: 2.61 us -> 0 us
  starting transfers between devices: 26.3 us -> 24.2 us
  Pallas kernels: 24 us -> 25.6 us
  local copies, waits for them, and re-layouts: 0.22 us -> 1.5 us
    pallas_call x3 -> x4, Pallas kernels: 17.4 us -> 21.8 us  [the longest x2 15.1 us: half_attention(): pl.pallas_call(half_kernel, in_specs=[in_smem, in_smem, in_hbm, in_hbm, p...]
    ppermute x7, waiting for transfers between devices: 31.3 us -> 27.8 us  [swapped(): return lax.ppermute(value, 'seq', [(i, i ^ stride) for i in range(count)])]
    dot_general x1 -> x0, matrix products: 2.61 us -> none  [contract(): return lax.dot_general(a, b, (dims, ((), ())), preferred_element_type=f32)]
    ppermute x7, starting transfers between devices: 18.7 us -> 16.2 us  [swapped(): return lax.ppermute(value, 'seq', [(i, i ^ stride) for i in range(count)])]
    pallas_call x2 -> x1, Pallas kernels: 3.86 us -> 1.92 us  [packed_rim(): pl.pallas_call(rim_kernel, grid_spec=pltpu.PrefetchScalarGridSpec(num_sca...]
    ppermute x1, starting transfers between devices: 1.55 us -> 2.72 us  [on_device(): second_rim = lax.ppermute(rim2, 'seq', near_pairs)]
  transfers between devices with their start and end apart: 17 -> 17, of which waited for: 7 -> 7; matrix products, arithmetic and copies ran while one was open for 3% -> 1% of each run, Pallas kernels for 25% -> 31%
where the time goes in v2:
time: 81.9 us; the launch traced here: 81.6 us
  waiting for transfers between devices  28.8 us (35%)
  Pallas kernels  25.6 us (31%)
  starting transfers between devices  24.2 us (30%)
  local copies, waits for them, and re-layouts  1.5 us (2%)
  between operations  0.83 us (1%)
    ppermute x7, waiting for transfers between devices, swapped(): return lax.ppermute(value, 'seq', [(i, i ^ stride) for i in range(count)])  27.8 us
    ppermute x7, starting transfers between devices, swapped(): return lax.ppermute(value, 'seq', [(i, i ^ stride) for i in range(count)])  16.2 us
    pallas_call x2, Pallas kernels, half_attention(): pl.pallas_call(half_kernel, in_specs=[in_smem, in_smem, in_hbm, in_hbm, p...  15.1 us
    pallas_call x1, Pallas kernels, prepared(): pl.pallas_call(prepare_kernel, in_specs=[in_smem] + [in_vmem] * 5, out_sp...  4.62 us
    ppermute x1, starting transfers between devices, on_device(): from_near = lax.ppermute(back2, 'seq', near_pairs)  3.03 us
    ppermute x1, starting transfers between devices, on_device(): second_rim = lax.ppermute(rim2, 'seq', near_pairs)  2.72 us
    pallas_call x1, Pallas kernels, joined(): pl.pallas_call(join_kernel, in_specs=[in_smem] + [in_vmem] * 6, out_specs...  2.06 us
    pallas_call x1, Pallas kernels, packed_rim(): pl.pallas_call(rim_kernel, grid_spec=pltpu.PrefetchScalarGridSpec(num_sca...  1.92 us
  transfers between devices with their start and end apart: 17, of which 7 were waited for; matrix products, arithmetic and copies ran while one was open for 1% of the time, Pallas kernels for 31%

profile of v2, /device:TPU:0, one launch (start us, length us, event | category | flops | bytes accessed | tf_op | source)
XLA Modules:
  0.0 81.6 jit_solution(17030922903656103453)
XLA Ops:
  0.6 3.1 %collective-permute-start.11 = (bf16[256,1024]{1,0:T(8,128)(2,1)}, bf16[256,1024]{1,0:T(8,128)(2,1)S(1)}, u32[]{:S(2)}, u32[]{:S(2)}) collective-permute-start(bf16[256,1024]{1,0:T(8,128)(2,1)} %bitcast.14), channel_id=1, source_target_pairs={{0,4},{2,6},{4,0},{6,2},{8,12},{10,14},{12,8},{14,10},{16,20},{18,... | collective-permute-start | bytes 1572872 | tf_op jit(solution)/shard_map/ppermute | solution.py:285
  3.7 1.9 %shard_map.84 = bf16[8,2,128,128]{3,2,1,0:T(8,128)(2,1)} custom-call(s32[1]{0:T(128)} %bitcast.side_ref, bf16[256,1024]{1,0:T(8,128)(2,1)} %bitcast.18, bf16[256,1024]{1,0:T(8,128)(2,1)} %bitcast.20), custom_call_target="tpu_custom_call" | custom-call | tf_op jit(solution)/shard_map/pallas_call | solution.py:164
  5.6 0.7 collective-permute-start
  6.3 0.6 stack.30.meta_ref
  7.0 0.0 copy-start
  7.0 0.0 copy-start.5
  7.0 4.6 %prepared.1 = (bf16[8,2,2,128,128]{4,3,2,1,0:T(8,128)(2,1)}, bf16[8,2,2,128,128]{4,3,2,1,0:T(8,128)(2,1)}, bf16[8,2,128,128]{3,2,1,0:T(8,128)(2,1)}) custom-call(s32[5]{0:T(128)} %stack.30.meta_ref, bf16[256,1024]{1,0:T(8,128)(2,1)} %bitcast.22, bf16[256,1024]{1,0:T(8,128)(2,1)} %bitcast.19, bf16[256,1024]{1,0:T(8,128)(2,1)} %bitcast.21, ...), custom_call_target="tpu_custom_call" | custom-call | flops 536870912 | bytes 5767168 | tf_op jit(solution)/shard_map/prepared/pallas_call | solution.py:198
  11.6 2.7 %collective-permute-start.1 = (bf16[8,2,128,128]{3,2,1,0:T(8,128)(2,1)}, bf16[8,2,128,128]{3,2,1,0:T(8,128)(2,1)S(1)}, u32[]{:S(2)}, u32[]{:S(2)}) collective-permute-start(bf16[8,2,128,128]{3,2,1,0:T(8,128)(2,1)} %get-tuple-element.30), channel_id=1, source_target_pairs={{0,2},{2,0},{4,6},{6,4},{8,10},{10,8},{12,14},{14,12},{16,18},{18,... | collective-permute-start | bytes 1572872 | tf_op jit(solution)/shard_map/ppermute | solution.py:354
  14.3 0.0 copy-done
  14.3 0.0 collective-permute-start.10
  14.3 12.1 %collective-permute-done.11.refs_10_ = bf16[256,1024]{1,0:T(8,128)(2,1)S(1)} collective-permute-done((bf16[256,1024]{1,0:T(8,128)(2,1)}, bf16[256,1024]{1,0:T(8,128)(2,1)S(1)}, u32[]{:S(2)}, u32[]{:S(2)}) %collective-permute-start.11) | collective-permute-done | bytes 524320 | tf_op jit(solution)/shard_map/ppermute | solution.py:285
  26.4 0.0 collective-permute-start.12
  26.4 0.0 collective-permute-done.rim_hbm
  26.4 0.0 copy-done.5
  26.4 7.9 %shard_map.85 = (bf16[512,128]{1,0:T(8,128)(2,1)S(1)}, bf16[512,128]{1,0:T(8,128)(2,1)}, bf16[8,2,128,128]{3,2,1,0:T(8,128)(2,1)S(1)}, bf16[8,128,128]{2,1,0:T(8,128)(2,1)}, bf16[8,2,256,128]{3,2,1,0:T(8,128)(2,1)}) custom-call(s32[5]{0:T(128)S(1)} %copy-done.5, f32[1]{0:T(128)} %bitcast.4.bias_ref, bf16[8,2,2,128,128]{4,3,2,1,0:T(8,128)(2,1)} %get-tuple-element.26.thin_hbm, ...), custom_call_target="tpu_custom_call" | custom-call | flops 603979776 | bytes 4194304 | tf_op jit(solution)/shard_map/pallas_call | solution.py:123
  34.3 0.0 copy-start.6
  34.3 0.8 copy-done.6
  35.1 2.4 %collective-permute-start.4 = (bf16[512,128]{1,0:T(8,128)(2,1)}, bf16[512,128]{1,0:T(8,128)(2,1)S(1)}, u32[]{:S(2)}, u32[]{:S(2)}) collective-permute-start(bf16[512,128]{1,0:T(8,128)(2,1)} %get-tuple-element.39), channel_id=1, source_target_pairs={{0,4},{2,6},{4,0},{6,2},{8,12},{10,14},{12,8},{14,10},{16,20},{18,... | collective-permute-start | bytes 393224 | tf_op jit(solution)/shard_map/ppermute | solution.py:285
  37.5 0.2 collective-permute-start.5
  37.7 0.1 stack.32.meta_ref
  37.8 0.0 collective-permute-done.1.rim_hbm
  37.8 0.9 %collective-permute-start.2 = (bf16[8,2,128,128]{3,2,1,0:T(8,128)(2,1)}, bf16[8,2,128,128]{3,2,1,0:T(8,128)(2,1)S(1)}, u32[]{:S(2)}, u32[]{:S(2)}) collective-permute-start(bf16[8,2,128,128]{3,2,1,0:T(8,128)(2,1)} %copy-done.6), channel_id=1, source_target_pairs={{2,4},{4,2},{6,8},{8,6},{10,12},{12,10},{14,16},{16,14},{18,20},{2... | collective-permute-start | bytes 1572872 | tf_op jit(solution)/shard_map/ppermute | solution.py:363
  38.7 7.2 %shard_map.86 = (bf16[512,128]{1,0:T(8,128)(2,1)S(1)}, bf16[512,128]{1,0:T(8,128)(2,1)S(1)}, bf16[8,2,128,128]{3,2,1,0:T(8,128)(2,1)S(1)}, bf16[8,128,128]{2,1,0:T(8,128)(2,1)}, bf16[8,2,256,128]{3,2,1,0:T(8,128)(2,1)}) custom-call(s32[5]{0:T(128)S(1)} %stack.32.meta_ref, f32[1]{0:T(128)} %bitcast.10.bias_ref, ...), custom_call_target="tpu_custom_call" | custom-call | flops 603979776 | bytes 4194304 | tf_op jit(solution)/shard_map/pallas_call | solution.py:123
  45.9 0.0 copy-start.1
  45.9 0.0 copy-start.2
  45.9 0.0 copy-start.3
  45.9 0.0 copy-start.4
  46.0 0.0 collective-permute-done.10.refs_9_
  46.0 3.0 %collective-permute-start.3 = (bf16[8,2,128,128]{3,2,1,0:T(8,128)(2,1)S(1)}, bf16[8,2,128,128]{3,2,1,0:T(8,128)(2,1)S(1)}, u32[]{:S(2)}, u32[]{:S(2)}) collective-permute-start(bf16[8,2,128,128]{3,2,1,0:T(8,128)(2,1)S(1)} %get-tuple-element.34), channel_id=1, source_target_pairs={{0,2},{2,0},{4,6},{6,4},{8,10},{10,8},{12,14},{14,12},{16,18},{18,... | collective-permute-start | bytes 1572872 | tf_op jit(solution)/shard_map/ppermute | solution.py:373
  49.0 0.0 collective-permute-done.4.refs_1_
  49.0 2.7 %collective-permute-start.7 = (bf16[512,128]{1,0:T(8,128)(2,1)S(1)}, bf16[512,128]{1,0:T(8,128)(2,1)S(1)}, u32[]{:S(2)}, u32[]{:S(2)}) collective-permute-start(bf16[512,128]{1,0:T(8,128)(2,1)S(1)} %get-tuple-element.41), channel_id=1, source_target_pairs={{0,4},{2,6},{4,0},{6,2},{8,12},{10,14},{12,8},{14,10},{16,20},{18,... | collective-permute-start | bytes 393224 | tf_op jit(solution)/shard_map/ppermute | solution.py:285
  51.8 0.0 collective-permute-done.5.refs_2_
  51.8 0.0 collective-permute-start.8
  51.8 3.8 %collective-permute-done.7.refs_5_ = bf16[512,128]{1,0:T(8,128)(2,1)S(1)} collective-permute-done((bf16[512,128]{1,0:T(8,128)(2,1)S(1)}, bf16[512,128]{1,0:T(8,128)(2,1)S(1)}, u32[]{:S(2)}, u32[]{:S(2)}) %collective-permute-start.7) | collective-permute-done | bytes 131104 | tf_op jit(solution)/shard_map/ppermute | solution.py:285
  55.6 0.0 collective-permute-start.6
  55.6 0.0 collective-permute-done.8.refs_6_
  55.6 0.5 collective-permute-start.9
  56.1 0.8 %collective-permute-done.6.refs_3_ = bf16[512,128]{1,0:T(8,128)(2,1)S(1)} collective-permute-done((bf16[512,128]{1,0:T(8,128)(2,1)S(1)}, bf16[512,128]{1,0:T(8,128)(2,1)S(1)}, u32[]{:S(2)}, u32[]{:S(2)}) %collective-permute-start.6) | collective-permute-done | bytes 131104 | tf_op jit(solution)/shard_map/ppermute | solution.py:289
  56.9 0.2 collective-permute-done.9.refs_7_
  57.1 0.0 collective-permute-done.12.refs_11_
  57.1 1.3 %product.1 = (f32[128,512]{1,0:T(8,128)S(1)}, bf16[128,512]{1,0:T(8,128)(2,1)S(1)}, bf16[128,512]{1,0:T(8,128)(2,1)S(1)}, bf16[128,512]{1,0:T(8,128)(2,1)S(1)}) custom-call(s32[5]{0:T(128)S(1)} %copy-done.5, bf16[512,128]{1,0:T(8,128)(2,1)S(1)} %get-tuple-element.38.refs_0_, bf16[512,128]{1,0:T(8,128)(2,1)S(1)} %collective-permute-done.4.refs_1_, ...), custom_call_target="tpu_custom_call" | custom-call | tf_op jit(solution)/shard_map/product/pallas_call | solution.py:227
  58.4 4.7 %collective-permute-start.13 = (bf16[128,512]{1,0:T(8,128)(2,1)S(1)}, bf16[128,512]{1,0:T(8,128)(2,1)S(1)}, u32[]{:S(2)}, u32[]{:S(2)}) collective-permute-start(bf16[128,512]{1,0:T(8,128)(2,1)S(1)} %get-tuple-element.43), channel_id=1, source_target_pairs={{0,8},{2,10},{4,12},{6,14},{8,0},{10,2},{12,4},{14,6},{16,24},{18,... | collective-permute-start | bytes 393224 | tf_op jit(solution)/shard_map/ppermute | solution.py:285
  63.1 2.7 %collective-permute-start.14 = (bf16[128,512]{1,0:T(8,128)(2,1)S(1)}, bf16[128,512]{1,0:T(8,128)(2,1)S(1)}, u32[]{:S(2)}, u32[]{:S(2)}) collective-permute-start(bf16[128,512]{1,0:T(8,128)(2,1)S(1)} %get-tuple-element.44), channel_id=1, source_target_pairs={{0,16},{2,18},{4,20},{6,22},{8,24},{10,26},{12,28},{14,30},{16,0},... | collective-permute-start | bytes 393224 | tf_op jit(solution)/shard_map/ppermute | solution.py:285
  65.8 0.0 collective-permute-start.15
  65.8 3.4 %collective-permute-done.13.refs_0_ = bf16[128,512]{1,0:T(8,128)(2,1)S(1)} collective-permute-done((bf16[128,512]{1,0:T(8,128)(2,1)S(1)}, bf16[128,512]{1,0:T(8,128)(2,1)S(1)}, u32[]{:S(2)}, u32[]{:S(2)}) %collective-permute-start.13) | collective-permute-done | bytes 131104 | tf_op jit(solution)/shard_map/ppermute | solution.py:285
  69.1 6.9 %collective-permute-done.14.refs_1_ = bf16[128,512]{1,0:T(8,128)(2,1)S(1)} collective-permute-done((bf16[128,512]{1,0:T(8,128)(2,1)S(1)}, bf16[128,512]{1,0:T(8,128)(2,1)S(1)}, u32[]{:S(2)}, u32[]{:S(2)}) %collective-permute-start.14) | collective-permute-done | bytes 131104 | tf_op jit(solution)/shard_map/ppermute | solution.py:285
  76.0 0.0 collective-permute-done.15.refs_2_
  76.0 0.6 summed.1
  76.6 0.7 collective-permute-start.16
  77.3 0.0 collective-permute-done.2.long_ref
  77.3 0.0 collective-permute-done.3.near_ref
  77.3 0.0 copy-done.1
  77.3 0.0 copy-done.2
  77.3 0.0 copy-done.3
  77.3 0.0 copy-done.4
  77.3 2.1 %joined.1 = (bf16[256,1024]{1,0:T(8,128)(2,1)}, bf16[256,1024]{1,0:T(8,128)(2,1)}, bf16[256,1024]{1,0:T(8,128)(2,1)}) custom-call(s32[5]{0:T(128)S(1)} %copy-done.5, bf16[8,128,128]{2,1,0:T(8,128)(2,1)S(1)} %copy-done.3, bf16[8,2,256,128]{3,2,1,0:T(8,128)(2,1)S(1)} %copy-done.1, bf16[8,128,128]{2,1,0:T(8,128)(2,1)S(1)} %copy-done.4, ...), custom_call_target="tpu_custom_call" | custom-call | tf_op jit(solution)/shard_map/joined/pallas_call | solution.py:274
  79.4 1.6 %collective-permute-done.16 = bf16[64,512]{1,0:T(8,128)(2,1)S(1)} collective-permute-done((bf16[64,512]{1,0:T(8,128)(2,1)S(1)}, bf16[64,512]{1,0:T(8,128)(2,1)S(1)}, u32[]{:S(2)}, u32[]{:S(2)}) %collective-permute-start.16) | collective-permute-done | bytes 65568 | tf_op jit(solution)/shard_map/ppermute | solution.py:285
  81.0 0.7 add_multiply_fusion
Async XLA Ops:
  0.6 25.8 %collective-permute-start.11 = (bf16[256,1024]{1,0:T(8,128)(2,1)}, bf16[256,1024]{1,0:T(8,128)(2,1)S(1)}, u32[]{:S(2)}, u32[]{:S(2)}) collective-permute-start(bf16[256,1024]{1,0:T(8,128)(2,1)} %bitcast.14), channel_id=1, source_target_pairs={{0,4},{2,6},{4,0},{6,2},{8,12},{10,14},{12,8},{14,10},{16,20},{18,... | collective-permute-start | bytes 1572872 | tf_op jit(solution)/shard_map/ppermute | solution.py:285
  5.6 20.8 %collective-permute-start = (bf16[8,2,128,128]{3,2,1,0:T(8,128)(2,1)}, bf16[8,2,128,128]{3,2,1,0:T(8,128)(2,1)S(1)}, u32[]{:S(2)}, u32[]{:S(2)}) collective-permute-start(bf16[8,2,128,128]{3,2,1,0:T(8,128)(2,1)} %shard_map.84), channel_id=1, source_target_pairs={{2,4},{4,2},{6,8},{8,6},{10,12},{12,10},{14,16},{16,14},{18,20},{2... | collective-permute-start | bytes 1572872 | tf_op jit(solution)/shard_map/ppermute | solution.py:352
  7.0 7.3 %copy-start = (bf16[1,256,1024]{2,1,0:T(8,128)(2,1)S(1)}, bf16[1,256,1024]{2,1,0:T(8,128)(2,1)}, u32[]{:S(2)}) copy-start(bf16[1,256,1024]{2,1,0:T(8,128)(2,1)} %param.8) | copy-start | bytes 1572868
  7.0 19.5 %copy-start.5 = (s32[5]{0:T(128)S(1)}, s32[5]{0:T(128)}, u32[]{:S(2)}) copy-start(s32[5]{0:T(128)} %stack.30.meta_ref) | copy-start | bytes 64
  11.6 26.2 %collective-permute-start.1 = (bf16[8,2,128,128]{3,2,1,0:T(8,128)(2,1)}, bf16[8,2,128,128]{3,2,1,0:T(8,128)(2,1)S(1)}, u32[]{:S(2)}, u32[]{:S(2)}) collective-permute-start(bf16[8,2,128,128]{3,2,1,0:T(8,128)(2,1)} %get-tuple-element.30), channel_id=1, source_target_pairs={{0,2},{2,0},{4,6},{6,4},{8,10},{10,8},{12,14},{14,12},{16,18},{18,... | collective-permute-start | bytes 1572872 | tf_op jit(solution)/shard_map/ppermute | solution.py:354
  14.3 31.7 %collective-permute-start.10 = (bf16[256,1024]{1,0:T(8,128)(2,1)S(1)}, bf16[256,1024]{1,0:T(8,128)(2,1)S(1)}, u32[]{:S(2)}, u32[]{:S(2)}) collective-permute-start(bf16[256,1024]{1,0:T(8,128)(2,1)S(1)} %bitcast.16), channel_id=1, source_target_pairs={{0,1},{1,0},{2,3},{3,2},{4,5},{5,4},{6,7},{7,6},{8,9},{9,8},{10,11... | collective-permute-start | bytes 1572872 | tf_op jit(solution)/shard_map/ppermute | solution.py:289
  26.4 30.7 %collective-permute-start.12 = (bf16[256,1024]{1,0:T(8,128)(2,1)S(1)}, bf16[256,1024]{1,0:T(8,128)(2,1)S(1)}, u32[]{:S(2)}, u32[]{:S(2)}) collective-permute-start(bf16[256,1024]{1,0:T(8,128)(2,1)S(1)} %collective-permute-done.11.refs_10_), channel_id=1, source_target_pairs={{0,1},{1,0},{2,3},{3,2},{4,5},{5,4},{6,7},{7,6},{8,9},{9,8},{10,11... | collective-permute-start | bytes 1572872 | tf_op jit(solution)/shard_map/ppermute | solution.py:289
  34.3 0.8 copy-start.6
  35.1 13.9 %collective-permute-start.4 = (bf16[512,128]{1,0:T(8,128)(2,1)}, bf16[512,128]{1,0:T(8,128)(2,1)S(1)}, u32[]{:S(2)}, u32[]{:S(2)}) collective-permute-start(bf16[512,128]{1,0:T(8,128)(2,1)} %get-tuple-element.39), channel_id=1, source_target_pairs={{0,4},{2,6},{4,0},{6,2},{8,12},{10,14},{12,8},{14,10},{16,20},{18,... | collective-permute-start | bytes 393224 | tf_op jit(solution)/shard_map/ppermute | solution.py:285
  37.5 14.3 %collective-permute-start.5 = (bf16[512,128]{1,0:T(8,128)(2,1)S(1)}, bf16[512,128]{1,0:T(8,128)(2,1)S(1)}, u32[]{:S(2)}, u32[]{:S(2)}) collective-permute-start(bf16[512,128]{1,0:T(8,128)(2,1)S(1)} %get-tuple-element.38.refs_0_), channel_id=1, source_target_pairs={{0,1},{1,0},{2,3},{3,2},{4,5},{5,4},{6,7},{7,6},{8,9},{9,8},{10,11... | collective-permute-start | bytes 393224 | tf_op jit(solution)/shard_map/ppermute | solution.py:289
  37.8 39.5 %collective-permute-start.2 = (bf16[8,2,128,128]{3,2,1,0:T(8,128)(2,1)}, bf16[8,2,128,128]{3,2,1,0:T(8,128)(2,1)S(1)}, u32[]{:S(2)}, u32[]{:S(2)}) collective-permute-start(bf16[8,2,128,128]{3,2,1,0:T(8,128)(2,1)} %copy-done.6), channel_id=1, source_target_pairs={{2,4},{4,2},{6,8},{8,6},{10,12},{12,10},{14,16},{16,14},{18,20},{2... | collective-permute-start | bytes 1572872 | tf_op jit(solution)/shard_map/ppermute | solution.py:363
  45.9 31.4 %copy-start.1 = (bf16[8,2,256,128]{3,2,1,0:T(8,128)(2,1)S(1)}, bf16[8,2,256,128]{3,2,1,0:T(8,128)(2,1)}, u32[]{:S(2)}) copy-start(bf16[8,2,256,128]{3,2,1,0:T(8,128)(2,1)} %get-tuple-element.29.own1_ref) | copy-start | bytes 3145732
  45.9 31.4 %copy-start.2 = (bf16[8,2,256,128]{3,2,1,0:T(8,128)(2,1)S(1)}, bf16[8,2,256,128]{3,2,1,0:T(8,128)(2,1)}, u32[]{:S(2)}) copy-start(bf16[8,2,256,128]{3,2,1,0:T(8,128)(2,1)} %get-tuple-element.32.own2_ref) | copy-start | bytes 3145732
  45.9 31.4 %copy-start.3 = (bf16[8,128,128]{2,1,0:T(8,128)(2,1)S(1)}, bf16[8,128,128]{2,1,0:T(8,128)(2,1)}, u32[]{:S(2)}) copy-start(bf16[8,128,128]{2,1,0:T(8,128)(2,1)} %get-tuple-element.28.dq1_ref) | copy-start | bytes 786436
  45.9 31.4 %copy-start.4 = (bf16[8,128,128]{2,1,0:T(8,128)(2,1)S(1)}, bf16[8,128,128]{2,1,0:T(8,128)(2,1)}, u32[]{:S(2)}) copy-start(bf16[8,128,128]{2,1,0:T(8,128)(2,1)} %get-tuple-element.31.dq2_ref) | copy-start | bytes 786436
  46.0 31.3 %collective-permute-start.3 = (bf16[8,2,128,128]{3,2,1,0:T(8,128)(2,1)S(1)}, bf16[8,2,128,128]{3,2,1,0:T(8,128)(2,1)S(1)}, u32[]{:S(2)}, u32[]{:S(2)}) collective-permute-start(bf16[8,2,128,128]{3,2,1,0:T(8,128)(2,1)S(1)} %get-tuple-element.34), channel_id=1, source_target_pairs={{0,2},{2,0},{4,6},{6,4},{8,10},{10,8},{12,14},{14,12},{16,18},{18,... | collective-permute-start | bytes 1572872 | tf_op jit(solution)/shard_map/ppermute | solution.py:373
  49.0 6.6 %collective-permute-start.7 = (bf16[512,128]{1,0:T(8,128)(2,1)S(1)}, bf16[512,128]{1,0:T(8,128)(2,1)S(1)}, u32[]{:S(2)}, u32[]{:S(2)}) collective-permute-start(bf16[512,128]{1,0:T(8,128)(2,1)S(1)} %get-tuple-element.41), channel_id=1, source_target_pairs={{0,4},{2,6},{4,0},{6,2},{8,12},{10,14},{12,8},{14,10},{16,20},{18,... | collective-permute-start | bytes 393224 | tf_op jit(solution)/shard_map/ppermute | solution.py:285
  51.8 3.8 %collective-permute-start.8 = (bf16[512,128]{1,0:T(8,128)(2,1)S(1)}, bf16[512,128]{1,0:T(8,128)(2,1)S(1)}, u32[]{:S(2)}, u32[]{:S(2)}) collective-permute-start(bf16[512,128]{1,0:T(8,128)(2,1)S(1)} %get-tuple-element.40.refs_4_), channel_id=1, source_target_pairs={{0,1},{1,0},{2,3},{3,2},{4,5},{5,4},{6,7},{7,6},{8,9},{9,8},{10,11... | collective-permute-start | bytes 393224 | tf_op jit(solution)/shard_map/ppermute | solution.py:289
  55.6 1.3 %collective-permute-start.6 = (bf16[512,128]{1,0:T(8,128)(2,1)S(1)}, bf16[512,128]{1,0:T(8,128)(2,1)S(1)}, u32[]{:S(2)}, u32[]{:S(2)}) collective-permute-start(bf16[512,128]{1,0:T(8,128)(2,1)S(1)} %collective-permute-done.4.refs_1_), channel_id=1, source_target_pairs={{0,1},{1,0},{2,3},{3,2},{4,5},{5,4},{6,7},{7,6},{8,9},{9,8},{10,11... | collective-permute-start | bytes 393224 | tf_op jit(solution)/shard_map/ppermute | solution.py:289
  55.6 1.5 %collective-permute-start.9 = (bf16[512,128]{1,0:T(8,128)(2,1)S(1)}, bf16[512,128]{1,0:T(8,128)(2,1)S(1)}, u32[]{:S(2)}, u32[]{:S(2)}) collective-permute-start(bf16[512,128]{1,0:T(8,128)(2,1)S(1)} %collective-permute-done.7.refs_5_), channel_id=1, source_target_pairs={{0,1},{1,0},{2,3},{3,2},{4,5},{5,4},{6,7},{7,6},{8,9},{9,8},{10,11... | collective-permute-start | bytes 393224 | tf_op jit(solution)/shard_map/ppermute | solution.py:289
  58.4 10.7 %collective-permute-start.13 = (bf16[128,512]{1,0:T(8,128)(2,1)S(1)}, bf16[128,512]{1,0:T(8,128)(2,1)S(1)}, u32[]{:S(2)}, u32[]{:S(2)}) collective-permute-start(bf16[128,512]{1,0:T(8,128)(2,1)S(1)} %get-tuple-element.43), channel_id=1, source_target_pairs={{0,8},{2,10},{4,12},{6,14},{8,0},{10,2},{12,4},{14,6},{16,24},{18,... | collective-permute-start | bytes 393224 | tf_op jit(solution)/shard_map/ppermute | solution.py:285
  63.1 12.9 %collective-permute-start.14 = (bf16[128,512]{1,0:T(8,128)(2,1)S(1)}, bf16[128,512]{1,0:T(8,128)(2,1)S(1)}, u32[]{:S(2)}, u32[]{:S(2)}) collective-permute-start(bf16[128,512]{1,0:T(8,128)(2,1)S(1)} %get-tuple-element.44), channel_id=1, source_target_pairs={{0,16},{2,18},{4,20},{6,22},{8,24},{10,26},{12,28},{14,30},{16,0},... | collective-permute-start | bytes 393224 | tf_op jit(solution)/shard_map/ppermute | solution.py:285
  65.8 10.3 %collective-permute-start.15 = (bf16[128,512]{1,0:T(8,128)(2,1)S(1)}, bf16[128,512]{1,0:T(8,128)(2,1)S(1)}, u32[]{:S(2)}, u32[]{:S(2)}) collective-permute-start(bf16[128,512]{1,0:T(8,128)(2,1)S(1)} %get-tuple-element.45), channel_id=1, source_target_pairs={{0,24},{2,26},{4,28},{6,30},{8,16},{10,18},{12,20},{14,22},{16,8},... | collective-permute-start | bytes 393224 | tf_op jit(solution)/shard_map/ppermute | solution.py:285
  76.6 4.3 %collective-permute-start.16 = (bf16[64,512]{1,0:T(8,128)(2,1)S(1)}, bf16[64,512]{1,0:T(8,128)(2,1)S(1)}, u32[]{:S(2)}, u32[]{:S(2)}) collective-permute-start(bf16[64,512]{1,0:T(8,128)(2,1)S(1)} %get-tuple-element.47), channel_id=1, source_target_pairs={{0,2},{2,0},{4,6},{6,4},{8,10},{10,8},{12,14},{14,12},{16,18},{18,... | collective-permute-start | bytes 196616 | tf_op jit(solution)/shard_map/ppermute | solution.py:285

commit v3 on v2

--- a/solution.py
+++ b/solution.py
@@ -1,3 +1,5 @@
+import functools
+
 import jax
 import jax.numpy as jnp
 from jax import lax
@@ -26,46 +28,49 @@
     return lax.dot_general(a, b, (dims, ((), ())), preferred_element_type=f32)
 
 
-def half_kernel(meta_ref, bias_ref, thin_hbm, thick_hbm, rim_hbm, keep_ref, send_ref, back_ref, dq_hbm, own_hbm,
-                one_ref, wide_ref, two_ref, score_ref, dp_ref, p_ref, ds_ref, dq_ref, own_ref, in_sem, out_sem):
-    side = meta_ref[0]
+def half_kernel(meta_ref, thin_hbm, thick_hbm, rim_hbm, keep_ref, send_ref, back_ref, dq_hbm, own_hbm,
+                one_ref, wide_ref, two_ref, score_ref, dp_ref, p_ref, ds_ref, dq_ref, own_ref, in_sem, out_sem, *, second):
+    side = 1 - meta_ref[0] if second else meta_ref[0]
+    alone = meta_ref[6 if second else 5]
+    bias = jnp.where(alone == 1, masked_score, 0.0).astype(f32)
     y_digit = meta_ref[1]
     scale = HEAD_DIM ** -0.5
     near_rows = pl.ds(pl.multiple_of(side * HALF, HALF), HALF)
     far_rows = pl.ds(pl.multiple_of((1 - side) * HALF, HALF), HALF)
     pairs = one_ref.shape[0]
+    early = 2
+    middle = pairs // 2
 
     def pair_of(number):
         return 2 * (number // 2) + (y_digit if number % 2 == 0 else 1 - y_digit)
 
-    def fetches(number):
+    def fetches(group):
+        some = pl.ds(0, early) if group == 0 else pl.ds(early, pairs - early)
+        found = [(thin_hbm.at[some, :, side], one_ref.at[some])]
+        for place, source in enumerate((rim_hbm.at[some], thick_hbm.at[some, :, side], thick_hbm.at[some, :, 1 - side])):
+            found.append((source, wide_ref.at[some, :, pl.ds(place * HALF, HALF)]))
+        return [pltpu.make_async_copy(a, b, in_sem.at[group, place]) for place, (a, b) in enumerate(found)]
+
+    def stores(group):
+        some = pl.ds(group * middle, middle)
+        found = [(dq_ref.at[some], dq_hbm.at[some]), (own_ref.at[some], own_hbm.at[some])]
+        return [pltpu.make_async_copy(a, b, out_sem.at[group, place]) for place, (a, b) in enumerate(found)]
+
+    def multiply(number):
         pair = pair_of(number)
-        found = [(thin_hbm.at[pair, :, side], one_ref.at[number])]
-        for place, source in enumerate((rim_hbm.at[pair], thick_hbm.at[pair, :, side], thick_hbm.at[pair, :, 1 - side])):
-            found.append((source, wide_ref.at[number, :, pl.ds(place * HALF, HALF)]))
-        return [pltpu.make_async_copy(a, b, in_sem.at[number, place]) for place, (a, b) in enumerate(found)]
-
-    def stores(number):
-        pair = pair_of(number)
-        found = [(dq_ref.at[number], dq_hbm.at[pair]), (own_ref.at[number], own_hbm.at[pair])]
-        return [pltpu.make_async_copy(a, b, out_sem.at[number, place]) for place, (a, b) in enumerate(found)]
-
-    def multiply(number):
-        for copy in fetches(number):
-            copy.wait()
         slot = number % 3
         first_head = lax.broadcasted_iota(jnp.int32, (HALF, PAIR), 1) < HEAD_DIM
         for which, (factor, out) in enumerate(((scale, score_ref), (1.0, dp_ref))):
-            one = one_ref[number, which].astype(f32) * factor
+            one = one_ref[pair, which].astype(f32) * factor
             two_ref[slot, which, :HALF] = jnp.where(first_head, one, 0.0).astype(bf16)
             two_ref[slot, which, HALF:] = jnp.where(first_head, 0.0, one).astype(bf16)
-            out[number % 2] = contract(wide_ref[number, which], two_ref[slot, which], NT)
+            out[number % 2] = contract(wide_ref[pair, which], two_ref[slot, which], NT)
 
     def weigh(number):
         slot = number % 2
         ahead = lax.broadcasted_iota(jnp.int32, (HALF, 2 * HALF), 0) - lax.broadcasted_iota(jnp.int32, (HALF, 2 * HALF), 1) % HALF
         in_rim = ahead * (1 - 2 * side) >= side
-        s_edge = jnp.where(in_rim, score_ref[slot, :HALF] + bias_ref[0], score_ref[slot, 2 * HALF :])
+        s_edge = jnp.where(in_rim, score_ref[slot, :HALF] + bias, score_ref[slot, 2 * HALF :])
         s_near = score_ref[slot, HALF : 2 * HALF]
         top = jnp.max(jnp.maximum(s_edge, s_near), axis=0, keepdims=True)
         e_edge = jnp.exp(s_edge - top)
@@ -83,46 +88,51 @@
 
     def spread(number):
         slot = number % 2
+        pair = pair_of(number)
         at_ref = send_ref if number % 2 else keep_ref
         start = number // 2 * PAIR
-        at = contract(wide_ref[number, 1], p_ref[slot], TN)
+        at = contract(wide_ref[pair, 1], p_ref[slot], TN)
         at_ref[start : start + HEAD_DIM, :] = at[:HEAD_DIM, :HALF].astype(bf16)
         at_ref[start + HEAD_DIM : start + PAIR, :] = at[HEAD_DIM:, HALF:].astype(bf16)
         for which, left in enumerate((ds_ref, p_ref)):
             part = contract(left[slot], two_ref[number % 3, which], NN)
-            back_ref[pair_of(number), which] = part[:HALF].astype(bf16)
-            own_ref[number, which, near_rows, :] = part[HALF : 2 * HALF].astype(bf16)
-            own_ref[number, which, far_rows, :] = part[2 * HALF :].astype(bf16)
-        dqt = contract(wide_ref[number, 0], ds_ref[slot], TN)
+            back_ref[pair, which] = part[:HALF].astype(bf16)
+            own_ref[pair, which, near_rows, :] = part[HALF : 2 * HALF].astype(bf16)
+            own_ref[pair, which, far_rows, :] = part[2 * HALF :].astype(bf16)
+        dqt = contract(wide_ref[pair, 0], ds_ref[slot], TN)
         dqt = jnp.concatenate([dqt[:HEAD_DIM, :HALF], dqt[HEAD_DIM:, HALF:]], axis=0) * scale
-        dq_ref[number] = dqt.T.astype(bf16)
-        for copy in stores(number):
-            copy.start()
-
-    for number in range(pairs):
-        for copy in fetches(number):
+        dq_ref[pair] = dqt.T.astype(bf16)
+        if (number + 1) % middle == 0:
+            for copy in stores(number // middle):
+                copy.start()
+
+    for group in range(2):
+        for copy in fetches(group):
             copy.start()
     for step in range(pairs + 2):
+        if step in (0, early):
+            for copy in fetches(step // early):
+                copy.wait()
         if step < pairs:
             multiply(step)
         if 0 <= step - 2:
             spread(step - 2)
         if 0 <= step - 1 < pairs:
             weigh(step - 1)
-    for number in range(pairs):
-        for copy in stores(number):
+    for group in range(2):
+        for copy in stores(group):
             copy.wait()
 
 
-def half_attention(meta, bias, thin, thick, rim):
+def half_attention(meta, thin, thick, rim, second):
     pairs, _, blocks, _, _ = thick.shape
     rows = blocks * HALF
     width = pairs * PAIR
     in_hbm = pl.BlockSpec(memory_space=pltpu.HBM)
     held = [pltpu.with_memory_space_constraint(array, pltpu.HBM) for array in (thin, thick)]
     return pl.pallas_call(
-        half_kernel,
-        in_specs=[in_smem, in_smem, in_hbm, in_hbm, pl.BlockSpec(memory_space=pl.ANY)],
+        functools.partial(half_kernel, second=second),
+        in_specs=[in_smem, in_hbm, in_hbm, pl.BlockSpec(memory_space=pl.ANY)],
         out_specs=[in_vmem] * 3 + [in_hbm] * 2,
         out_shape=[
             jax.ShapeDtypeStruct((width // 2, HALF), bf16),
@@ -141,13 +151,13 @@
             pltpu.VMEM((2, 3 * HALF, 2 * HALF), bf16),
             pltpu.VMEM((pairs, HALF, PAIR), bf16),
             pltpu.VMEM((pairs, 2, rows, PAIR), bf16),
-            pltpu.SemaphoreType.DMA((pairs, 4)),
-            pltpu.SemaphoreType.DMA((pairs, 2)),
+            pltpu.SemaphoreType.DMA((2, 4)),
+            pltpu.SemaphoreType.DMA((2, 2)),
         ],
         cost_estimate=pl.CostEstimate(flops=12 * HALF * 3 * HALF * width, bytes_accessed=16 * rows * width,
                                       transcendentals=HALF * 2 * HALF * width // HEAD_DIM),
         compiler_params=pltpu.CompilerParams(vmem_limit_bytes=24 << 20),
-    )(meta, bias, *held, rim)
+    )(meta, *held, rim)
 
 
 def rim_kernel(side_ref, k_ref, v_ref, out_ref):
@@ -257,9 +267,9 @@
     )(meta, own, *pieces)
 
 
-def join_kernel(meta_ref, dq1_ref, own1_ref, dq2_ref, own2_ref, long_ref, near_ref, dq_out, dk_out, dv_out):
+def join_kernel(meta_ref, dq1_ref, own1_ref, dq2_ref, own2_ref, rim1_ref, rim2_ref, dq_out, dk_out, dv_out):
     side = meta_ref[0]
-    for row, rim, dq_ref in ((side, long_ref, dq1_ref), (1 - side, near_ref, dq2_ref)):
+    for row, rim, dq_ref in ((side, rim1_ref, dq1_ref), (1 - side, rim2_ref, dq2_ref)):
         rows = pl.ds(pl.multiple_of(row * HALF, HALF), HALF)
         for pair in range(dq1_ref.shape[0]):
             cols = slice(pair * PAIR, (pair + 1) * PAIR)
@@ -269,7 +279,7 @@
                 out[rows, cols] = (total + rim[pair, which].astype(f32)).astype(bf16)
 
 
-def joined(meta, own1, own2, from_long, from_near, shape):
+def joined(meta, own1, own2, rim1, rim2, shape):
     out = jax.ShapeDtypeStruct(shape, bf16)
     return pl.pallas_call(
         join_kernel,
@@ -278,7 +288,7 @@
         out_shape=[out] * 3,
         compiler_params=pltpu.CompilerParams(vmem_limit_bytes=12 << 20),
         name="joined",
-    )(meta, *own1, *own2, from_long, from_near)
+    )(meta, *own1, *own2, rim1, rim2)
 
 
 def swapped(value, stride, count):
@@ -337,53 +347,52 @@
     mine = lax.axis_index("dp")
     odd = place % 2
     y_digit = (place // 2) % 2
-    sides = (odd, 1 - odd)
+    sides = (1 - odd, odd)
     long_pairs = [(i, i + 1 if i % 2 else i - 1) for i in range(1, count - 1)]
     near_pairs = [(i, i ^ 1) for i in range(count)]
     block = width // count
     own_width = width // dp_count
     stages = upper_stages(count)
     direct = 2 * block == PAIR and len(stages) == 1 and dp_count == 2
-    metas = [jnp.stack([side, y_digit if direct else 0 * y_digit, mine, place // 4 % stages[0][1], odd]).astype(jnp.int32) for side in sides]
-    alone = [jnp.where(side == 0, place == 0, place == count - 1) for side in sides]
-    bias = [jnp.where(one, masked_score, 0.0).astype(f32).reshape(1) for one in alone]
-
-    rim1 = packed_rim(metas[0][:1], k, v)
-    first_rim = lax.ppermute(rim1, "seq", long_pairs)
-    thin, thick, rim2 = prepared(metas[0], q, k, v, g, out_weight)
-    second_rim = lax.ppermute(rim2, "seq", near_pairs)
-
+    alone = (place == 0) | (place == count - 1)
+    meta = jnp.stack([1 - odd, y_digit if direct else 0 * y_digit, mine, place // 4 % stages[0][1], odd, 0 * odd, alone]).astype(jnp.int32)
+
+    rim1 = packed_rim(meta[:1], k, v)
+    first_rim = lax.ppermute(rim1, "seq", near_pairs)
     if direct:
         g_y = swapped(g, 2, count)
+    thin, thick, rim2 = prepared(meta, q, k, v, g, out_weight)
+    second_rim = lax.ppermute(rim2, "seq", long_pairs)
+    if direct:
         g_dp = turned(g, dp_count)[0]
         g_y_dp = turned(g_y, dp_count)[0]
         gs = [g, g_dp, g_y, g_y_dp]
 
-    keep1, send1, back1, *own1 = half_attention(metas[0], bias[0], thin, thick, first_rim)
-    from_long = lax.ppermute(back1, "seq", long_pairs)
+    keep1, send1, back1, *own1 = half_attention(meta, thin, thick, first_rim, False)
+    from_near = lax.ppermute(back1, "seq", near_pairs)
     if direct:
         at_y1 = swapped(send1, 2, count)
         at_dp1 = turned(keep1, dp_count)[0]
         at_y_dp1 = turned(at_y1, dp_count)[0]
-    keep2, send2, back2, *own2 = half_attention(metas[1], bias[1], thin, thick, second_rim)
+    keep2, send2, back2, *own2 = half_attention(meta, thin, thick, second_rim, True)
     if direct:
         at_y2 = swapped(send2, 2, count)
         at_dp2 = turned(keep2, dp_count)[0]
         at_y_dp2 = turned(at_y2, dp_count)[0]
-    from_near = lax.ppermute(back2, "seq", near_pairs)
+    from_long = lax.ppermute(back2, "seq", long_pairs)
 
     frames = rows * count * dp_count
     if direct:
         ats = [keep1, at_y1, at_dp1, at_y_dp1, keep2, at_y2, at_dp2, at_y_dp2]
-        terms = products(metas[0], ats, gs, count // 4, own_width)
+        terms = products(meta, ats, gs, count // 4, own_width)
         pieces = []
         for step in range(1, count // 4):
             pieces.append(swapped(terms[step], 4 * step, count))
-        kept, sent = summed(metas[0], terms[0], pieces)
+        kept, sent = summed(meta, terms[0], pieces)
         wo_grad = kept + swapped(sent, 1, count).astype(f32)
     else:
         wo_grad = general_sum((keep1, send1), (keep2, send2), g, sides, place, mine, y_digit, count, dp_count)
-    dq, dk, dv = joined(metas[0], own1, own2, from_long, from_near, q.shape)
+    dq, dk, dv = joined(meta, own1, own2, from_near, from_long, q.shape)
     return dq[None], dk[None], dv[None], wo_grad * frames ** -0.5
 
 

time: 81.9 us -> 86.5 us (1.056)
  waiting for transfers between devices: 28.8 us -> 42.6 us
  Pallas kernels: 25.6 us -> 21.3 us
  starting transfers between devices: 24.2 us -> 20.2 us
    ppermute x4, waiting for transfers between devices: 0.01 us -> 13.7 us  [the longest x1 13.7 us: on_device(): first_rim = lax.ppermute(rim1, 'seq', near_pairs)]
    pallas_call x2, Pallas kernels: 15.1 us -> 10.9 us  [half_attention(): pl.pallas_call(functools.partial(half_kernel, second=second), in_specs=[i...]
    ppermute x7, starting transfers between devices: 16.2 us -> 14.1 us  [swapped(): return lax.ppermute(value, 'seq', [(i, i ^ stride) for i in range(count)])]
    ppermute x4, starting transfers between devices: 7.3 us -> 5.44 us  [the longest x1 2.44 us: on_device(): from_near = lax.ppermute(back1, 'seq', near_pairs)]
  transfers between devices with their start and end apart: 17 -> 17, of which waited for: 7 -> 8; matrix products, arithmetic and copies ran while one was open for 1% -> 1% of each run, Pallas kernels for 31% -> 25%
where the time goes in v3:
time: 86.5 us; the launch traced here: 86.3 us
  waiting for transfers between devices  42.6 us (49%)
  Pallas kernels  21.3 us (25%)
  starting transfers between devices  20.2 us (23%)
    ppermute x7, waiting for transfers between devices, swapped(): return lax.ppermute(value, 'seq', [(i, i ^ stride) for i in range(count)])  27.9 us
    ppermute x7, starting transfers between devices, swapped(): return lax.ppermute(value, 'seq', [(i, i ^ stride) for i in range(count)])  14.1 us
    ppermute x1, waiting for transfers between devices, on_device(): first_rim = lax.ppermute(rim1, 'seq', near_pairs)  13.7 us
    pallas_call x2, Pallas kernels, half_attention(): pl.pallas_call(functools.partial(half_kernel, second=second), in_specs=[i...  10.9 us
    pallas_call x1, Pallas kernels, prepared(): pl.pallas_call(prepare_kernel, in_specs=[in_smem] + [in_vmem] * 5, out_sp...  4.62 us
    ppermute x1, starting transfers between devices, on_device(): from_near = lax.ppermute(back1, 'seq', near_pairs)  2.44 us
    pallas_call x1, Pallas kernels, joined(): pl.pallas_call(join_kernel, in_specs=[in_smem] + [in_vmem] * 6, out_specs...  2.04 us
    pallas_call x1, Pallas kernels, packed_rim(): pl.pallas_call(rim_kernel, grid_spec=pltpu.PrefetchScalarGridSpec(num_sca...  1.92 us
  transfers between devices with their start and end apart: 17, of which 8 were waited for; matrix products, arithmetic and copies ran while one was open for 1% of the time, Pallas kernels for 25%

profile of v3, /device:TPU:0, one launch (start us, length us, event | category | flops | bytes accessed | tf_op | source)
XLA Modules:
  0.0 86.3 jit_solution(14282845252878372211)
XLA Ops:
  0.6 3.1 %collective-permute-start.11 = (bf16[256,1024]{1,0:T(8,128)(2,1)}, bf16[256,1024]{1,0:T(8,128)(2,1)S(1)}, u32[]{:S(2)}, u32[]{:S(2)}) collective-permute-start(bf16[256,1024]{1,0:T(8,128)(2,1)} %bitcast.13), channel_id=1, source_target_pairs={{0,4},{2,6},{4,0},{6,2},{8,12},{10,14},{12,8},{14,10},{16,20},{18,... | collective-permute-start | bytes 1572872 | tf_op jit(solution)/shard_map/ppermute | solution.py:295
  3.7 1.9 %shard_map.84 = bf16[8,2,128,128]{3,2,1,0:T(8,128)(2,1)} custom-call(s32[1]{0:T(128)} %bitcast.side_ref, bf16[256,1024]{1,0:T(8,128)(2,1)} %bitcast.17, bf16[256,1024]{1,0:T(8,128)(2,1)} %bitcast.19), custom_call_target="tpu_custom_call" | custom-call | tf_op jit(solution)/shard_map/pallas_call | solution.py:174
  5.6 1.5 %collective-permute-start = (bf16[8,2,128,128]{3,2,1,0:T(8,128)(2,1)}, bf16[8,2,128,128]{3,2,1,0:T(8,128)(2,1)S(1)}, u32[]{:S(2)}, u32[]{:S(2)}) collective-permute-start(bf16[8,2,128,128]{3,2,1,0:T(8,128)(2,1)} %shard_map.84), channel_id=1, source_target_pairs={{0,2},{2,0},{4,6},{6,4},{8,10},{10,8},{12,14},{14,12},{16,18},{18,... | collective-permute-start | bytes 1572872 | tf_op jit(solution)/shard_map/ppermute | solution.py:361
  7.1 0.6 stack.31.meta_ref
  7.7 0.0 copy-start
  7.7 0.0 copy-start.5
  7.7 4.6 %prepared.1 = (bf16[8,2,2,128,128]{4,3,2,1,0:T(8,128)(2,1)}, bf16[8,2,2,128,128]{4,3,2,1,0:T(8,128)(2,1)}, bf16[8,2,128,128]{3,2,1,0:T(8,128)(2,1)}) custom-call(s32[7]{0:T(128)} %stack.31.meta_ref, bf16[256,1024]{1,0:T(8,128)(2,1)} %bitcast.21, bf16[256,1024]{1,0:T(8,128)(2,1)} %bitcast.18, bf16[256,1024]{1,0:T(8,128)(2,1)} %bitcast.20, ...), custom_call_target="tpu_custom_call" | custom-call | flops 536870912 | bytes 5767168 | tf_op jit(solution)/shard_map/prepared/pallas_call | solution.py:208
  12.3 0.7 collective-permute-start.1
  13.0 0.0 copy-done
  13.0 0.1 collective-permute-start.10
  13.1 2.7 %collective-permute-done.11.refs_10_ = bf16[256,1024]{1,0:T(8,128)(2,1)S(1)} collective-permute-done((bf16[256,1024]{1,0:T(8,128)(2,1)}, bf16[256,1024]{1,0:T(8,128)(2,1)S(1)}, u32[]{:S(2)}, u32[]{:S(2)}) %collective-permute-start.11) | collective-permute-done | bytes 524320 | tf_op jit(solution)/shard_map/ppermute | solution.py:295
  15.8 0.0 collective-permute-start.12
  15.8 13.7 %collective-permute-done.rim_hbm = bf16[8,2,128,128]{3,2,1,0:T(8,128)(2,1)S(1)} collective-permute-done((bf16[8,2,128,128]{3,2,1,0:T(8,128)(2,1)}, bf16[8,2,128,128]{3,2,1,0:T(8,128)(2,1)S(1)}, u32[]{:S(2)}, u32[]{:S(2)}) %collective-permute-start) | collective-permute-done | bytes 524320 | tf_op jit(solution)/shard_map/ppermute | solution.py:361
  29.6 0.0 copy-done.5
  29.6 5.5 %shard_map.85 = (bf16[512,128]{1,0:T(8,128)(2,1)S(1)}, bf16[512,128]{1,0:T(8,128)(2,1)S(1)}, bf16[8,2,128,128]{3,2,1,0:T(8,128)(2,1)S(1)}, bf16[8,128,128]{2,1,0:T(8,128)(2,1)}, bf16[8,2,256,128]{3,2,1,0:T(8,128)(2,1)}) custom-call(s32[7]{0:T(128)S(1)} %copy-done.5, bf16[8,2,2,128,128]{4,3,2,1,0:T(8,128)(2,1)} %get-tuple-element.26.thin_hbm, ...), custom_call_target="tpu_custom_call" | custom-call | flops 603979776 | bytes 4194304 | tf_op jit(solution)/shard_map/pallas_call | solution.py:133
  35.0 0.1 collective-permute-start.4
  35.1 0.1 collective-permute-start.5
  35.2 0.0 collective-permute-done.1.rim_hbm
  35.2 2.4 %collective-permute-start.2 = (bf16[8,2,128,128]{3,2,1,0:T(8,128)(2,1)S(1)}, bf16[8,2,128,128]{3,2,1,0:T(8,128)(2,1)S(1)}, u32[]{:S(2)}, u32[]{:S(2)}) collective-permute-start(bf16[8,2,128,128]{3,2,1,0:T(8,128)(2,1)S(1)} %get-tuple-element.33), channel_id=1, source_target_pairs={{0,2},{2,0},{4,6},{6,4},{8,10},{10,8},{12,14},{14,12},{16,18},{18,... | collective-permute-start | bytes 1572872 | tf_op jit(solution)/shard_map/ppermute | solution.py:372
  37.6 5.4 %shard_map.86 = (bf16[512,128]{1,0:T(8,128)(2,1)S(1)}, bf16[512,128]{1,0:T(8,128)(2,1)S(1)}, bf16[8,2,128,128]{3,2,1,0:T(8,128)(2,1)S(1)}, bf16[8,128,128]{2,1,0:T(8,128)(2,1)}, bf16[8,2,256,128]{3,2,1,0:T(8,128)(2,1)}) custom-call(s32[7]{0:T(128)S(1)} %copy-done.5, bf16[8,2,2,128,128]{4,3,2,1,0:T(8,128)(2,1)} %get-tuple-element.26.thin_hbm, ...), custom_call_target="tpu_custom_call" | custom-call | flops 603979776 | bytes 4194304 | tf_op jit(solution)/shard_map/pallas_call | solution.py:133
  43.0 0.0 copy-start.1
  43.1 0.0 copy-start.2
  43.1 0.0 copy-start.3
  43.1 0.0 copy-start.4
  43.1 0.0 collective-permute-done.10.refs_9_
  43.1 0.8 collective-permute-start.3
  43.9 0.0 collective-permute-done.4.refs_1_
  43.9 3.2 %collective-permute-start.7 = (bf16[512,128]{1,0:T(8,128)(2,1)S(1)}, bf16[512,128]{1,0:T(8,128)(2,1)S(1)}, u32[]{:S(2)}, u32[]{:S(2)}) collective-permute-start(bf16[512,128]{1,0:T(8,128)(2,1)S(1)} %get-tuple-element.41), channel_id=1, source_target_pairs={{0,4},{2,6},{4,0},{6,2},{8,12},{10,14},{12,8},{14,10},{16,20},{18,... | collective-permute-start | bytes 393224 | tf_op jit(solution)/shard_map/ppermute | solution.py:295
  47.1 0.0 collective-permute-done.5.refs_2_
  47.1 0.0 collective-permute-start.8
  47.1 14.4 %collective-permute-done.7.refs_5_ = bf16[512,128]{1,0:T(8,128)(2,1)S(1)} collective-permute-done((bf16[512,128]{1,0:T(8,128)(2,1)S(1)}, bf16[512,128]{1,0:T(8,128)(2,1)S(1)}, u32[]{:S(2)}, u32[]{:S(2)}) %collective-permute-start.7) | collective-permute-done | bytes 131104 | tf_op jit(solution)/shard_map/ppermute | solution.py:295
  61.5 0.0 collective-permute-start.6
  61.5 0.0 collective-permute-done.8.refs_6_
  61.5 0.5 collective-permute-start.9
  62.0 0.8 collective-permute-done.6.refs_3_
  62.8 0.2 collective-permute-done.9.refs_7_
  63.0 0.0 collective-permute-done.12.refs_11_
  63.0 1.3 %product.1 = (f32[128,512]{1,0:T(8,128)S(1)}, bf16[128,512]{1,0:T(8,128)(2,1)S(1)}, bf16[128,512]{1,0:T(8,128)(2,1)S(1)}, bf16[128,512]{1,0:T(8,128)(2,1)S(1)}) custom-call(s32[7]{0:T(128)S(1)} %copy-done.5, bf16[512,128]{1,0:T(8,128)(2,1)S(1)} %get-tuple-element.38.refs_0_, bf16[512,128]{1,0:T(8,128)(2,1)S(1)} %collective-permute-done.4.refs_1_, ...), custom_call_target="tpu_custom_call" | custom-call | tf_op jit(solution)/shard_map/product/pallas_call | solution.py:237
  64.3 3.4 %collective-permute-start.13 = (bf16[128,512]{1,0:T(8,128)(2,1)S(1)}, bf16[128,512]{1,0:T(8,128)(2,1)S(1)}, u32[]{:S(2)}, u32[]{:S(2)}) collective-permute-start(bf16[128,512]{1,0:T(8,128)(2,1)S(1)} %get-tuple-element.43), channel_id=1, source_target_pairs={{0,8},{2,10},{4,12},{6,14},{8,0},{10,2},{12,4},{14,6},{16,24},{18,... | collective-permute-start | bytes 393224 | tf_op jit(solution)/shard_map/ppermute | solution.py:295
  67.7 2.3 %collective-permute-start.14 = (bf16[128,512]{1,0:T(8,128)(2,1)S(1)}, bf16[128,512]{1,0:T(8,128)(2,1)S(1)}, u32[]{:S(2)}, u32[]{:S(2)}) collective-permute-start(bf16[128,512]{1,0:T(8,128)(2,1)S(1)} %get-tuple-element.44), channel_id=1, source_target_pairs={{0,16},{2,18},{4,20},{6,22},{8,24},{10,26},{12,28},{14,30},{16,0},... | collective-permute-start | bytes 393224 | tf_op jit(solution)/shard_map/ppermute | solution.py:295
  70.1 0.1 collective-permute-start.15
  70.2 3.5 %collective-permute-done.13.refs_0_ = bf16[128,512]{1,0:T(8,128)(2,1)S(1)} collective-permute-done((bf16[128,512]{1,0:T(8,128)(2,1)S(1)}, bf16[128,512]{1,0:T(8,128)(2,1)S(1)}, u32[]{:S(2)}, u32[]{:S(2)}) %collective-permute-start.13) | collective-permute-done | bytes 131104 | tf_op jit(solution)/shard_map/ppermute | solution.py:295
  73.8 6.9 %collective-permute-done.14.refs_1_ = bf16[128,512]{1,0:T(8,128)(2,1)S(1)} collective-permute-done((bf16[128,512]{1,0:T(8,128)(2,1)S(1)}, bf16[128,512]{1,0:T(8,128)(2,1)S(1)}, u32[]{:S(2)}, u32[]{:S(2)}) %collective-permute-start.14) | collective-permute-done | bytes 131104 | tf_op jit(solution)/shard_map/ppermute | solution.py:295
  80.7 0.0 collective-permute-done.15.refs_2_
  80.7 0.6 summed.1
  81.3 1.9 %collective-permute-start.16 = (bf16[64,512]{1,0:T(8,128)(2,1)S(1)}, bf16[64,512]{1,0:T(8,128)(2,1)S(1)}, u32[]{:S(2)}, u32[]{:S(2)}) collective-permute-start(bf16[64,512]{1,0:T(8,128)(2,1)S(1)} %get-tuple-element.47), channel_id=1, source_target_pairs={{0,2},{2,0},{4,6},{6,4},{8,10},{10,8},{12,14},{14,12},{16,18},{18,... | collective-permute-start | bytes 196616 | tf_op jit(solution)/shard_map/ppermute | solution.py:295
  83.2 0.0 collective-permute-done.2.rim1_ref
  83.2 0.0 collective-permute-done.3.rim2_ref
  83.2 0.0 copy-done.1
  83.2 0.0 copy-done.2
  83.2 0.0 copy-done.3
  83.2 0.0 copy-done.4
  83.3 2.0 %joined.1 = (bf16[256,1024]{1,0:T(8,128)(2,1)}, bf16[256,1024]{1,0:T(8,128)(2,1)}, bf16[256,1024]{1,0:T(8,128)(2,1)}) custom-call(s32[7]{0:T(128)S(1)} %copy-done.5, bf16[8,128,128]{2,1,0:T(8,128)(2,1)S(1)} %copy-done.3, bf16[8,2,256,128]{3,2,1,0:T(8,128)(2,1)S(1)} %copy-done.1, bf16[8,128,128]{2,1,0:T(8,128)(2,1)S(1)} %copy-done.4, ...), custom_call_target="tpu_custom_call" | custom-call | tf_op jit(solution)/shard_map/joined/pallas_call | solution.py:284
  85.3 0.3 collective-permute-done.16
  85.6 0.7 add_multiply_fusion
Async XLA Ops:
  0.6 15.2 %collective-permute-start.11 = (bf16[256,1024]{1,0:T(8,128)(2,1)}, bf16[256,1024]{1,0:T(8,128)(2,1)S(1)}, u32[]{:S(2)}, u32[]{:S(2)}) collective-permute-start(bf16[256,1024]{1,0:T(8,128)(2,1)} %bitcast.13), channel_id=1, source_target_pairs={{0,4},{2,6},{4,0},{6,2},{8,12},{10,14},{12,8},{14,10},{16,20},{18,... | collective-permute-start | bytes 1572872 | tf_op jit(solution)/shard_map/ppermute | solution.py:295
  5.6 23.9 %collective-permute-start = (bf16[8,2,128,128]{3,2,1,0:T(8,128)(2,1)}, bf16[8,2,128,128]{3,2,1,0:T(8,128)(2,1)S(1)}, u32[]{:S(2)}, u32[]{:S(2)}) collective-permute-start(bf16[8,2,128,128]{3,2,1,0:T(8,128)(2,1)} %shard_map.84), channel_id=1, source_target_pairs={{0,2},{2,0},{4,6},{6,4},{8,10},{10,8},{12,14},{14,12},{16,18},{18,... | collective-permute-start | bytes 1572872 | tf_op jit(solution)/shard_map/ppermute | solution.py:361
  7.7 5.3 %copy-start = (bf16[1,256,1024]{2,1,0:T(8,128)(2,1)S(1)}, bf16[1,256,1024]{2,1,0:T(8,128)(2,1)}, u32[]{:S(2)}) copy-start(bf16[1,256,1024]{2,1,0:T(8,128)(2,1)} %param.8) | copy-start | bytes 1572868
  7.7 21.8 %copy-start.5 = (s32[7]{0:T(128)S(1)}, s32[7]{0:T(128)}, u32[]{:S(2)}) copy-start(s32[7]{0:T(128)} %stack.31.meta_ref) | copy-start | bytes 88
  12.3 22.8 %collective-permute-start.1 = (bf16[8,2,128,128]{3,2,1,0:T(8,128)(2,1)}, bf16[8,2,128,128]{3,2,1,0:T(8,128)(2,1)S(1)}, u32[]{:S(2)}, u32[]{:S(2)}) collective-permute-start(bf16[8,2,128,128]{3,2,1,0:T(8,128)(2,1)} %get-tuple-element.30), channel_id=1, source_target_pairs={{2,4},{4,2},{6,8},{8,6},{10,12},{12,10},{14,16},{16,14},{18,20},{2... | collective-permute-start | bytes 1572872 | tf_op jit(solution)/shard_map/ppermute | solution.py:365
  13.0 30.1 %collective-permute-start.10 = (bf16[256,1024]{1,0:T(8,128)(2,1)S(1)}, bf16[256,1024]{1,0:T(8,128)(2,1)S(1)}, u32[]{:S(2)}, u32[]{:S(2)}) collective-permute-start(bf16[256,1024]{1,0:T(8,128)(2,1)S(1)} %bitcast.15), channel_id=1, source_target_pairs={{0,1},{1,0},{2,3},{3,2},{4,5},{5,4},{6,7},{7,6},{8,9},{9,8},{10,11... | collective-permute-start | bytes 1572872 | tf_op jit(solution)/shard_map/ppermute | solution.py:299
  15.8 47.2 %collective-permute-start.12 = (bf16[256,1024]{1,0:T(8,128)(2,1)S(1)}, bf16[256,1024]{1,0:T(8,128)(2,1)S(1)}, u32[]{:S(2)}, u32[]{:S(2)}) collective-permute-start(bf16[256,1024]{1,0:T(8,128)(2,1)S(1)} %collective-permute-done.11.refs_10_), channel_id=1, source_target_pairs={{0,1},{1,0},{2,3},{3,2},{4,5},{5,4},{6,7},{7,6},{8,9},{9,8},{10,11... | collective-permute-start | bytes 1572872 | tf_op jit(solution)/shard_map/ppermute | solution.py:299
  35.0 8.9 %collective-permute-start.4 = (bf16[512,128]{1,0:T(8,128)(2,1)S(1)}, bf16[512,128]{1,0:T(8,128)(2,1)S(1)}, u32[]{:S(2)}, u32[]{:S(2)}) collective-permute-start(bf16[512,128]{1,0:T(8,128)(2,1)S(1)} %get-tuple-element.39), channel_id=1, source_target_pairs={{0,4},{2,6},{4,0},{6,2},{8,12},{10,14},{12,8},{14,10},{16,20},{18,... | collective-permute-start | bytes 393224 | tf_op jit(solution)/shard_map/ppermute | solution.py:295
  35.1 12.0 %collective-permute-start.5 = (bf16[512,128]{1,0:T(8,128)(2,1)S(1)}, bf16[512,128]{1,0:T(8,128)(2,1)S(1)}, u32[]{:S(2)}, u32[]{:S(2)}) collective-permute-start(bf16[512,128]{1,0:T(8,128)(2,1)S(1)} %get-tuple-element.38.refs_0_), channel_id=1, source_target_pairs={{0,1},{1,0},{2,3},{3,2},{4,5},{5,4},{6,7},{7,6},{8,9},{9,8},{10,11... | collective-permute-start | bytes 393224 | tf_op jit(solution)/shard_map/ppermute | solution.py:299
  35.2 48.0 %collective-permute-start.2 = (bf16[8,2,128,128]{3,2,1,0:T(8,128)(2,1)S(1)}, bf16[8,2,128,128]{3,2,1,0:T(8,128)(2,1)S(1)}, u32[]{:S(2)}, u32[]{:S(2)}) collective-permute-start(bf16[8,2,128,128]{3,2,1,0:T(8,128)(2,1)S(1)} %get-tuple-element.33), channel_id=1, source_target_pairs={{0,2},{2,0},{4,6},{6,4},{8,10},{10,8},{12,14},{14,12},{16,18},{18,... | collective-permute-start | bytes 1572872 | tf_op jit(solution)/shard_map/ppermute | solution.py:372
  43.0 40.2 %copy-start.1 = (bf16[8,2,256,128]{3,2,1,0:T(8,128)(2,1)S(1)}, bf16[8,2,256,128]{3,2,1,0:T(8,128)(2,1)}, u32[]{:S(2)}) copy-start(bf16[8,2,256,128]{3,2,1,0:T(8,128)(2,1)} %get-tuple-element.29.own1_ref) | copy-start | bytes 3145732
  43.1 40.2 %copy-start.2 = (bf16[8,2,256,128]{3,2,1,0:T(8,128)(2,1)S(1)}, bf16[8,2,256,128]{3,2,1,0:T(8,128)(2,1)}, u32[]{:S(2)}) copy-start(bf16[8,2,256,128]{3,2,1,0:T(8,128)(2,1)} %get-tuple-element.32.own2_ref) | copy-start | bytes 3145732
  43.1 40.2 %copy-start.3 = (bf16[8,128,128]{2,1,0:T(8,128)(2,1)S(1)}, bf16[8,128,128]{2,1,0:T(8,128)(2,1)}, u32[]{:S(2)}) copy-start(bf16[8,128,128]{2,1,0:T(8,128)(2,1)} %get-tuple-element.28.dq1_ref) | copy-start | bytes 786436
  43.1 40.2 %copy-start.4 = (bf16[8,128,128]{2,1,0:T(8,128)(2,1)S(1)}, bf16[8,128,128]{2,1,0:T(8,128)(2,1)}, u32[]{:S(2)}) copy-start(bf16[8,128,128]{2,1,0:T(8,128)(2,1)} %get-tuple-element.31.dq2_ref) | copy-start | bytes 786436
  43.1 40.1 %collective-permute-start.3 = (bf16[8,2,128,128]{3,2,1,0:T(8,128)(2,1)S(1)}, bf16[8,2,128,128]{3,2,1,0:T(8,128)(2,1)S(1)}, u32[]{:S(2)}, u32[]{:S(2)}) collective-permute-start(bf16[8,2,128,128]{3,2,1,0:T(8,128)(2,1)S(1)} %get-tuple-element.34), channel_id=1, source_target_pairs={{2,4},{4,2},{6,8},{8,6},{10,12},{12,10},{14,16},{16,14},{18,20},{2... | collective-permute-start | bytes 1572872 | tf_op jit(solution)/shard_map/ppermute | solution.py:382
  43.9 17.5 %collective-permute-start.7 = (bf16[512,128]{1,0:T(8,128)(2,1)S(1)}, bf16[512,128]{1,0:T(8,128)(2,1)S(1)}, u32[]{:S(2)}, u32[]{:S(2)}) collective-permute-start(bf16[512,128]{1,0:T(8,128)(2,1)S(1)} %get-tuple-element.41), channel_id=1, source_target_pairs={{0,4},{2,6},{4,0},{6,2},{8,12},{10,14},{12,8},{14,10},{16,20},{18,... | collective-permute-start | bytes 393224 | tf_op jit(solution)/shard_map/ppermute | solution.py:295
  47.1 14.4 %collective-permute-start.8 = (bf16[512,128]{1,0:T(8,128)(2,1)S(1)}, bf16[512,128]{1,0:T(8,128)(2,1)S(1)}, u32[]{:S(2)}, u32[]{:S(2)}) collective-permute-start(bf16[512,128]{1,0:T(8,128)(2,1)S(1)} %get-tuple-element.40.refs_4_), channel_id=1, source_target_pairs={{0,1},{1,0},{2,3},{3,2},{4,5},{5,4},{6,7},{7,6},{8,9},{9,8},{10,11... | collective-permute-start | bytes 393224 | tf_op jit(solution)/shard_map/ppermute | solution.py:299
  61.5 1.3 %collective-permute-start.6 = (bf16[512,128]{1,0:T(8,128)(2,1)S(1)}, bf16[512,128]{1,0:T(8,128)(2,1)S(1)}, u32[]{:S(2)}, u32[]{:S(2)}) collective-permute-start(bf16[512,128]{1,0:T(8,128)(2,1)S(1)} %collective-permute-done.4.refs_1_), channel_id=1, source_target_pairs={{0,1},{1,0},{2,3},{3,2},{4,5},{5,4},{6,7},{7,6},{8,9},{9,8},{10,11... | collective-permute-start | bytes 393224 | tf_op jit(solution)/shard_map/ppermute | solution.py:299
  61.5 1.5 %collective-permute-start.9 = (bf16[512,128]{1,0:T(8,128)(2,1)S(1)}, bf16[512,128]{1,0:T(8,128)(2,1)S(1)}, u32[]{:S(2)}, u32[]{:S(2)}) collective-permute-start(bf16[512,128]{1,0:T(8,128)(2,1)S(1)} %collective-permute-done.7.refs_5_), channel_id=1, source_target_pairs={{0,1},{1,0},{2,3},{3,2},{4,5},{5,4},{6,7},{7,6},{8,9},{9,8},{10,11... | collective-permute-start | bytes 393224 | tf_op jit(solution)/shard_map/ppermute | solution.py:299
  64.3 9.5 %collective-permute-start.13 = (bf16[128,512]{1,0:T(8,128)(2,1)S(1)}, bf16[128,512]{1,0:T(8,128)(2,1)S(1)}, u32[]{:S(2)}, u32[]{:S(2)}) collective-permute-start(bf16[128,512]{1,0:T(8,128)(2,1)S(1)} %get-tuple-element.43), channel_id=1, source_target_pairs={{0,8},{2,10},{4,12},{6,14},{8,0},{10,2},{12,4},{14,6},{16,24},{18,... | collective-permute-start | bytes 393224 | tf_op jit(solution)/shard_map/ppermute | solution.py:295
  67.7 12.9 %collective-permute-start.14 = (bf16[128,512]{1,0:T(8,128)(2,1)S(1)}, bf16[128,512]{1,0:T(8,128)(2,1)S(1)}, u32[]{:S(2)}, u32[]{:S(2)}) collective-permute-start(bf16[128,512]{1,0:T(8,128)(2,1)S(1)} %get-tuple-element.44), channel_id=1, source_target_pairs={{0,16},{2,18},{4,20},{6,22},{8,24},{10,26},{12,28},{14,30},{16,0},... | collective-permute-start | bytes 393224 | tf_op jit(solution)/shard_map/ppermute | solution.py:295
  70.1 10.6 %collective-permute-start.15 = (bf16[128,512]{1,0:T(8,128)(2,1)S(1)}, bf16[128,512]{1,0:T(8,128)(2,1)S(1)}, u32[]{:S(2)}, u32[]{:S(2)}) collective-permute-start(bf16[128,512]{1,0:T(8,128)(2,1)S(1)} %get-tuple-element.45), channel_id=1, source_target_pairs={{0,24},{2,26},{4,28},{6,30},{8,16},{10,18},{12,20},{14,22},{16,8},... | collective-permute-start | bytes 393224 | tf_op jit(solution)/shard_map/ppermute | solution.py:295
  81.3 4.3 %collective-permute-start.16 = (bf16[64,512]{1,0:T(8,128)(2,1)S(1)}, bf16[64,512]{1,0:T(8,128)(2,1)S(1)}, u32[]{:S(2)}, u32[]{:S(2)}) collective-permute-start(bf16[64,512]{1,0:T(8,128)(2,1)S(1)} %get-tuple-element.47), channel_id=1, source_target_pairs={{0,2},{2,0},{4,6},{6,4},{8,10},{10,8},{12,14},{14,12},{16,18},{18,... | collective-permute-start | bytes 196616 | tf_op jit(solution)/shard_map/ppermute | solution.py:295

commit v4 on v3

--- a/solution.py
+++ b/solution.py
@@ -347,7 +347,7 @@
     mine = lax.axis_index("dp")
     odd = place % 2
     y_digit = (place // 2) % 2
-    sides = (1 - odd, odd)
+    sides = (odd, 1 - odd)
     long_pairs = [(i, i + 1 if i % 2 else i - 1) for i in range(1, count - 1)]
     near_pairs = [(i, i ^ 1) for i in range(count)]
     block = width // count
@@ -355,21 +355,21 @@
     stages = upper_stages(count)
     direct = 2 * block == PAIR and len(stages) == 1 and dp_count == 2
     alone = (place == 0) | (place == count - 1)
-    meta = jnp.stack([1 - odd, y_digit if direct else 0 * y_digit, mine, place // 4 % stages[0][1], odd, 0 * odd, alone]).astype(jnp.int32)
+    meta = jnp.stack([odd, y_digit if direct else 0 * y_digit, mine, place // 4 % stages[0][1], odd, alone, 0 * odd]).astype(jnp.int32)
 
     rim1 = packed_rim(meta[:1], k, v)
-    first_rim = lax.ppermute(rim1, "seq", near_pairs)
+    first_rim = lax.ppermute(rim1, "seq", long_pairs)
     if direct:
         g_y = swapped(g, 2, count)
     thin, thick, rim2 = prepared(meta, q, k, v, g, out_weight)
-    second_rim = lax.ppermute(rim2, "seq", long_pairs)
+    second_rim = lax.ppermute(rim2, "seq", near_pairs)
     if direct:
         g_dp = turned(g, dp_count)[0]
         g_y_dp = turned(g_y, dp_count)[0]
         gs = [g, g_dp, g_y, g_y_dp]
 
     keep1, send1, back1, *own1 = half_attention(meta, thin, thick, first_rim, False)
-    from_near = lax.ppermute(back1, "seq", near_pairs)
+    from_long = lax.ppermute(back1, "seq", long_pairs)
     if direct:
         at_y1 = swapped(send1, 2, count)
         at_dp1 = turned(keep1, dp_count)[0]
@@ -379,7 +379,7 @@
         at_y2 = swapped(send2, 2, count)
         at_dp2 = turned(keep2, dp_count)[0]
         at_y_dp2 = turned(at_y2, dp_count)[0]
-    from_long = lax.ppermute(back2, "seq", long_pairs)
+    from_near = lax.ppermute(back2, "seq", near_pairs)
 
     frames = rows * count * dp_count
     if direct:
@@ -392,7 +392,7 @@
         wo_grad = kept + swapped(sent, 1, count).astype(f32)
     else:
         wo_grad = general_sum((keep1, send1), (keep2, send2), g, sides, place, mine, y_digit, count, dp_count)
-    dq, dk, dv = joined(meta, own1, own2, from_near, from_long, q.shape)
+    dq, dk, dv = joined(meta, own1, own2, from_long, from_near, q.shape)
     return dq[None], dk[None], dv[None], wo_grad * frames ** -0.5
 
 

time: 86.5 us -> 78.4 us (0.906)
  waiting for transfers between devices: 42.6 us -> 30.6 us
  starting transfers between devices: 20.2 us -> 24.1 us
    ppermute x4, waiting for transfers between devices: 13.7 us -> 0.01 us  [the longest x1 0.01 us: on_device(): second_rim = lax.ppermute(rim2, 'seq', near_pairs)]
    ppermute x7, starting transfers between devices: 14.1 us -> 16.2 us  [swapped(): return lax.ppermute(value, 'seq', [(i, i ^ stride) for i in range(count)])]
    ppermute x4, starting transfers between devices: 5.44 us -> 7.19 us  [the longest x1 3.1 us: on_device(): from_near = lax.ppermute(back2, 'seq', near_pairs)]
    ppermute x7, waiting for transfers between devices: 27.9 us -> 29.6 us  [swapped(): return lax.ppermute(value, 'seq', [(i, i ^ stride) for i in range(count)])]
  transfers between devices with their start and end apart: 17 -> 17, of which waited for: 8 -> 7; matrix products, arithmetic and copies ran while one was open for 1% -> 1% of each run, Pallas kernels for 25% -> 27%
where the time goes in v4:
time: 78.4 us; the launch traced here: 78.2 us
  waiting for transfers between devices  30.6 us (39%)
  starting transfers between devices  24.1 us (31%)
  Pallas kernels  21.3 us (27%)
  between operations  0.83 us (1%)
    ppermute x7, waiting for transfers between devices, swapped(): return lax.ppermute(value, 'seq', [(i, i ^ stride) for i in range(count)])  29.6 us
    ppermute x7, starting transfers between devices, swapped(): return lax.ppermute(value, 'seq', [(i, i ^ stride) for i in range(count)])  16.2 us
    pallas_call x2, Pallas kernels, half_attention(): pl.pallas_call(functools.partial(half_kernel, second=second), in_specs=[i...  10.9 us
    pallas_call x1, Pallas kernels, prepared(): pl.pallas_call(prepare_kernel, in_specs=[in_smem] + [in_vmem] * 5, out_sp...  4.62 us
    ppermute x1, starting transfers between devices, on_device(): from_near = lax.ppermute(back2, 'seq', near_pairs)  3.1 us
    ppermute x1, starting transfers between devices, on_device(): second_rim = lax.ppermute(rim2, 'seq', near_pairs)  2.72 us
    pallas_call x1, Pallas kernels, joined(): pl.pallas_call(join_kernel, in_specs=[in_smem] + [in_vmem] * 6, out_specs...  2.04 us
    pallas_call x1, Pallas kernels, packed_rim(): pl.pallas_call(rim_kernel, grid_spec=pltpu.PrefetchScalarGridSpec(num_sca...  1.92 us
  transfers between devices with their start and end apart: 17, of which 7 were waited for; matrix products, arithmetic and copies ran while one was open for 1% of the time, Pallas kernels for 27%

profile of v4, /device:TPU:0, one launch (start us, length us, event | category | flops | bytes accessed | tf_op | source)
XLA Modules:
  0.0 78.2 jit_solution(14945625845296034513)
XLA Ops:
  0.6 3.1 %collective-permute-start.11 = (bf16[256,1024]{1,0:T(8,128)(2,1)}, bf16[256,1024]{1,0:T(8,128)(2,1)S(1)}, u32[]{:S(2)}, u32[]{:S(2)}) collective-permute-start(bf16[256,1024]{1,0:T(8,128)(2,1)} %bitcast.12), channel_id=1, source_target_pairs={{0,4},{2,6},{4,0},{6,2},{8,12},{10,14},{12,8},{14,10},{16,20},{18,... | collective-permute-start | bytes 1572872 | tf_op jit(solution)/shard_map/ppermute | solution.py:295
  3.7 1.9 %shard_map.84 = bf16[8,2,128,128]{3,2,1,0:T(8,128)(2,1)} custom-call(s32[1]{0:T(128)} %bitcast.side_ref, bf16[256,1024]{1,0:T(8,128)(2,1)} %bitcast.16, bf16[256,1024]{1,0:T(8,128)(2,1)} %bitcast.18), custom_call_target="tpu_custom_call" | custom-call | tf_op jit(solution)/shard_map/pallas_call | solution.py:174
  5.6 0.7 collective-permute-start
  6.4 0.6 stack.28.meta_ref
  7.0 0.0 copy-start
  7.0 0.0 copy-start.5
  7.0 4.6 %prepared.1 = (bf16[8,2,2,128,128]{4,3,2,1,0:T(8,128)(2,1)}, bf16[8,2,2,128,128]{4,3,2,1,0:T(8,128)(2,1)}, bf16[8,2,128,128]{3,2,1,0:T(8,128)(2,1)}) custom-call(s32[7]{0:T(128)} %stack.28.meta_ref, bf16[256,1024]{1,0:T(8,128)(2,1)} %bitcast.20, bf16[256,1024]{1,0:T(8,128)(2,1)} %bitcast.17, bf16[256,1024]{1,0:T(8,128)(2,1)} %bitcast.19, ...), custom_call_target="tpu_custom_call" | custom-call | flops 536870912 | bytes 5767168 | tf_op jit(solution)/shard_map/prepared/pallas_call | solution.py:208
  11.6 2.7 %collective-permute-start.1 = (bf16[8,2,128,128]{3,2,1,0:T(8,128)(2,1)}, bf16[8,2,128,128]{3,2,1,0:T(8,128)(2,1)S(1)}, u32[]{:S(2)}, u32[]{:S(2)}) collective-permute-start(bf16[8,2,128,128]{3,2,1,0:T(8,128)(2,1)} %get-tuple-element.30), channel_id=1, source_target_pairs={{0,2},{2,0},{4,6},{6,4},{8,10},{10,8},{12,14},{14,12},{16,18},{18,... | collective-permute-start | bytes 1572872 | tf_op jit(solution)/shard_map/ppermute | solution.py:365
  14.3 0.0 copy-done
  14.3 0.0 collective-permute-start.10
  14.3 12.1 %collective-permute-done.11.refs_10_ = bf16[256,1024]{1,0:T(8,128)(2,1)S(1)} collective-permute-done((bf16[256,1024]{1,0:T(8,128)(2,1)}, bf16[256,1024]{1,0:T(8,128)(2,1)S(1)}, u32[]{:S(2)}, u32[]{:S(2)}) %collective-permute-start.11) | collective-permute-done | bytes 524320 | tf_op jit(solution)/shard_map/ppermute | solution.py:295
  26.4 0.0 collective-permute-start.12
  26.4 0.0 collective-permute-done.rim_hbm
  26.4 0.0 copy-done.5
  26.4 5.5 %shard_map.85 = (bf16[512,128]{1,0:T(8,128)(2,1)S(1)}, bf16[512,128]{1,0:T(8,128)(2,1)S(1)}, bf16[8,2,128,128]{3,2,1,0:T(8,128)(2,1)S(1)}, bf16[8,128,128]{2,1,0:T(8,128)(2,1)}, bf16[8,2,256,128]{3,2,1,0:T(8,128)(2,1)}) custom-call(s32[7]{0:T(128)S(1)} %copy-done.5, bf16[8,2,2,128,128]{4,3,2,1,0:T(8,128)(2,1)} %get-tuple-element.26.thin_hbm, ...), custom_call_target="tpu_custom_call" | custom-call | flops 603979776 | bytes 4194304 | tf_op jit(solution)/shard_map/pallas_call | solution.py:133
  31.9 2.4 %collective-permute-start.4 = (bf16[512,128]{1,0:T(8,128)(2,1)S(1)}, bf16[512,128]{1,0:T(8,128)(2,1)S(1)}, u32[]{:S(2)}, u32[]{:S(2)}) collective-permute-start(bf16[512,128]{1,0:T(8,128)(2,1)S(1)} %get-tuple-element.39), channel_id=1, source_target_pairs={{0,4},{2,6},{4,0},{6,2},{8,12},{10,14},{12,8},{14,10},{16,20},{18,... | collective-permute-start | bytes 393224 | tf_op jit(solution)/shard_map/ppermute | solution.py:295
  34.3 0.2 collective-permute-start.5
  34.6 0.0 collective-permute-done.1.rim_hbm
  34.6 0.7 collective-permute-start.2
  35.3 5.4 %shard_map.86 = (bf16[512,128]{1,0:T(8,128)(2,1)S(1)}, bf16[512,128]{1,0:T(8,128)(2,1)S(1)}, bf16[8,2,128,128]{3,2,1,0:T(8,128)(2,1)S(1)}, bf16[8,128,128]{2,1,0:T(8,128)(2,1)}, bf16[8,2,256,128]{3,2,1,0:T(8,128)(2,1)}) custom-call(s32[7]{0:T(128)S(1)} %copy-done.5, bf16[8,2,2,128,128]{4,3,2,1,0:T(8,128)(2,1)} %get-tuple-element.26.thin_hbm, ...), custom_call_target="tpu_custom_call" | custom-call | flops 603979776 | bytes 4194304 | tf_op jit(solution)/shard_map/pallas_call | solution.py:133
  40.7 0.0 copy-start.1
  40.7 0.0 copy-start.2
  40.7 0.0 copy-start.3
  40.7 0.0 copy-start.4
  40.7 0.0 collective-permute-done.10.refs_9_
  40.7 3.1 %collective-permute-start.3 = (bf16[8,2,128,128]{3,2,1,0:T(8,128)(2,1)S(1)}, bf16[8,2,128,128]{3,2,1,0:T(8,128)(2,1)S(1)}, u32[]{:S(2)}, u32[]{:S(2)}) collective-permute-start(bf16[8,2,128,128]{3,2,1,0:T(8,128)(2,1)S(1)} %get-tuple-element.34), channel_id=1, source_target_pairs={{0,2},{2,0},{4,6},{6,4},{8,10},{10,8},{12,14},{14,12},{16,18},{18,... | collective-permute-start | bytes 1572872 | tf_op jit(solution)/shard_map/ppermute | solution.py:382
  43.8 0.0 collective-permute-done.4.refs_1_
  43.9 2.7 %collective-permute-start.7 = (bf16[512,128]{1,0:T(8,128)(2,1)S(1)}, bf16[512,128]{1,0:T(8,128)(2,1)S(1)}, u32[]{:S(2)}, u32[]{:S(2)}) collective-permute-start(bf16[512,128]{1,0:T(8,128)(2,1)S(1)} %get-tuple-element.41), channel_id=1, source_target_pairs={{0,4},{2,6},{4,0},{6,2},{8,12},{10,14},{12,8},{14,10},{16,20},{18,... | collective-permute-start | bytes 393224 | tf_op jit(solution)/shard_map/ppermute | solution.py:295
  46.5 0.0 collective-permute-done.5.refs_2_
  46.5 0.0 collective-permute-start.8
  46.5 5.6 %collective-permute-done.7.refs_5_ = bf16[512,128]{1,0:T(8,128)(2,1)S(1)} collective-permute-done((bf16[512,128]{1,0:T(8,128)(2,1)S(1)}, bf16[512,128]{1,0:T(8,128)(2,1)S(1)}, u32[]{:S(2)}, u32[]{:S(2)}) %collective-permute-start.7) | collective-permute-done | bytes 131104 | tf_op jit(solution)/shard_map/ppermute | solution.py:295
  52.1 0.0 collective-permute-start.6
  52.1 0.0 collective-permute-done.8.refs_6_
  52.1 0.5 collective-permute-start.9
  52.6 0.8 %collective-permute-done.6.refs_3_ = bf16[512,128]{1,0:T(8,128)(2,1)S(1)} collective-permute-done((bf16[512,128]{1,0:T(8,128)(2,1)S(1)}, bf16[512,128]{1,0:T(8,128)(2,1)S(1)}, u32[]{:S(2)}, u32[]{:S(2)}) %collective-permute-start.6) | collective-permute-done | bytes 131104 | tf_op jit(solution)/shard_map/ppermute | solution.py:299
  53.5 0.2 collective-permute-done.9.refs_7_
  53.6 0.0 collective-permute-done.12.refs_11_
  53.6 1.3 %product.1 = (f32[128,512]{1,0:T(8,128)S(1)}, bf16[128,512]{1,0:T(8,128)(2,1)S(1)}, bf16[128,512]{1,0:T(8,128)(2,1)S(1)}, bf16[128,512]{1,0:T(8,128)(2,1)S(1)}) custom-call(s32[7]{0:T(128)S(1)} %copy-done.5, bf16[512,128]{1,0:T(8,128)(2,1)S(1)} %get-tuple-element.38.refs_0_, bf16[512,128]{1,0:T(8,128)(2,1)S(1)} %collective-permute-done.4.refs_1_, ...), custom_call_target="tpu_custom_call" | custom-call | tf_op jit(solution)/shard_map/product/pallas_call | solution.py:237
  54.9 4.7 %collective-permute-start.13 = (bf16[128,512]{1,0:T(8,128)(2,1)S(1)}, bf16[128,512]{1,0:T(8,128)(2,1)S(1)}, u32[]{:S(2)}, u32[]{:S(2)}) collective-permute-start(bf16[128,512]{1,0:T(8,128)(2,1)S(1)} %get-tuple-element.43), channel_id=1, source_target_pairs={{0,8},{2,10},{4,12},{6,14},{8,0},{10,2},{12,4},{14,6},{16,24},{18,... | collective-permute-start | bytes 393224 | tf_op jit(solution)/shard_map/ppermute | solution.py:295
  59.6 2.6 %collective-permute-start.14 = (bf16[128,512]{1,0:T(8,128)(2,1)S(1)}, bf16[128,512]{1,0:T(8,128)(2,1)S(1)}, u32[]{:S(2)}, u32[]{:S(2)}) collective-permute-start(bf16[128,512]{1,0:T(8,128)(2,1)S(1)} %get-tuple-element.44), channel_id=1, source_target_pairs={{0,16},{2,18},{4,20},{6,22},{8,24},{10,26},{12,28},{14,30},{16,0},... | collective-permute-start | bytes 393224 | tf_op jit(solution)/shard_map/ppermute | solution.py:295
  62.3 0.0 collective-permute-start.15
  62.3 3.4 %collective-permute-done.13.refs_0_ = bf16[128,512]{1,0:T(8,128)(2,1)S(1)} collective-permute-done((bf16[128,512]{1,0:T(8,128)(2,1)S(1)}, bf16[128,512]{1,0:T(8,128)(2,1)S(1)}, u32[]{:S(2)}, u32[]{:S(2)}) %collective-permute-start.13) | collective-permute-done | bytes 131104 | tf_op jit(solution)/shard_map/ppermute | solution.py:295
  65.7 6.9 %collective-permute-done.14.refs_1_ = bf16[128,512]{1,0:T(8,128)(2,1)S(1)} collective-permute-done((bf16[128,512]{1,0:T(8,128)(2,1)S(1)}, bf16[128,512]{1,0:T(8,128)(2,1)S(1)}, u32[]{:S(2)}, u32[]{:S(2)}) %collective-permute-start.14) | collective-permute-done | bytes 131104 | tf_op jit(solution)/shard_map/ppermute | solution.py:295
  72.6 0.0 collective-permute-done.15.refs_2_
  72.6 0.6 summed.1
  73.2 0.7 collective-permute-start.16
  73.8 0.0 collective-permute-done.2.rim1_ref
  73.8 0.0 collective-permute-done.3.rim2_ref
  73.8 0.0 copy-done.1
  73.8 0.0 copy-done.2
  73.9 0.0 copy-done.3
  73.9 0.0 copy-done.4
  73.9 2.0 %joined.1 = (bf16[256,1024]{1,0:T(8,128)(2,1)}, bf16[256,1024]{1,0:T(8,128)(2,1)}, bf16[256,1024]{1,0:T(8,128)(2,1)}) custom-call(s32[7]{0:T(128)S(1)} %copy-done.5, bf16[8,128,128]{2,1,0:T(8,128)(2,1)S(1)} %copy-done.3, bf16[8,2,256,128]{3,2,1,0:T(8,128)(2,1)S(1)} %copy-done.1, bf16[8,128,128]{2,1,0:T(8,128)(2,1)S(1)} %copy-done.4, ...), custom_call_target="tpu_custom_call" | custom-call | tf_op jit(solution)/shard_map/joined/pallas_call | solution.py:284
  75.9 1.6 %collective-permute-done.16 = bf16[64,512]{1,0:T(8,128)(2,1)S(1)} collective-permute-done((bf16[64,512]{1,0:T(8,128)(2,1)S(1)}, bf16[64,512]{1,0:T(8,128)(2,1)S(1)}, u32[]{:S(2)}, u32[]{:S(2)}) %collective-permute-start.16) | collective-permute-done | bytes 65568 | tf_op jit(solution)/shard_map/ppermute | solution.py:295
  77.5 0.7 add_multiply_fusion
Async XLA Ops:
  0.6 25.8 %collective-permute-start.11 = (bf16[256,1024]{1,0:T(8,128)(2,1)}, bf16[256,1024]{1,0:T(8,128)(2,1)S(1)}, u32[]{:S(2)}, u32[]{:S(2)}) collective-permute-start(bf16[256,1024]{1,0:T(8,128)(2,1)} %bitcast.12), channel_id=1, source_target_pairs={{0,4},{2,6},{4,0},{6,2},{8,12},{10,14},{12,8},{14,10},{16,20},{18,... | collective-permute-start | bytes 1572872 | tf_op jit(solution)/shard_map/ppermute | solution.py:295
  5.6 20.8 %collective-permute-start = (bf16[8,2,128,128]{3,2,1,0:T(8,128)(2,1)}, bf16[8,2,128,128]{3,2,1,0:T(8,128)(2,1)S(1)}, u32[]{:S(2)}, u32[]{:S(2)}) collective-permute-start(bf16[8,2,128,128]{3,2,1,0:T(8,128)(2,1)} %shard_map.84), channel_id=1, source_target_pairs={{2,4},{4,2},{6,8},{8,6},{10,12},{12,10},{14,16},{16,14},{18,20},{2... | collective-permute-start | bytes 1572872 | tf_op jit(solution)/shard_map/ppermute | solution.py:361
  7.0 7.3 %copy-start = (bf16[1,256,1024]{2,1,0:T(8,128)(2,1)S(1)}, bf16[1,256,1024]{2,1,0:T(8,128)(2,1)}, u32[]{:S(2)}) copy-start(bf16[1,256,1024]{2,1,0:T(8,128)(2,1)} %param.8) | copy-start | bytes 1572868
  7.0 19.5 %copy-start.5 = (s32[7]{0:T(128)S(1)}, s32[7]{0:T(128)}, u32[]{:S(2)}) copy-start(s32[7]{0:T(128)} %stack.28.meta_ref) | copy-start | bytes 88
  11.6 23.0 %collective-permute-start.1 = (bf16[8,2,128,128]{3,2,1,0:T(8,128)(2,1)}, bf16[8,2,128,128]{3,2,1,0:T(8,128)(2,1)S(1)}, u32[]{:S(2)}, u32[]{:S(2)}) collective-permute-start(bf16[8,2,128,128]{3,2,1,0:T(8,128)(2,1)} %get-tuple-element.30), channel_id=1, source_target_pairs={{0,2},{2,0},{4,6},{6,4},{8,10},{10,8},{12,14},{14,12},{16,18},{18,... | collective-permute-start | bytes 1572872 | tf_op jit(solution)/shard_map/ppermute | solution.py:365
  14.3 26.4 %collective-permute-start.10 = (bf16[256,1024]{1,0:T(8,128)(2,1)S(1)}, bf16[256,1024]{1,0:T(8,128)(2,1)S(1)}, u32[]{:S(2)}, u32[]{:S(2)}) collective-permute-start(bf16[256,1024]{1,0:T(8,128)(2,1)S(1)} %bitcast.14), channel_id=1, source_target_pairs={{0,1},{1,0},{2,3},{3,2},{4,5},{5,4},{6,7},{7,6},{8,9},{9,8},{10,11... | collective-permute-start | bytes 1572872 | tf_op jit(solution)/shard_map/ppermute | solution.py:299
  26.4 27.2 %collective-permute-start.12 = (bf16[256,1024]{1,0:T(8,128)(2,1)S(1)}, bf16[256,1024]{1,0:T(8,128)(2,1)S(1)}, u32[]{:S(2)}, u32[]{:S(2)}) collective-permute-start(bf16[256,1024]{1,0:T(8,128)(2,1)S(1)} %collective-permute-done.11.refs_10_), channel_id=1, source_target_pairs={{0,1},{1,0},{2,3},{3,2},{4,5},{5,4},{6,7},{7,6},{8,9},{9,8},{10,11... | collective-permute-start | bytes 1572872 | tf_op jit(solution)/shard_map/ppermute | solution.py:299
  31.9 12.0 %collective-permute-start.4 = (bf16[512,128]{1,0:T(8,128)(2,1)S(1)}, bf16[512,128]{1,0:T(8,128)(2,1)S(1)}, u32[]{:S(2)}, u32[]{:S(2)}) collective-permute-start(bf16[512,128]{1,0:T(8,128)(2,1)S(1)} %get-tuple-element.39), channel_id=1, source_target_pairs={{0,4},{2,6},{4,0},{6,2},{8,12},{10,14},{12,8},{14,10},{16,20},{18,... | collective-permute-start | bytes 393224 | tf_op jit(solution)/shard_map/ppermute | solution.py:295
  34.3 12.2 %collective-permute-start.5 = (bf16[512,128]{1,0:T(8,128)(2,1)S(1)}, bf16[512,128]{1,0:T(8,128)(2,1)S(1)}, u32[]{:S(2)}, u32[]{:S(2)}) collective-permute-start(bf16[512,128]{1,0:T(8,128)(2,1)S(1)} %get-tuple-element.38.refs_0_), channel_id=1, source_target_pairs={{0,1},{1,0},{2,3},{3,2},{4,5},{5,4},{6,7},{7,6},{8,9},{9,8},{10,11... | collective-permute-start | bytes 393224 | tf_op jit(solution)/shard_map/ppermute | solution.py:299
  34.6 39.3 %collective-permute-start.2 = (bf16[8,2,128,128]{3,2,1,0:T(8,128)(2,1)S(1)}, bf16[8,2,128,128]{3,2,1,0:T(8,128)(2,1)S(1)}, u32[]{:S(2)}, u32[]{:S(2)}) collective-permute-start(bf16[8,2,128,128]{3,2,1,0:T(8,128)(2,1)S(1)} %get-tuple-element.33), channel_id=1, source_target_pairs={{2,4},{4,2},{6,8},{8,6},{10,12},{12,10},{14,16},{16,14},{18,20},{2... | collective-permute-start | bytes 1572872 | tf_op jit(solution)/shard_map/ppermute | solution.py:372
  40.7 33.2 %copy-start.1 = (bf16[8,2,256,128]{3,2,1,0:T(8,128)(2,1)S(1)}, bf16[8,2,256,128]{3,2,1,0:T(8,128)(2,1)}, u32[]{:S(2)}) copy-start(bf16[8,2,256,128]{3,2,1,0:T(8,128)(2,1)} %get-tuple-element.29.own1_ref) | copy-start | bytes 3145732
  40.7 33.2 %copy-start.2 = (bf16[8,2,256,128]{3,2,1,0:T(8,128)(2,1)S(1)}, bf16[8,2,256,128]{3,2,1,0:T(8,128)(2,1)}, u32[]{:S(2)}) copy-start(bf16[8,2,256,128]{3,2,1,0:T(8,128)(2,1)} %get-tuple-element.32.own2_ref) | copy-start | bytes 3145732
  40.7 33.2 %copy-start.3 = (bf16[8,128,128]{2,1,0:T(8,128)(2,1)S(1)}, bf16[8,128,128]{2,1,0:T(8,128)(2,1)}, u32[]{:S(2)}) copy-start(bf16[8,128,128]{2,1,0:T(8,128)(2,1)} %get-tuple-element.28.dq1_ref) | copy-start | bytes 786436
  40.7 33.2 %copy-start.4 = (bf16[8,128,128]{2,1,0:T(8,128)(2,1)S(1)}, bf16[8,128,128]{2,1,0:T(8,128)(2,1)}, u32[]{:S(2)}) copy-start(bf16[8,128,128]{2,1,0:T(8,128)(2,1)} %get-tuple-element.31.dq2_ref) | copy-start | bytes 786436
  40.7 33.1 %collective-permute-start.3 = (bf16[8,2,128,128]{3,2,1,0:T(8,128)(2,1)S(1)}, bf16[8,2,128,128]{3,2,1,0:T(8,128)(2,1)S(1)}, u32[]{:S(2)}, u32[]{:S(2)}) collective-permute-start(bf16[8,2,128,128]{3,2,1,0:T(8,128)(2,1)S(1)} %get-tuple-element.34), channel_id=1, source_target_pairs={{0,2},{2,0},{4,6},{6,4},{8,10},{10,8},{12,14},{14,12},{16,18},{18,... | collective-permute-start | bytes 1572872 | tf_op jit(solution)/shard_map/ppermute | solution.py:382
  43.9 8.3 %collective-permute-start.7 = (bf16[512,128]{1,0:T(8,128)(2,1)S(1)}, bf16[512,128]{1,0:T(8,128)(2,1)S(1)}, u32[]{:S(2)}, u32[]{:S(2)}) collective-permute-start(bf16[512,128]{1,0:T(8,128)(2,1)S(1)} %get-tuple-element.41), channel_id=1, source_target_pairs={{0,4},{2,6},{4,0},{6,2},{8,12},{10,14},{12,8},{14,10},{16,20},{18,... | collective-permute-start | bytes 393224 | tf_op jit(solution)/shard_map/ppermute | solution.py:295
  46.5 5.6 %collective-permute-start.8 = (bf16[512,128]{1,0:T(8,128)(2,1)S(1)}, bf16[512,128]{1,0:T(8,128)(2,1)S(1)}, u32[]{:S(2)}, u32[]{:S(2)}) collective-permute-start(bf16[512,128]{1,0:T(8,128)(2,1)S(1)} %get-tuple-element.40.refs_4_), channel_id=1, source_target_pairs={{0,1},{1,0},{2,3},{3,2},{4,5},{5,4},{6,7},{7,6},{8,9},{9,8},{10,11... | collective-permute-start | bytes 393224 | tf_op jit(solution)/shard_map/ppermute | solution.py:299
  52.1 1.3 %collective-permute-start.6 = (bf16[512,128]{1,0:T(8,128)(2,1)S(1)}, bf16[512,128]{1,0:T(8,128)(2,1)S(1)}, u32[]{:S(2)}, u32[]{:S(2)}) collective-permute-start(bf16[512,128]{1,0:T(8,128)(2,1)S(1)} %collective-permute-done.4.refs_1_), channel_id=1, source_target_pairs={{0,1},{1,0},{2,3},{3,2},{4,5},{5,4},{6,7},{7,6},{8,9},{9,8},{10,11... | collective-permute-start | bytes 393224 | tf_op jit(solution)/shard_map/ppermute | solution.py:299
  52.1 1.5 %collective-permute-start.9 = (bf16[512,128]{1,0:T(8,128)(2,1)S(1)}, bf16[512,128]{1,0:T(8,128)(2,1)S(1)}, u32[]{:S(2)}, u32[]{:S(2)}) collective-permute-start(bf16[512,128]{1,0:T(8,128)(2,1)S(1)} %collective-permute-done.7.refs_5_), channel_id=1, source_target_pairs={{0,1},{1,0},{2,3},{3,2},{4,5},{5,4},{6,7},{7,6},{8,9},{9,8},{10,11... | collective-permute-start | bytes 393224 | tf_op jit(solution)/shard_map/ppermute | solution.py:299
  54.9 10.7 %collective-permute-start.13 = (bf16[128,512]{1,0:T(8,128)(2,1)S(1)}, bf16[128,512]{1,0:T(8,128)(2,1)S(1)}, u32[]{:S(2)}, u32[]{:S(2)}) collective-permute-start(bf16[128,512]{1,0:T(8,128)(2,1)S(1)} %get-tuple-element.43), channel_id=1, source_target_pairs={{0,8},{2,10},{4,12},{6,14},{8,0},{10,2},{12,4},{14,6},{16,24},{18,... | collective-permute-start | bytes 393224 | tf_op jit(solution)/shard_map/ppermute | solution.py:295
  59.6 12.9 %collective-permute-start.14 = (bf16[128,512]{1,0:T(8,128)(2,1)S(1)}, bf16[128,512]{1,0:T(8,128)(2,1)S(1)}, u32[]{:S(2)}, u32[]{:S(2)}) collective-permute-start(bf16[128,512]{1,0:T(8,128)(2,1)S(1)} %get-tuple-element.44), channel_id=1, source_target_pairs={{0,16},{2,18},{4,20},{6,22},{8,24},{10,26},{12,28},{14,30},{16,0},... | collective-permute-start | bytes 393224 | tf_op jit(solution)/shard_map/ppermute | solution.py:295
  62.3 10.3 %collective-permute-start.15 = (bf16[128,512]{1,0:T(8,128)(2,1)S(1)}, bf16[128,512]{1,0:T(8,128)(2,1)S(1)}, u32[]{:S(2)}, u32[]{:S(2)}) collective-permute-start(bf16[128,512]{1,0:T(8,128)(2,1)S(1)} %get-tuple-element.45), channel_id=1, source_target_pairs={{0,24},{2,26},{4,28},{6,30},{8,16},{10,18},{12,20},{14,22},{16,8},... | collective-permute-start | bytes 393224 | tf_op jit(solution)/shard_map/ppermute | solution.py:295
  73.2 4.3 %collective-permute-start.16 = (bf16[64,512]{1,0:T(8,128)(2,1)S(1)}, bf16[64,512]{1,0:T(8,128)(2,1)S(1)}, u32[]{:S(2)}, u32[]{:S(2)}) collective-permute-start(bf16[64,512]{1,0:T(8,128)(2,1)S(1)} %get-tuple-element.47), channel_id=1, source_target_pairs={{0,2},{2,0},{4,6},{6,4},{8,10},{10,8},{12,14},{14,12},{16,18},{18,... | collective-permute-start | bytes 196616 | tf_op jit(solution)/shard_map/ppermute | solution.py:295

commit v5 on v4

--- a/solution.py
+++ b/solution.py
@@ -28,8 +28,13 @@
     return lax.dot_general(a, b, (dims, ((), ())), preferred_element_type=f32)
 
 
-def half_kernel(meta_ref, thin_hbm, thick_hbm, rim_hbm, keep_ref, send_ref, back_ref, dq_hbm, own_hbm,
-                one_ref, wide_ref, two_ref, score_ref, dp_ref, p_ref, ds_ref, dq_ref, own_ref, in_sem, out_sem, *, second):
+def half_kernel(meta_ref, thin_hbm, thick_hbm, rim_hbm, *refs, second, front, back):
+    refs = list(refs)
+    keep_ref, send_ref = [refs.pop(0) for _ in range(2)] if front else (None, None)
+    back_ref, dq_hbm, own_hbm = [refs.pop(0) for _ in range(3)] if back else (None, None, None)
+    one_ref, wide_ref, two_ref, score_ref, p_ref, in_sem = refs[:6]
+    if back:
+        dp_ref, ds_ref, dq_ref, own_ref, out_sem = refs[6:]
     side = 1 - meta_ref[0] if second else meta_ref[0]
     alone = meta_ref[6 if second else 5]
     bias = jnp.where(alone == 1, masked_score, 0.0).astype(f32)
@@ -40,13 +45,15 @@
     pairs = one_ref.shape[0]
     early = 2
     middle = pairs // 2
+    kinds = range(2 if back else 1)
 
     def pair_of(number):
         return 2 * (number // 2) + (y_digit if number % 2 == 0 else 1 - y_digit)
 
     def fetches(group):
         some = pl.ds(0, early) if group == 0 else pl.ds(early, pairs - early)
-        found = [(thin_hbm.at[some, :, side], one_ref.at[some])]
+        these = pl.ds(0, len(kinds))
+        found = [(thin_hbm.at[some, these, side], one_ref.at[some])]
         for place, source in enumerate((rim_hbm.at[some], thick_hbm.at[some, :, side], thick_hbm.at[some, :, 1 - side])):
             found.append((source, wide_ref.at[some, :, pl.ds(place * HALF, HALF)]))
         return [pltpu.make_async_copy(a, b, in_sem.at[group, place]) for place, (a, b) in enumerate(found)]
@@ -60,10 +67,11 @@
         pair = pair_of(number)
         slot = number % 3
         first_head = lax.broadcasted_iota(jnp.int32, (HALF, PAIR), 1) < HEAD_DIM
-        for which, (factor, out) in enumerate(((scale, score_ref), (1.0, dp_ref))):
-            one = one_ref[pair, which].astype(f32) * factor
+        for which in kinds:
+            one = one_ref[pair, which].astype(f32) * (1.0 if which else scale)
             two_ref[slot, which, :HALF] = jnp.where(first_head, one, 0.0).astype(bf16)
             two_ref[slot, which, HALF:] = jnp.where(first_head, 0.0, one).astype(bf16)
+            out = dp_ref if which else score_ref
             out[number % 2] = contract(wide_ref[pair, which], two_ref[slot, which], NT)
 
     def weigh(number):
@@ -78,10 +86,13 @@
         inv = 1.0 / jnp.sum(e_edge + e_near, axis=0, keepdims=True)
         p_edge = e_edge * inv
         p_near = e_near * inv
-        d_edge = jnp.where(in_rim, dp_ref[slot, :HALF], dp_ref[slot, 2 * HALF :])
-        d_near = dp_ref[slot, HALF : 2 * HALF]
-        delta = jnp.sum(p_edge * d_edge + p_near * d_near, axis=0, keepdims=True)
-        for ref, edge, near in ((p_ref, p_edge, p_near), (ds_ref, p_edge * (d_edge - delta), p_near * (d_near - delta))):
+        found = [(p_ref, p_edge, p_near)]
+        if back:
+            d_edge = jnp.where(in_rim, dp_ref[slot, :HALF], dp_ref[slot, 2 * HALF :])
+            d_near = dp_ref[slot, HALF : 2 * HALF]
+            delta = jnp.sum(p_edge * d_edge + p_near * d_near, axis=0, keepdims=True)
+            found.append((ds_ref, p_edge * (d_edge - delta), p_near * (d_near - delta)))
+        for ref, edge, near in found:
             ref[slot, :HALF] = jnp.where(in_rim, edge, 0.0).astype(bf16)
             ref[slot, HALF : 2 * HALF] = near.astype(bf16)
             ref[slot, 2 * HALF :] = jnp.where(in_rim, 0.0, edge).astype(bf16)
@@ -89,11 +100,14 @@
     def spread(number):
         slot = number % 2
         pair = pair_of(number)
-        at_ref = send_ref if number % 2 else keep_ref
-        start = number // 2 * PAIR
-        at = contract(wide_ref[pair, 1], p_ref[slot], TN)
-        at_ref[start : start + HEAD_DIM, :] = at[:HEAD_DIM, :HALF].astype(bf16)
-        at_ref[start + HEAD_DIM : start + PAIR, :] = at[HEAD_DIM:, HALF:].astype(bf16)
+        if front:
+            at_ref = send_ref if number % 2 else keep_ref
+            start = number // 2 * PAIR
+            at = contract(wide_ref[pair, 1], p_ref[slot], TN)
+            at_ref[start : start + HEAD_DIM, :] = at[:HEAD_DIM, :HALF].astype(bf16)
+            at_ref[start + HEAD_DIM : start + PAIR, :] = at[HEAD_DIM:, HALF:].astype(bf16)
+        if not back:
+            return
         for which, left in enumerate((ds_ref, p_ref)):
             part = contract(left[slot], two_ref[number % 3, which], NN)
             back_ref[pair, which] = part[:HALF].astype(bf16)
@@ -119,42 +133,53 @@
             spread(step - 2)
         if 0 <= step - 1 < pairs:
             weigh(step - 1)
-    for group in range(2):
-        for copy in stores(group):
-            copy.wait()
-
-
-def half_attention(meta, thin, thick, rim, second):
+    if back:
+        for group in range(2):
+            for copy in stores(group):
+                copy.wait()
+
+
+def half_attention(meta, thin, thick, rim, second, front=True, back=True):
     pairs, _, blocks, _, _ = thick.shape
     rows = blocks * HALF
     width = pairs * PAIR
+    kinds = 2 if back else 1
     in_hbm = pl.BlockSpec(memory_space=pltpu.HBM)
     held = [pltpu.with_memory_space_constraint(array, pltpu.HBM) for array in (thin, thick)]
-    return pl.pallas_call(
-        functools.partial(half_kernel, second=second),
-        in_specs=[in_smem, in_hbm, in_hbm, pl.BlockSpec(memory_space=pl.ANY)],
-        out_specs=[in_vmem] * 3 + [in_hbm] * 2,
-        out_shape=[
-            jax.ShapeDtypeStruct((width // 2, HALF), bf16),
-            jax.ShapeDtypeStruct((width // 2, HALF), bf16),
+    out_specs, out_shape = [], []
+    if front:
+        out_specs += [in_vmem] * 2
+        out_shape += [jax.ShapeDtypeStruct((width // 2, HALF), bf16)] * 2
+    if back:
+        out_specs += [in_vmem, in_hbm, in_hbm]
+        out_shape += [
             jax.ShapeDtypeStruct((pairs, 2, HALF, PAIR), bf16),
             pltpu.HBM((pairs, HALF, PAIR), bf16),
             pltpu.HBM((pairs, 2, rows, PAIR), bf16),
-        ],
-        scratch_shapes=[
-            pltpu.VMEM((pairs, 2, HALF, PAIR), bf16),
-            pltpu.VMEM((pairs, 2, 3 * HALF, PAIR), bf16),
-            pltpu.VMEM((3, 2, 2 * HALF, PAIR), bf16),
+        ]
+    scratch = [
+        pltpu.VMEM((pairs, kinds, HALF, PAIR), bf16),
+        pltpu.VMEM((pairs, 2, 3 * HALF, PAIR), bf16),
+        pltpu.VMEM((3, kinds, 2 * HALF, PAIR), bf16),
+        pltpu.VMEM((2, 3 * HALF, 2 * HALF), f32),
+        pltpu.VMEM((2, 3 * HALF, 2 * HALF), bf16),
+        pltpu.SemaphoreType.DMA((2, 4)),
+    ]
+    if back:
+        scratch += [
             pltpu.VMEM((2, 3 * HALF, 2 * HALF), f32),
-            pltpu.VMEM((2, 3 * HALF, 2 * HALF), f32),
-            pltpu.VMEM((2, 3 * HALF, 2 * HALF), bf16),
             pltpu.VMEM((2, 3 * HALF, 2 * HALF), bf16),
             pltpu.VMEM((pairs, HALF, PAIR), bf16),
             pltpu.VMEM((pairs, 2, rows, PAIR), bf16),
-            pltpu.SemaphoreType.DMA((2, 4)),
             pltpu.SemaphoreType.DMA((2, 2)),
-        ],
-        cost_estimate=pl.CostEstimate(flops=12 * HALF * 3 * HALF * width, bytes_accessed=16 * rows * width,
+        ]
+    return pl.pallas_call(
+        functools.partial(half_kernel, second=second, front=front, back=back),
+        in_specs=[in_smem, in_hbm, in_hbm, pl.BlockSpec(memory_space=pl.ANY)],
+        out_specs=out_specs,
+        out_shape=out_shape,
+        scratch_shapes=scratch,
+        cost_estimate=pl.CostEstimate(flops=(4 * front + 8 * back) * HALF * 3 * HALF * width, bytes_accessed=16 * rows * width,
                                       transcendentals=HALF * 2 * HALF * width // HEAD_DIM),
         compiler_params=pltpu.CompilerParams(vmem_limit_bytes=24 << 20),
     )(meta, *held, rim)
@@ -374,7 +399,8 @@
         at_y1 = swapped(send1, 2, count)
         at_dp1 = turned(keep1, dp_count)[0]
         at_y_dp1 = turned(at_y1, dp_count)[0]
-    keep2, send2, back2, *own2 = half_attention(meta, thin, thick, second_rim, True)
+    keep2, send2 = half_attention(meta, thin, thick, second_rim, True, back=False)
+    back2, *own2 = half_attention(meta, thin, thick, second_rim, True, front=False)
     if direct:
         at_y2 = swapped(send2, 2, count)
         at_dp2 = turned(keep2, dp_count)[0]

time: 78.4 us -> 93 us (1.19)
  waiting for transfers between devices: 30.6 us -> 46 us
  starting transfers between devices: 24.1 us -> 20.3 us
  Pallas kernels: 21.3 us -> 24.4 us
    ppermute x1, waiting for transfers between devices: 0.01 us -> 17 us  [on_device(): second_rim = lax.ppermute(rim2, 'seq', near_pairs)]
    pallas_call x2 -> x3, Pallas kernels: 10.9 us -> 13.9 us  [half_attention(): pl.pallas_call(functools.partial(half_kernel, second=second, front=front,...]
    ppermute x7, starting transfers between devices: 16.2 us -> 14.2 us  [swapped(): return lax.ppermute(value, 'seq', [(i, i ^ stride) for i in range(count)])]
    ppermute x7, waiting for transfers between devices: 29.6 us -> 27.9 us  [swapped(): return lax.ppermute(value, 'seq', [(i, i ^ stride) for i in range(count)])]
    ppermute x1, starting transfers between devices: 2.72 us -> 1.49 us  [on_device(): second_rim = lax.ppermute(rim2, 'seq', near_pairs)]
  transfers between devices with their start and end apart: 17 -> 17, of which waited for: 7 -> 8; matrix products, arithmetic and copies ran while one was open for 1% -> 1% of each run, Pallas kernels for 27% -> 26%
where the time goes in v5:
time: 93 us; the launch traced here: 92.8 us
  waiting for transfers between devices  46 us (49%)
  Pallas kernels  24.4 us (26%)
  starting transfers between devices  20.3 us (22%)
    ppermute x7, waiting for transfers between devices, swapped(): return lax.ppermute(value, 'seq', [(i, i ^ stride) for i in range(count)])  27.9 us
    ppermute x1, waiting for transfers between devices, on_device(): second_rim = lax.ppermute(rim2, 'seq', near_pairs)  17 us
    ppermute x7, starting transfers between devices, swapped(): return lax.ppermute(value, 'seq', [(i, i ^ stride) for i in range(count)])  14.2 us
    pallas_call x3, Pallas kernels, half_attention(): pl.pallas_call(functools.partial(half_kernel, second=second, front=front,...  13.9 us
    pallas_call x1, Pallas kernels, prepared(): pl.pallas_call(prepare_kernel, in_specs=[in_smem] + [in_vmem] * 5, out_sp...  4.62 us
    ppermute x1, starting transfers between devices, on_device(): from_near = lax.ppermute(back2, 'seq', near_pairs)  2.44 us
    pallas_call x1, Pallas kernels, joined(): pl.pallas_call(join_kernel, in_specs=[in_smem] + [in_vmem] * 6, out_specs...  2.04 us
    pallas_call x1, Pallas kernels, packed_rim(): pl.pallas_call(rim_kernel, grid_spec=pltpu.PrefetchScalarGridSpec(num_sca...  1.92 us
  transfers between devices with their start and end apart: 17, of which 8 were waited for; matrix products, arithmetic and copies ran while one was open for 1% of the time, Pallas kernels for 26%

profile of v5, /device:TPU:0, one launch (start us, length us, event | category | flops | bytes accessed | tf_op | source)
XLA Modules:
  0.0 92.8 jit_solution(2020547153620053108)
XLA Ops:
  0.6 3.1 %collective-permute-start.11 = (bf16[256,1024]{1,0:T(8,128)(2,1)}, bf16[256,1024]{1,0:T(8,128)(2,1)S(1)}, u32[]{:S(2)}, u32[]{:S(2)}) collective-permute-start(bf16[256,1024]{1,0:T(8,128)(2,1)} %bitcast.12), channel_id=1, source_target_pairs={{0,4},{2,6},{4,0},{6,2},{8,12},{10,14},{12,8},{14,10},{16,20},{18,... | collective-permute-start | bytes 1572872 | tf_op jit(solution)/shard_map/ppermute | solution.py:320
  3.7 0.6 stack.28.meta_ref
  4.3 0.0 copy-start
  4.3 0.0 copy-start.5
  4.3 4.6 %prepared.1 = (bf16[8,2,2,128,128]{4,3,2,1,0:T(8,128)(2,1)}, bf16[8,2,2,128,128]{4,3,2,1,0:T(8,128)(2,1)}, bf16[8,2,128,128]{3,2,1,0:T(8,128)(2,1)}) custom-call(s32[7]{0:T(128)} %stack.28.meta_ref, bf16[256,1024]{1,0:T(8,128)(2,1)} %bitcast.20, bf16[256,1024]{1,0:T(8,128)(2,1)} %bitcast.16, bf16[256,1024]{1,0:T(8,128)(2,1)} %bitcast.18, ...), custom_call_target="tpu_custom_call" | custom-call | flops 536870912 | bytes 5767168 | tf_op jit(solution)/shard_map/prepared/pallas_call | solution.py:233
  8.9 1.5 %collective-permute-start.1 = (bf16[8,2,128,128]{3,2,1,0:T(8,128)(2,1)}, bf16[8,2,128,128]{3,2,1,0:T(8,128)(2,1)S(1)}, u32[]{:S(2)}, u32[]{:S(2)}) collective-permute-start(bf16[8,2,128,128]{3,2,1,0:T(8,128)(2,1)} %get-tuple-element.30), channel_id=1, source_target_pairs={{0,2},{2,0},{4,6},{6,4},{8,10},{10,8},{12,14},{14,12},{16,18},{18,... | collective-permute-start | bytes 1572872 | tf_op jit(solution)/shard_map/ppermute | solution.py:390
  10.4 1.9 %shard_map.84 = bf16[8,2,128,128]{3,2,1,0:T(8,128)(2,1)} custom-call(s32[1]{0:T(128)} %bitcast.side_ref, bf16[256,1024]{1,0:T(8,128)(2,1)} %bitcast.17, bf16[256,1024]{1,0:T(8,128)(2,1)} %bitcast.19), custom_call_target="tpu_custom_call" | custom-call | tf_op jit(solution)/shard_map/pallas_call | solution.py:199
  12.3 0.7 collective-permute-start
  13.0 0.0 copy-done
  13.0 0.1 collective-permute-start.10
  13.1 2.7 %collective-permute-done.11.refs_10_ = bf16[256,1024]{1,0:T(8,128)(2,1)S(1)} collective-permute-done((bf16[256,1024]{1,0:T(8,128)(2,1)}, bf16[256,1024]{1,0:T(8,128)(2,1)S(1)}, u32[]{:S(2)}, u32[]{:S(2)}) %collective-permute-start.11) | collective-permute-done | bytes 524320 | tf_op jit(solution)/shard_map/ppermute | solution.py:320
  15.8 0.0 collective-permute-start.12
  15.8 17.0 %collective-permute-done.1.rim_hbm = bf16[8,2,128,128]{3,2,1,0:T(8,128)(2,1)S(1)} collective-permute-done((bf16[8,2,128,128]{3,2,1,0:T(8,128)(2,1)}, bf16[8,2,128,128]{3,2,1,0:T(8,128)(2,1)S(1)}, u32[]{:S(2)}, u32[]{:S(2)}) %collective-permute-start.1) | collective-permute-done | bytes 524320 | tf_op jit(solution)/shard_map/ppermute | solution.py:390
  32.9 0.0 copy-done.5
  32.9 3.2 %shard_map.87 = (bf16[512,128]{1,0:T(8,128)(2,1)S(1)}, bf16[512,128]{1,0:T(8,128)(2,1)S(1)}) custom-call(s32[7]{0:T(128)S(1)} %copy-done.5, bf16[8,2,2,128,128]{4,3,2,1,0:T(8,128)(2,1)} %get-tuple-element.26.thin_hbm, bf16[8,2,2,128,128]{4,3,2,1,0:T(8,128)(2,1)} %get-tuple-element.27.thick_hbm, bf16[8,2,128,128]{3,2,1,0:T(8,128)(2,1)S(1)} %collective-permute-done.1.rim_hbm), custom_call_target="tpu_custom_call" | custom-call | flops 201326592 | bytes 4194304 | tf_op jit(solution)/shard_map/pallas_call | solution.py:176
  36.1 0.1 collective-permute-start.7
  36.2 0.1 collective-permute-start.8
  36.3 5.3 %shard_map.86 = (bf16[8,2,128,128]{3,2,1,0:T(8,128)(2,1)S(1)}, bf16[8,128,128]{2,1,0:T(8,128)(2,1)}, bf16[8,2,256,128]{3,2,1,0:T(8,128)(2,1)}) custom-call(s32[7]{0:T(128)S(1)} %copy-done.5, bf16[8,2,2,128,128]{4,3,2,1,0:T(8,128)(2,1)} %get-tuple-element.26.thin_hbm, bf16[8,2,2,128,128]{4,3,2,1,0:T(8,128)(2,1)} %get-tuple-element.27.thick_hbm, ...), custom_call_target="tpu_custom_call" | custom-call | flops 402653184 | bytes 4194304 | tf_op jit(solution)/shard_map/pallas_call | solution.py:176
  41.5 0.0 collective-permute-done.rim_hbm
  41.5 2.4 %collective-permute-start.3 = (bf16[8,2,128,128]{3,2,1,0:T(8,128)(2,1)S(1)}, bf16[8,2,128,128]{3,2,1,0:T(8,128)(2,1)S(1)}, u32[]{:S(2)}, u32[]{:S(2)}) collective-permute-start(bf16[8,2,128,128]{3,2,1,0:T(8,128)(2,1)S(1)} %get-tuple-element.34), channel_id=1, source_target_pairs={{0,2},{2,0},{4,6},{6,4},{8,10},{10,8},{12,14},{14,12},{16,18},{18,... | collective-permute-start | bytes 1572872 | tf_op jit(solution)/shard_map/ppermute | solution.py:408
  44.0 5.4 %shard_map.85 = (bf16[512,128]{1,0:T(8,128)(2,1)S(1)}, bf16[512,128]{1,0:T(8,128)(2,1)S(1)}, bf16[8,2,128,128]{3,2,1,0:T(8,128)(2,1)S(1)}, bf16[8,128,128]{2,1,0:T(8,128)(2,1)}, bf16[8,2,256,128]{3,2,1,0:T(8,128)(2,1)}) custom-call(s32[7]{0:T(128)S(1)} %copy-done.5, bf16[8,2,2,128,128]{4,3,2,1,0:T(8,128)(2,1)} %get-tuple-element.26.thin_hbm, ...), custom_call_target="tpu_custom_call" | custom-call | flops 603979776 | bytes 4194304 | tf_op jit(solution)/shard_map/pallas_call | solution.py:176
  49.4 0.0 copy-start.1
  49.4 0.0 copy-start.2
  49.4 0.0 copy-start.3
  49.5 0.0 copy-start.4
  49.5 0.0 collective-permute-done.10.refs_9_
  49.5 0.8 collective-permute-start.2
  50.3 0.0 collective-permute-done.7.refs_5_
  50.3 3.2 %collective-permute-start.4 = (bf16[512,128]{1,0:T(8,128)(2,1)S(1)}, bf16[512,128]{1,0:T(8,128)(2,1)S(1)}, u32[]{:S(2)}, u32[]{:S(2)}) collective-permute-start(bf16[512,128]{1,0:T(8,128)(2,1)S(1)} %get-tuple-element.39), channel_id=1, source_target_pairs={{0,4},{2,6},{4,0},{6,2},{8,12},{10,14},{12,8},{14,10},{16,20},{18,... | collective-permute-start | bytes 393224 | tf_op jit(solution)/shard_map/ppermute | solution.py:320
  53.6 0.0 collective-permute-done.8.refs_6_
  53.6 0.0 collective-permute-start.5
  53.6 14.4 %collective-permute-done.4.refs_1_ = bf16[512,128]{1,0:T(8,128)(2,1)S(1)} collective-permute-done((bf16[512,128]{1,0:T(8,128)(2,1)S(1)}, bf16[512,128]{1,0:T(8,128)(2,1)S(1)}, u32[]{:S(2)}, u32[]{:S(2)}) %collective-permute-start.4) | collective-permute-done | bytes 131104 | tf_op jit(solution)/shard_map/ppermute | solution.py:320
  67.9 0.0 collective-permute-start.9
  67.9 0.0 collective-permute-done.5.refs_2_
  67.9 0.5 collective-permute-start.6
  68.5 0.8 collective-permute-done.9.refs_7_
  69.3 0.2 collective-permute-done.6.refs_3_
  69.5 0.0 collective-permute-done.12.refs_11_
  69.5 1.3 %product.1 = (f32[128,512]{1,0:T(8,128)S(1)}, bf16[128,512]{1,0:T(8,128)(2,1)S(1)}, bf16[128,512]{1,0:T(8,128)(2,1)S(1)}, bf16[128,512]{1,0:T(8,128)(2,1)S(1)}) custom-call(s32[7]{0:T(128)S(1)} %copy-done.5, bf16[512,128]{1,0:T(8,128)(2,1)S(1)} %get-tuple-element.38.refs_0_, bf16[512,128]{1,0:T(8,128)(2,1)S(1)} %collective-permute-done.4.refs_1_, ...), custom_call_target="tpu_custom_call" | custom-call | tf_op jit(solution)/shard_map/product/pallas_call | solution.py:262
  70.8 3.4 %collective-permute-start.13 = (bf16[128,512]{1,0:T(8,128)(2,1)S(1)}, bf16[128,512]{1,0:T(8,128)(2,1)S(1)}, u32[]{:S(2)}, u32[]{:S(2)}) collective-permute-start(bf16[128,512]{1,0:T(8,128)(2,1)S(1)} %get-tuple-element.43), channel_id=1, source_target_pairs={{0,8},{2,10},{4,12},{6,14},{8,0},{10,2},{12,4},{14,6},{16,24},{18,... | collective-permute-start | bytes 393224 | tf_op jit(solution)/shard_map/ppermute | solution.py:320
  74.2 2.3 %collective-permute-start.14 = (bf16[128,512]{1,0:T(8,128)(2,1)S(1)}, bf16[128,512]{1,0:T(8,128)(2,1)S(1)}, u32[]{:S(2)}, u32[]{:S(2)}) collective-permute-start(bf16[128,512]{1,0:T(8,128)(2,1)S(1)} %get-tuple-element.44), channel_id=1, source_target_pairs={{0,16},{2,18},{4,20},{6,22},{8,24},{10,26},{12,28},{14,30},{16,0},... | collective-permute-start | bytes 393224 | tf_op jit(solution)/shard_map/ppermute | solution.py:320
  76.6 0.1 collective-permute-start.15
  76.7 3.6 %collective-permute-done.13.refs_0_ = bf16[128,512]{1,0:T(8,128)(2,1)S(1)} collective-permute-done((bf16[128,512]{1,0:T(8,128)(2,1)S(1)}, bf16[128,512]{1,0:T(8,128)(2,1)S(1)}, u32[]{:S(2)}, u32[]{:S(2)}) %collective-permute-start.13) | collective-permute-done | bytes 131104 | tf_op jit(solution)/shard_map/ppermute | solution.py:320
  80.2 6.9 %collective-permute-done.14.refs_1_ = bf16[128,512]{1,0:T(8,128)(2,1)S(1)} collective-permute-done((bf16[128,512]{1,0:T(8,128)(2,1)S(1)}, bf16[128,512]{1,0:T(8,128)(2,1)S(1)}, u32[]{:S(2)}, u32[]{:S(2)}) %collective-permute-start.14) | collective-permute-done | bytes 131104 | tf_op jit(solution)/shard_map/ppermute | solution.py:320
  87.1 0.0 collective-permute-done.15.refs_2_
  87.1 0.6 summed.1
  87.8 1.9 %collective-permute-start.16 = (bf16[64,512]{1,0:T(8,128)(2,1)S(1)}, bf16[64,512]{1,0:T(8,128)(2,1)S(1)}, u32[]{:S(2)}, u32[]{:S(2)}) collective-permute-start(bf16[64,512]{1,0:T(8,128)(2,1)S(1)} %get-tuple-element.47), channel_id=1, source_target_pairs={{0,2},{2,0},{4,6},{6,4},{8,10},{10,8},{12,14},{14,12},{16,18},{18,... | collective-permute-start | bytes 196616 | tf_op jit(solution)/shard_map/ppermute | solution.py:320
  89.7 0.0 collective-permute-done.3.rim2_ref
  89.7 0.0 collective-permute-done.2.rim1_ref
  89.7 0.0 copy-done.1
  89.7 0.0 copy-done.2
  89.7 0.0 copy-done.3
  89.7 0.0 copy-done.4
  89.7 2.0 %joined.1 = (bf16[256,1024]{1,0:T(8,128)(2,1)}, bf16[256,1024]{1,0:T(8,128)(2,1)}, bf16[256,1024]{1,0:T(8,128)(2,1)}) custom-call(s32[7]{0:T(128)S(1)} %copy-done.5, bf16[8,128,128]{2,1,0:T(8,128)(2,1)S(1)} %copy-done.4, bf16[8,2,256,128]{3,2,1,0:T(8,128)(2,1)S(1)} %copy-done.2, bf16[8,128,128]{2,1,0:T(8,128)(2,1)S(1)} %copy-done.3, ...), custom_call_target="tpu_custom_call" | custom-call | tf_op jit(solution)/shard_map/joined/pallas_call | solution.py:309
  91.7 0.3 collective-permute-done.16
  92.1 0.7 add_multiply_fusion
Async XLA Ops:
  0.6 15.2 %collective-permute-start.11 = (bf16[256,1024]{1,0:T(8,128)(2,1)}, bf16[256,1024]{1,0:T(8,128)(2,1)S(1)}, u32[]{:S(2)}, u32[]{:S(2)}) collective-permute-start(bf16[256,1024]{1,0:T(8,128)(2,1)} %bitcast.12), channel_id=1, source_target_pairs={{0,4},{2,6},{4,0},{6,2},{8,12},{10,14},{12,8},{14,10},{16,20},{18,... | collective-permute-start | bytes 1572872 | tf_op jit(solution)/shard_map/ppermute | solution.py:320
  4.3 8.7 %copy-start = (bf16[1,256,1024]{2,1,0:T(8,128)(2,1)S(1)}, bf16[1,256,1024]{2,1,0:T(8,128)(2,1)}, u32[]{:S(2)}) copy-start(bf16[1,256,1024]{2,1,0:T(8,128)(2,1)} %param.8) | copy-start | bytes 1572868
  4.3 28.6 %copy-start.5 = (s32[7]{0:T(128)S(1)}, s32[7]{0:T(128)}, u32[]{:S(2)}) copy-start(s32[7]{0:T(128)} %stack.28.meta_ref) | copy-start | bytes 88
  8.9 23.9 %collective-permute-start.1 = (bf16[8,2,128,128]{3,2,1,0:T(8,128)(2,1)}, bf16[8,2,128,128]{3,2,1,0:T(8,128)(2,1)S(1)}, u32[]{:S(2)}, u32[]{:S(2)}) collective-permute-start(bf16[8,2,128,128]{3,2,1,0:T(8,128)(2,1)} %get-tuple-element.30), channel_id=1, source_target_pairs={{0,2},{2,0},{4,6},{6,4},{8,10},{10,8},{12,14},{14,12},{16,18},{18,... | collective-permute-start | bytes 1572872 | tf_op jit(solution)/shard_map/ppermute | solution.py:390
  12.3 29.2 %collective-permute-start = (bf16[8,2,128,128]{3,2,1,0:T(8,128)(2,1)}, bf16[8,2,128,128]{3,2,1,0:T(8,128)(2,1)S(1)}, u32[]{:S(2)}, u32[]{:S(2)}) collective-permute-start(bf16[8,2,128,128]{3,2,1,0:T(8,128)(2,1)} %shard_map.84), channel_id=1, source_target_pairs={{2,4},{4,2},{6,8},{8,6},{10,12},{12,10},{14,16},{16,14},{18,20},{2... | collective-permute-start | bytes 1572872 | tf_op jit(solution)/shard_map/ppermute | solution.py:386
  13.0 36.5 %collective-permute-start.10 = (bf16[256,1024]{1,0:T(8,128)(2,1)S(1)}, bf16[256,1024]{1,0:T(8,128)(2,1)S(1)}, u32[]{:S(2)}, u32[]{:S(2)}) collective-permute-start(bf16[256,1024]{1,0:T(8,128)(2,1)S(1)} %bitcast.14), channel_id=1, source_target_pairs={{0,1},{1,0},{2,3},{3,2},{4,5},{5,4},{6,7},{7,6},{8,9},{9,8},{10,11... | collective-permute-start | bytes 1572872 | tf_op jit(solution)/shard_map/ppermute | solution.py:324
  15.8 53.7 %collective-permute-start.12 = (bf16[256,1024]{1,0:T(8,128)(2,1)S(1)}, bf16[256,1024]{1,0:T(8,128)(2,1)S(1)}, u32[]{:S(2)}, u32[]{:S(2)}) collective-permute-start(bf16[256,1024]{1,0:T(8,128)(2,1)S(1)} %collective-permute-done.11.refs_10_), channel_id=1, source_target_pairs={{0,1},{1,0},{2,3},{3,2},{4,5},{5,4},{6,7},{7,6},{8,9},{9,8},{10,11... | collective-permute-start | bytes 1572872 | tf_op jit(solution)/shard_map/ppermute | solution.py:324
  36.1 14.2 %collective-permute-start.7 = (bf16[512,128]{1,0:T(8,128)(2,1)S(1)}, bf16[512,128]{1,0:T(8,128)(2,1)S(1)}, u32[]{:S(2)}, u32[]{:S(2)}) collective-permute-start(bf16[512,128]{1,0:T(8,128)(2,1)S(1)} %get-tuple-element.41), channel_id=1, source_target_pairs={{0,4},{2,6},{4,0},{6,2},{8,12},{10,14},{12,8},{14,10},{16,20},{18,... | collective-permute-start | bytes 393224 | tf_op jit(solution)/shard_map/ppermute | solution.py:320
  36.2 17.4 %collective-permute-start.8 = (bf16[512,128]{1,0:T(8,128)(2,1)S(1)}, bf16[512,128]{1,0:T(8,128)(2,1)S(1)}, u32[]{:S(2)}, u32[]{:S(2)}) collective-permute-start(bf16[512,128]{1,0:T(8,128)(2,1)S(1)} %get-tuple-element.40.refs_4_), channel_id=1, source_target_pairs={{0,1},{1,0},{2,3},{3,2},{4,5},{5,4},{6,7},{7,6},{8,9},{9,8},{10,11... | collective-permute-start | bytes 393224 | tf_op jit(solution)/shard_map/ppermute | solution.py:324
  41.5 48.1 %collective-permute-start.3 = (bf16[8,2,128,128]{3,2,1,0:T(8,128)(2,1)S(1)}, bf16[8,2,128,128]{3,2,1,0:T(8,128)(2,1)S(1)}, u32[]{:S(2)}, u32[]{:S(2)}) collective-permute-start(bf16[8,2,128,128]{3,2,1,0:T(8,128)(2,1)S(1)} %get-tuple-element.34), channel_id=1, source_target_pairs={{0,2},{2,0},{4,6},{6,4},{8,10},{10,8},{12,14},{14,12},{16,18},{18,... | collective-permute-start | bytes 1572872 | tf_op jit(solution)/shard_map/ppermute | solution.py:408
  49.4 40.2 %copy-start.1 = (bf16[8,2,256,128]{3,2,1,0:T(8,128)(2,1)S(1)}, bf16[8,2,256,128]{3,2,1,0:T(8,128)(2,1)}, u32[]{:S(2)}) copy-start(bf16[8,2,256,128]{3,2,1,0:T(8,128)(2,1)} %get-tuple-element.32.own2_ref) | copy-start | bytes 3145732
  49.4 40.2 %copy-start.2 = (bf16[8,2,256,128]{3,2,1,0:T(8,128)(2,1)S(1)}, bf16[8,2,256,128]{3,2,1,0:T(8,128)(2,1)}, u32[]{:S(2)}) copy-start(bf16[8,2,256,128]{3,2,1,0:T(8,128)(2,1)} %get-tuple-element.29.own1_ref) | copy-start | bytes 3145732
  49.4 40.2 %copy-start.3 = (bf16[8,128,128]{2,1,0:T(8,128)(2,1)S(1)}, bf16[8,128,128]{2,1,0:T(8,128)(2,1)}, u32[]{:S(2)}) copy-start(bf16[8,128,128]{2,1,0:T(8,128)(2,1)} %get-tuple-element.31.dq2_ref) | copy-start | bytes 786436
  49.5 40.2 %copy-start.4 = (bf16[8,128,128]{2,1,0:T(8,128)(2,1)S(1)}, bf16[8,128,128]{2,1,0:T(8,128)(2,1)}, u32[]{:S(2)}) copy-start(bf16[8,128,128]{2,1,0:T(8,128)(2,1)} %get-tuple-element.28.dq1_ref) | copy-start | bytes 786436
  49.5 40.2 %collective-permute-start.2 = (bf16[8,2,128,128]{3,2,1,0:T(8,128)(2,1)S(1)}, bf16[8,2,128,128]{3,2,1,0:T(8,128)(2,1)S(1)}, u32[]{:S(2)}, u32[]{:S(2)}) collective-permute-start(bf16[8,2,128,128]{3,2,1,0:T(8,128)(2,1)S(1)} %get-tuple-element.33), channel_id=1, source_target_pairs={{2,4},{4,2},{6,8},{8,6},{10,12},{12,10},{14,16},{16,14},{18,20},{2... | collective-permute-start | bytes 1572872 | tf_op jit(solution)/shard_map/ppermute | solution.py:397
  50.3 17.6 %collective-permute-start.4 = (bf16[512,128]{1,0:T(8,128)(2,1)S(1)}, bf16[512,128]{1,0:T(8,128)(2,1)S(1)}, u32[]{:S(2)}, u32[]{:S(2)}) collective-permute-start(bf16[512,128]{1,0:T(8,128)(2,1)S(1)} %get-tuple-element.39), channel_id=1, source_target_pairs={{0,4},{2,6},{4,0},{6,2},{8,12},{10,14},{12,8},{14,10},{16,20},{18,... | collective-permute-start | bytes 393224 | tf_op jit(solution)/shard_map/ppermute | solution.py:320
  53.6 14.4 %collective-permute-start.5 = (bf16[512,128]{1,0:T(8,128)(2,1)S(1)}, bf16[512,128]{1,0:T(8,128)(2,1)S(1)}, u32[]{:S(2)}, u32[]{:S(2)}) collective-permute-start(bf16[512,128]{1,0:T(8,128)(2,1)S(1)} %get-tuple-element.38.refs_0_), channel_id=1, source_target_pairs={{0,1},{1,0},{2,3},{3,2},{4,5},{5,4},{6,7},{7,6},{8,9},{9,8},{10,11... | collective-permute-start | bytes 393224 | tf_op jit(solution)/shard_map/ppermute | solution.py:324
  67.9 1.3 %collective-permute-start.9 = (bf16[512,128]{1,0:T(8,128)(2,1)S(1)}, bf16[512,128]{1,0:T(8,128)(2,1)S(1)}, u32[]{:S(2)}, u32[]{:S(2)}) collective-permute-start(bf16[512,128]{1,0:T(8,128)(2,1)S(1)} %collective-permute-done.7.refs_5_), channel_id=1, source_target_pairs={{0,1},{1,0},{2,3},{3,2},{4,5},{5,4},{6,7},{7,6},{8,9},{9,8},{10,11... | collective-permute-start | bytes 393224 | tf_op jit(solution)/shard_map/ppermute | solution.py:324
  67.9 1.5 %collective-permute-start.6 = (bf16[512,128]{1,0:T(8,128)(2,1)S(1)}, bf16[512,128]{1,0:T(8,128)(2,1)S(1)}, u32[]{:S(2)}, u32[]{:S(2)}) collective-permute-start(bf16[512,128]{1,0:T(8,128)(2,1)S(1)} %collective-permute-done.4.refs_1_), channel_id=1, source_target_pairs={{0,1},{1,0},{2,3},{3,2},{4,5},{5,4},{6,7},{7,6},{8,9},{9,8},{10,11... | collective-permute-start | bytes 393224 | tf_op jit(solution)/shard_map/ppermute | solution.py:324
  70.8 9.5 %collective-permute-start.13 = (bf16[128,512]{1,0:T(8,128)(2,1)S(1)}, bf16[128,512]{1,0:T(8,128)(2,1)S(1)}, u32[]{:S(2)}, u32[]{:S(2)}) collective-permute-start(bf16[128,512]{1,0:T(8,128)(2,1)S(1)} %get-tuple-element.43), channel_id=1, source_target_pairs={{0,8},{2,10},{4,12},{6,14},{8,0},{10,2},{12,4},{14,6},{16,24},{18,... | collective-permute-start | bytes 393224 | tf_op jit(solution)/shard_map/ppermute | solution.py:320
  74.2 12.9 %collective-permute-start.14 = (bf16[128,512]{1,0:T(8,128)(2,1)S(1)}, bf16[128,512]{1,0:T(8,128)(2,1)S(1)}, u32[]{:S(2)}, u32[]{:S(2)}) collective-permute-start(bf16[128,512]{1,0:T(8,128)(2,1)S(1)} %get-tuple-element.44), channel_id=1, source_target_pairs={{0,16},{2,18},{4,20},{6,22},{8,24},{10,26},{12,28},{14,30},{16,0},... | collective-permute-start | bytes 393224 | tf_op jit(solution)/shard_map/ppermute | solution.py:320
  76.6 10.6 %collective-permute-start.15 = (bf16[128,512]{1,0:T(8,128)(2,1)S(1)}, bf16[128,512]{1,0:T(8,128)(2,1)S(1)}, u32[]{:S(2)}, u32[]{:S(2)}) collective-permute-start(bf16[128,512]{1,0:T(8,128)(2,1)S(1)} %get-tuple-element.45), channel_id=1, source_target_pairs={{0,24},{2,26},{4,28},{6,30},{8,16},{10,18},{12,20},{14,22},{16,8},... | collective-permute-start | bytes 393224 | tf_op jit(solution)/shard_map/ppermute | solution.py:320
  87.8 4.3 %collective-permute-start.16 = (bf16[64,512]{1,0:T(8,128)(2,1)S(1)}, bf16[64,512]{1,0:T(8,128)(2,1)S(1)}, u32[]{:S(2)}, u32[]{:S(2)}) collective-permute-start(bf16[64,512]{1,0:T(8,128)(2,1)S(1)} %get-tuple-element.47), channel_id=1, source_target_pairs={{0,2},{2,0},{4,6},{6,4},{8,10},{10,8},{12,14},{14,12},{16,18},{18,... | collective-permute-start | bytes 196616 | tf_op jit(solution)/shard_map/ppermute | solution.py:320

commit v6 on v5

--- a/solution.py
+++ b/solution.py
@@ -292,28 +292,63 @@
     )(meta, own, *pieces)
 
 
-def join_kernel(meta_ref, dq1_ref, own1_ref, dq2_ref, own2_ref, rim1_ref, rim2_ref, dq_out, dk_out, dv_out):
+def join_kernel(meta_ref, dq1_ref, own1_ref, dq2_ref, own2_ref, rim_ref, dq_out, dk_out, dv_out):
     side = meta_ref[0]
-    for row, rim, dq_ref in ((side, rim1_ref, dq1_ref), (1 - side, rim2_ref, dq2_ref)):
+    for row, rim, dq_ref in ((side, rim_ref, dq1_ref), (1 - side, None, dq2_ref)):
         rows = pl.ds(pl.multiple_of(row * HALF, HALF), HALF)
         for pair in range(dq1_ref.shape[0]):
             cols = slice(pair * PAIR, (pair + 1) * PAIR)
             dq_out[rows, cols] = dq_ref[pair]
             for which, out in enumerate((dk_out, dv_out)):
                 total = own1_ref[pair, which, rows].astype(f32) + own2_ref[pair, which, rows].astype(f32)
-                out[rows, cols] = (total + rim[pair, which].astype(f32)).astype(bf16)
-
-
-def joined(meta, own1, own2, rim1, rim2, shape):
+                if rim is not None:
+                    total = total + rim[pair, which].astype(f32)
+                out[rows, cols] = total.astype(bf16)
+
+
+def joined(meta, own1, own2, rim, shape):
     out = jax.ShapeDtypeStruct(shape, bf16)
     return pl.pallas_call(
         join_kernel,
-        in_specs=[in_smem] + [in_vmem] * 6,
+        in_specs=[in_smem] + [in_vmem] * 5,
         out_specs=[in_vmem] * 3,
         out_shape=[out] * 3,
+        cost_estimate=pl.CostEstimate(flops=6 * shape[0] * shape[1], bytes_accessed=16 * shape[0] * shape[1], transcendentals=0),
+        name="joined",
+    )(meta, *own1, *own2, rim)
+
+
+def finish_kernel(meta_ref, dk_hbm, dv_hbm, rim_ref, dk_out, dv_out, rows_ref, in_sem, out_sem):
+    rows = pl.ds(pl.multiple_of((1 - meta_ref[0]) * HALF, HALF), HALF)
+    loads = [pltpu.make_async_copy(ref.at[rows, :], rows_ref.at[which], in_sem.at[which]) for which, ref in enumerate((dk_hbm, dv_hbm))]
+    saves = [pltpu.make_async_copy(rows_ref.at[which], ref.at[rows, :], out_sem.at[which]) for which, ref in enumerate((dk_out, dv_out))]
+    for load in loads:
+        load.start()
+    for which in range(2):
+        loads[which].wait()
+        for pair in range(rim_ref.shape[0]):
+            cols = slice(pair * PAIR, (pair + 1) * PAIR)
+            total = rows_ref[which, :, cols].astype(f32) + rim_ref[pair, which].astype(f32)
+            rows_ref[which, :, cols] = total.astype(bf16)
+        saves[which].start()
+    for save in saves:
+        save.wait()
+
+
+def finished(meta, dk, dv, rim):
+    in_hbm = pl.BlockSpec(memory_space=pltpu.HBM)
+    out = jax.ShapeDtypeStruct(dk.shape, bf16)
+    return pl.pallas_call(
+        finish_kernel,
+        in_specs=[in_smem, in_hbm, in_hbm, in_vmem],
+        out_specs=[in_hbm] * 2,
+        out_shape=[out] * 2,
+        scratch_shapes=[pltpu.VMEM((2, HALF, dk.shape[1]), bf16), pltpu.SemaphoreType.DMA((2,)), pltpu.SemaphoreType.DMA((2,))],
+        input_output_aliases={1: 0, 2: 1},
+        cost_estimate=pl.CostEstimate(flops=2 * HALF * dk.shape[1], bytes_accessed=12 * HALF * dk.shape[1], transcendentals=0),
         compiler_params=pltpu.CompilerParams(vmem_limit_bytes=12 << 20),
-        name="joined",
-    )(meta, *own1, *own2, rim1, rim2)
+        name="finished",
+    )(meta, pltpu.with_memory_space_constraint(dk, pltpu.HBM), pltpu.with_memory_space_constraint(dv, pltpu.HBM), rim)
 
 
 def swapped(value, stride, count):
@@ -418,7 +453,8 @@
         wo_grad = kept + swapped(sent, 1, count).astype(f32)
     else:
         wo_grad = general_sum((keep1, send1), (keep2, send2), g, sides, place, mine, y_digit, count, dp_count)
-    dq, dk, dv = joined(meta, own1, own2, from_long, from_near, q.shape)
+    dq, dk, dv = joined(meta, own1, own2, from_long, q.shape)
+    dk, dv = finished(meta, dk, dv, from_near)
     return dq[None], dk[None], dv[None], wo_grad * frames ** -0.5
 
 

time: 93 us -> 90.5 us (0.973)
  waiting for transfers between devices: 46 us -> 37.4 us
  Pallas kernels: 24.4 us -> 28.1 us
  starting transfers between devices: 20.3 us -> 21.4 us
    ppermute x7, waiting for transfers between devices: 27.9 us -> 19.2 us  [swapped(): return lax.ppermute(value, 'seq', [(i, i ^ stride) for i in range(count)])]
    pallas_call x1 -> x2, Pallas kernels: 2.04 us -> 5.72 us  [the longest x1 3.32 us: joined(): pl.pallas_call(join_kernel, in_specs=[in_smem] + [in_vmem] * 5, out_specs...]
    ppermute x1, starting transfers between devices: 2.44 us -> 4.67 us  [on_device(): from_near = lax.ppermute(back2, 'seq', near_pairs)]
    ppermute x7, starting transfers between devices: 14.2 us -> 13.2 us  [swapped(): return lax.ppermute(value, 'seq', [(i, i ^ stride) for i in range(count)])]
  transfers between devices with their start and end apart: 17 -> 17, of which waited for: 8 -> 7; matrix products, arithmetic and copies ran while one was open for 1% -> 1% of each run, Pallas kernels for 26% -> 31%
where the time goes in v6:
time: 90.5 us; the launch traced here: 89.8 us
  waiting for transfers between devices  37.4 us (41%)
  Pallas kernels  28.1 us (31%)
  starting transfers between devices  21.4 us (24%)
  local copies, waits for them, and re-layouts  1.49 us (2%)
    ppermute x7, waiting for transfers between devices, swapped(): return lax.ppermute(value, 'seq', [(i, i ^ stride) for i in range(count)])  19.2 us
    ppermute x1, waiting for transfers between devices, on_device(): second_rim = lax.ppermute(rim2, 'seq', near_pairs)  17.1 us
    pallas_call x3, Pallas kernels, half_attention(): pl.pallas_call(functools.partial(half_kernel, second=second, front=front,...  14 us
    ppermute x7, starting transfers between devices, swapped(): return lax.ppermute(value, 'seq', [(i, i ^ stride) for i in range(count)])  13.2 us
    ppermute x1, starting transfers between devices, on_device(): from_near = lax.ppermute(back2, 'seq', near_pairs)  4.67 us
    pallas_call x1, Pallas kernels, prepared(): pl.pallas_call(prepare_kernel, in_specs=[in_smem] + [in_vmem] * 5, out_sp...  4.62 us
    pallas_call x1, Pallas kernels, joined(): pl.pallas_call(join_kernel, in_specs=[in_smem] + [in_vmem] * 5, out_specs...  3.32 us
    pallas_call x1, Pallas kernels, finished(): pl.pallas_call(finish_kernel, in_specs=[in_smem, in_hbm, in_hbm, in_vmem]...  2.4 us
  transfers between devices with their start and end apart: 17, of which 7 were waited for; matrix products, arithmetic and copies ran while one was open for 1% of the time, Pallas kernels for 31%

profile of v6, /device:TPU:0, one launch (start us, length us, event | category | flops | bytes accessed | tf_op | source)
XLA Modules:
  0.0 89.8 jit_solution(6029100395080178990)
XLA Ops:
  0.6 3.1 %collective-permute-start.11 = (bf16[256,1024]{1,0:T(8,128)(2,1)}, bf16[256,1024]{1,0:T(8,128)(2,1)S(1)}, u32[]{:S(2)}, u32[]{:S(2)}) collective-permute-start(bf16[256,1024]{1,0:T(8,128)(2,1)} %bitcast.12), channel_id=1, source_target_pairs={{0,4},{2,6},{4,0},{6,2},{8,12},{10,14},{12,8},{14,10},{16,20},{18,... | collective-permute-start | bytes 1572872 | tf_op jit(solution)/shard_map/ppermute | solution.py:355
  3.7 0.7 stack.28.meta_ref
  4.4 0.0 copy-start
  4.4 0.0 copy-start.1
  4.4 4.6 %prepared.1 = (bf16[8,2,2,128,128]{4,3,2,1,0:T(8,128)(2,1)}, bf16[8,2,2,128,128]{4,3,2,1,0:T(8,128)(2,1)}, bf16[8,2,128,128]{3,2,1,0:T(8,128)(2,1)}) custom-call(s32[7]{0:T(128)} %stack.28.meta_ref, bf16[256,1024]{1,0:T(8,128)(2,1)} %bitcast.20, bf16[256,1024]{1,0:T(8,128)(2,1)} %bitcast.16, bf16[256,1024]{1,0:T(8,128)(2,1)} %bitcast.18, ...), custom_call_target="tpu_custom_call" | custom-call | flops 536870912 | bytes 5767168 | tf_op jit(solution)/shard_map/prepared/pallas_call | solution.py:233
  9.0 1.5 %collective-permute-start.1 = (bf16[8,2,128,128]{3,2,1,0:T(8,128)(2,1)}, bf16[8,2,128,128]{3,2,1,0:T(8,128)(2,1)S(1)}, u32[]{:S(2)}, u32[]{:S(2)}) collective-permute-start(bf16[8,2,128,128]{3,2,1,0:T(8,128)(2,1)} %get-tuple-element.32), channel_id=1, source_target_pairs={{0,2},{2,0},{4,6},{6,4},{8,10},{10,8},{12,14},{14,12},{16,18},{18,... | collective-permute-start | bytes 1572872 | tf_op jit(solution)/shard_map/ppermute | solution.py:425
  10.5 1.9 %shard_map.84 = bf16[8,2,128,128]{3,2,1,0:T(8,128)(2,1)} custom-call(s32[1]{0:T(128)} %bitcast.side_ref, bf16[256,1024]{1,0:T(8,128)(2,1)} %bitcast.17, bf16[256,1024]{1,0:T(8,128)(2,1)} %bitcast.19), custom_call_target="tpu_custom_call" | custom-call | tf_op jit(solution)/shard_map/pallas_call | solution.py:199
  12.4 0.7 collective-permute-start
  13.1 0.0 copy-done
  13.1 0.1 collective-permute-start.10
  13.2 2.7 %collective-permute-done.11.refs_10_ = bf16[256,1024]{1,0:T(8,128)(2,1)S(1)} collective-permute-done((bf16[256,1024]{1,0:T(8,128)(2,1)}, bf16[256,1024]{1,0:T(8,128)(2,1)S(1)}, u32[]{:S(2)}, u32[]{:S(2)}) %collective-permute-start.11) | collective-permute-done | bytes 524320 | tf_op jit(solution)/shard_map/ppermute | solution.py:355
  15.8 0.0 collective-permute-start.12
  15.8 17.1 %collective-permute-done.1.rim_hbm = bf16[8,2,128,128]{3,2,1,0:T(8,128)(2,1)S(1)} collective-permute-done((bf16[8,2,128,128]{3,2,1,0:T(8,128)(2,1)}, bf16[8,2,128,128]{3,2,1,0:T(8,128)(2,1)S(1)}, u32[]{:S(2)}, u32[]{:S(2)}) %collective-permute-start.1) | collective-permute-done | bytes 524320 | tf_op jit(solution)/shard_map/ppermute | solution.py:425
  32.9 0.0 copy-done.1
  32.9 3.2 %shard_map.87 = (bf16[512,128]{1,0:T(8,128)(2,1)S(1)}, bf16[512,128]{1,0:T(8,128)(2,1)S(1)}) custom-call(s32[7]{0:T(128)S(1)} %copy-done.1, bf16[8,2,2,128,128]{4,3,2,1,0:T(8,128)(2,1)} %get-tuple-element.28.thin_hbm, bf16[8,2,2,128,128]{4,3,2,1,0:T(8,128)(2,1)} %get-tuple-element.29.thick_hbm, bf16[8,2,128,128]{3,2,1,0:T(8,128)(2,1)S(1)} %collective-permute-done.1.rim_hbm), custom_call_target="tpu_custom_call" | custom-call | flops 201326592 | bytes 4194304 | tf_op jit(solution)/shard_map/pallas_call | solution.py:176
  36.2 0.1 collective-permute-start.7
  36.3 0.1 collective-permute-start.8
  36.3 0.0 collective-permute-done.rim_hbm
  36.3 5.5 %shard_map.85 = (bf16[512,128]{1,0:T(8,128)(2,1)S(1)}, bf16[512,128]{1,0:T(8,128)(2,1)S(1)}, bf16[8,2,128,128]{3,2,1,0:T(8,128)(2,1)S(1)}, bf16[8,128,128]{2,1,0:T(8,128)(2,1)}, bf16[8,2,256,128]{3,2,1,0:T(8,128)(2,1)}) custom-call(s32[7]{0:T(128)S(1)} %copy-done.1, bf16[8,2,2,128,128]{4,3,2,1,0:T(8,128)(2,1)} %get-tuple-element.28.thin_hbm, ...), custom_call_target="tpu_custom_call" | custom-call | flops 603979776 | bytes 4194304 | tf_op jit(solution)/shard_map/pallas_call | solution.py:176
  41.8 0.7 collective-permute-start.2
  42.5 5.3 %shard_map.86 = (bf16[8,2,128,128]{3,2,1,0:T(8,128)(2,1)S(1)}, bf16[8,128,128]{2,1,0:T(8,128)(2,1)}, bf16[8,2,256,128]{3,2,1,0:T(8,128)(2,1)}) custom-call(s32[7]{0:T(128)S(1)} %copy-done.1, bf16[8,2,2,128,128]{4,3,2,1,0:T(8,128)(2,1)} %get-tuple-element.28.thin_hbm, bf16[8,2,2,128,128]{4,3,2,1,0:T(8,128)(2,1)} %get-tuple-element.29.thick_hbm, ...), custom_call_target="tpu_custom_call" | custom-call | flops 402653184 | bytes 4194304 | tf_op jit(solution)/shard_map/pallas_call | solution.py:176
  47.8 0.0 collective-permute-done.10.refs_9_
  47.8 4.7 %collective-permute-start.3 = (bf16[8,2,128,128]{3,2,1,0:T(8,128)(2,1)S(1)}, bf16[8,2,128,128]{3,2,1,0:T(8,128)(2,1)S(1)}, u32[]{:S(2)}, u32[]{:S(2)}) collective-permute-start(bf16[8,2,128,128]{3,2,1,0:T(8,128)(2,1)S(1)} %get-tuple-element.39), channel_id=1, source_target_pairs={{0,2},{2,0},{4,6},{6,4},{8,10},{10,8},{12,14},{14,12},{16,18},{18,... | collective-permute-start | bytes 1572872 | tf_op jit(solution)/shard_map/ppermute | solution.py:443
  52.5 0.0 collective-permute-done.7.refs_5_
  52.5 2.4 %collective-permute-start.4 = (bf16[512,128]{1,0:T(8,128)(2,1)S(1)}, bf16[512,128]{1,0:T(8,128)(2,1)S(1)}, u32[]{:S(2)}, u32[]{:S(2)}) collective-permute-start(bf16[512,128]{1,0:T(8,128)(2,1)S(1)} %get-tuple-element.43), channel_id=1, source_target_pairs={{0,4},{2,6},{4,0},{6,2},{8,12},{10,14},{12,8},{14,10},{16,20},{18,... | collective-permute-start | bytes 393224 | tf_op jit(solution)/shard_map/ppermute | solution.py:355
  54.9 0.0 collective-permute-done.8.refs_6_
  54.9 0.0 collective-permute-start.5
  54.9 6.3 %collective-permute-done.4.refs_1_ = bf16[512,128]{1,0:T(8,128)(2,1)S(1)} collective-permute-done((bf16[512,128]{1,0:T(8,128)(2,1)S(1)}, bf16[512,128]{1,0:T(8,128)(2,1)S(1)}, u32[]{:S(2)}, u32[]{:S(2)}) %collective-permute-start.4) | collective-permute-done | bytes 131104 | tf_op jit(solution)/shard_map/ppermute | solution.py:355
  61.2 0.0 collective-permute-start.9
  61.2 0.0 collective-permute-done.5.refs_2_
  61.2 0.5 collective-permute-start.6
  61.7 0.8 collective-permute-done.9.refs_7_
  62.5 0.2 collective-permute-done.6.refs_3_
  62.7 0.0 collective-permute-done.12.refs_11_
  62.7 1.3 %product.1 = (f32[128,512]{1,0:T(8,128)S(1)}, bf16[128,512]{1,0:T(8,128)(2,1)S(1)}, bf16[128,512]{1,0:T(8,128)(2,1)S(1)}, bf16[128,512]{1,0:T(8,128)(2,1)S(1)}) custom-call(s32[7]{0:T(128)S(1)} %copy-done.1, bf16[512,128]{1,0:T(8,128)(2,1)S(1)} %get-tuple-element.42.refs_0_, bf16[512,128]{1,0:T(8,128)(2,1)S(1)} %collective-permute-done.4.refs_1_, ...), custom_call_target="tpu_custom_call" | custom-call | tf_op jit(solution)/shard_map/product/pallas_call | solution.py:262
  64.0 0.0 copy-start.2
  64.0 4.4 %collective-permute-start.13 = (bf16[128,512]{1,0:T(8,128)(2,1)S(1)}, bf16[128,512]{1,0:T(8,128)(2,1)S(1)}, u32[]{:S(2)}, u32[]{:S(2)}) collective-permute-start(bf16[128,512]{1,0:T(8,128)(2,1)S(1)} %get-tuple-element.47), channel_id=1, source_target_pairs={{0,8},{2,10},{4,12},{6,14},{8,0},{10,2},{12,4},{14,6},{16,24},{18,... | collective-permute-start | bytes 393224 | tf_op jit(solution)/shard_map/ppermute | solution.py:355
  68.4 2.7 %collective-permute-start.14 = (bf16[128,512]{1,0:T(8,128)(2,1)S(1)}, bf16[128,512]{1,0:T(8,128)(2,1)S(1)}, u32[]{:S(2)}, u32[]{:S(2)}) collective-permute-start(bf16[128,512]{1,0:T(8,128)(2,1)S(1)} %get-tuple-element.48), channel_id=1, source_target_pairs={{0,16},{2,18},{4,20},{6,22},{8,24},{10,26},{12,28},{14,30},{16,0},... | collective-permute-start | bytes 393224 | tf_op jit(solution)/shard_map/ppermute | solution.py:355
  71.1 0.0 collective-permute-start.15
  71.1 3.4 %collective-permute-done.13.refs_0_ = bf16[128,512]{1,0:T(8,128)(2,1)S(1)} collective-permute-done((bf16[128,512]{1,0:T(8,128)(2,1)S(1)}, bf16[128,512]{1,0:T(8,128)(2,1)S(1)}, u32[]{:S(2)}, u32[]{:S(2)}) %collective-permute-start.13) | collective-permute-done | bytes 131104 | tf_op jit(solution)/shard_map/ppermute | solution.py:355
  74.5 6.9 %collective-permute-done.14.refs_1_ = bf16[128,512]{1,0:T(8,128)(2,1)S(1)} collective-permute-done((bf16[128,512]{1,0:T(8,128)(2,1)S(1)}, bf16[128,512]{1,0:T(8,128)(2,1)S(1)}, u32[]{:S(2)}, u32[]{:S(2)}) %collective-permute-start.14) | collective-permute-done | bytes 131104 | tf_op jit(solution)/shard_map/ppermute | solution.py:355
  81.4 0.0 collective-permute-done.15.refs_2_
  81.4 0.6 summed.1
  82.0 0.6 collective-permute-start.16
  82.6 0.0 collective-permute-done.2.rim_ref
  82.6 0.0 copy-start.3
  82.6 0.8 copy-done.3
  83.4 3.3 %joined.1 = (bf16[256,1024]{1,0:T(8,128)(2,1)}, bf16[256,1024]{1,0:T(8,128)(2,1)}, bf16[256,1024]{1,0:T(8,128)(2,1)}) custom-call(s32[7]{0:T(128)} %stack.28.meta_ref, bf16[8,128,128]{2,1,0:T(8,128)(2,1)} %get-tuple-element.30.dq1_ref, bf16[8,2,256,128]{3,2,1,0:T(8,128)(2,1)} %get-tuple-element.31.own1_ref, bf16[8,128,128]{2,1,0:T(8,128)(2,1)} %get-tuple-element.33.dq2_ref, ...), custom_call_target="tpu_custom_call" | custom-call | flops 1572864 | bytes 4194304 | tf_op jit(solution)/shard_map/joined/pallas_call | solution.py:311
  86.8 0.0 collective-permute-done.3.rim_ref
  86.8 0.0 copy-done.2
  86.8 2.4 %finished.1 = (bf16[256,1024]{1,0:T(8,128)(2,1)}, bf16[256,1024]{1,0:T(8,128)(2,1)}) custom-call(s32[7]{0:T(128)S(1)} %copy-done.2, bf16[256,1024]{1,0:T(8,128)(2,1)} %get-tuple-element.37.dk_hbm, bf16[256,1024]{1,0:T(8,128)(2,1)} %get-tuple-element.38.dv_hbm, ...), custom_call_target="tpu_custom_call", output_to_operand_aliasing={{0}: (1, {}), {1}: (2, {})} | custom-call | flops 262144 | bytes 1572864 | tf_op jit(solution)/shard_map/finished/pallas_call | solution.py:341
  89.2 0.0 collective-permute-done.16
  89.2 0.7 add_multiply_fusion
Async XLA Ops:
  0.6 15.2 %collective-permute-start.11 = (bf16[256,1024]{1,0:T(8,128)(2,1)}, bf16[256,1024]{1,0:T(8,128)(2,1)S(1)}, u32[]{:S(2)}, u32[]{:S(2)}) collective-permute-start(bf16[256,1024]{1,0:T(8,128)(2,1)} %bitcast.12), channel_id=1, source_target_pairs={{0,4},{2,6},{4,0},{6,2},{8,12},{10,14},{12,8},{14,10},{16,20},{18,... | collective-permute-start | bytes 1572872 | tf_op jit(solution)/shard_map/ppermute | solution.py:355
  4.4 8.7 %copy-start = (bf16[1,256,1024]{2,1,0:T(8,128)(2,1)S(1)}, bf16[1,256,1024]{2,1,0:T(8,128)(2,1)}, u32[]{:S(2)}) copy-start(bf16[1,256,1024]{2,1,0:T(8,128)(2,1)} %param.8) | copy-start | bytes 1572868
  4.4 28.6 %copy-start.1 = (s32[7]{0:T(128)S(1)}, s32[7]{0:T(128)}, u32[]{:S(2)}) copy-start(s32[7]{0:T(128)} %stack.28.meta_ref) | copy-start | bytes 88
  9.0 23.9 %collective-permute-start.1 = (bf16[8,2,128,128]{3,2,1,0:T(8,128)(2,1)}, bf16[8,2,128,128]{3,2,1,0:T(8,128)(2,1)S(1)}, u32[]{:S(2)}, u32[]{:S(2)}) collective-permute-start(bf16[8,2,128,128]{3,2,1,0:T(8,128)(2,1)} %get-tuple-element.32), channel_id=1, source_target_pairs={{0,2},{2,0},{4,6},{6,4},{8,10},{10,8},{12,14},{14,12},{16,18},{18,... | collective-permute-start | bytes 1572872 | tf_op jit(solution)/shard_map/ppermute | solution.py:425
  12.4 23.9 %collective-permute-start = (bf16[8,2,128,128]{3,2,1,0:T(8,128)(2,1)}, bf16[8,2,128,128]{3,2,1,0:T(8,128)(2,1)S(1)}, u32[]{:S(2)}, u32[]{:S(2)}) collective-permute-start(bf16[8,2,128,128]{3,2,1,0:T(8,128)(2,1)} %shard_map.84), channel_id=1, source_target_pairs={{2,4},{4,2},{6,8},{8,6},{10,12},{12,10},{14,16},{16,14},{18,20},{2... | collective-permute-start | bytes 1572872 | tf_op jit(solution)/shard_map/ppermute | solution.py:421
  13.1 34.7 %collective-permute-start.10 = (bf16[256,1024]{1,0:T(8,128)(2,1)S(1)}, bf16[256,1024]{1,0:T(8,128)(2,1)S(1)}, u32[]{:S(2)}, u32[]{:S(2)}) collective-permute-start(bf16[256,1024]{1,0:T(8,128)(2,1)S(1)} %bitcast.14), channel_id=1, source_target_pairs={{0,1},{1,0},{2,3},{3,2},{4,5},{5,4},{6,7},{7,6},{8,9},{9,8},{10,11... | collective-permute-start | bytes 1572872 | tf_op jit(solution)/shard_map/ppermute | solution.py:359
  15.8 46.9 %collective-permute-start.12 = (bf16[256,1024]{1,0:T(8,128)(2,1)S(1)}, bf16[256,1024]{1,0:T(8,128)(2,1)S(1)}, u32[]{:S(2)}, u32[]{:S(2)}) collective-permute-start(bf16[256,1024]{1,0:T(8,128)(2,1)S(1)} %collective-permute-done.11.refs_10_), channel_id=1, source_target_pairs={{0,1},{1,0},{2,3},{3,2},{4,5},{5,4},{6,7},{7,6},{8,9},{9,8},{10,11... | collective-permute-start | bytes 1572872 | tf_op jit(solution)/shard_map/ppermute | solution.py:359
  36.2 16.3 %collective-permute-start.7 = (bf16[512,128]{1,0:T(8,128)(2,1)S(1)}, bf16[512,128]{1,0:T(8,128)(2,1)S(1)}, u32[]{:S(2)}, u32[]{:S(2)}) collective-permute-start(bf16[512,128]{1,0:T(8,128)(2,1)S(1)} %get-tuple-element.45), channel_id=1, source_target_pairs={{0,4},{2,6},{4,0},{6,2},{8,12},{10,14},{12,8},{14,10},{16,20},{18,... | collective-permute-start | bytes 393224 | tf_op jit(solution)/shard_map/ppermute | solution.py:355
  36.3 18.6 %collective-permute-start.8 = (bf16[512,128]{1,0:T(8,128)(2,1)S(1)}, bf16[512,128]{1,0:T(8,128)(2,1)S(1)}, u32[]{:S(2)}, u32[]{:S(2)}) collective-permute-start(bf16[512,128]{1,0:T(8,128)(2,1)S(1)} %get-tuple-element.44.refs_4_), channel_id=1, source_target_pairs={{0,1},{1,0},{2,3},{3,2},{4,5},{5,4},{6,7},{7,6},{8,9},{9,8},{10,11... | collective-permute-start | bytes 393224 | tf_op jit(solution)/shard_map/ppermute | solution.py:359
  41.8 40.8 %collective-permute-start.2 = (bf16[8,2,128,128]{3,2,1,0:T(8,128)(2,1)S(1)}, bf16[8,2,128,128]{3,2,1,0:T(8,128)(2,1)S(1)}, u32[]{:S(2)}, u32[]{:S(2)}) collective-permute-start(bf16[8,2,128,128]{3,2,1,0:T(8,128)(2,1)S(1)} %get-tuple-element.35), channel_id=1, source_target_pairs={{2,4},{4,2},{6,8},{8,6},{10,12},{12,10},{14,16},{16,14},{18,20},{2... | collective-permute-start | bytes 1572872 | tf_op jit(solution)/shard_map/ppermute | solution.py:432
  47.8 38.9 %collective-permute-start.3 = (bf16[8,2,128,128]{3,2,1,0:T(8,128)(2,1)S(1)}, bf16[8,2,128,128]{3,2,1,0:T(8,128)(2,1)S(1)}, u32[]{:S(2)}, u32[]{:S(2)}) collective-permute-start(bf16[8,2,128,128]{3,2,1,0:T(8,128)(2,1)S(1)} %get-tuple-element.39), channel_id=1, source_target_pairs={{0,2},{2,0},{4,6},{6,4},{8,10},{10,8},{12,14},{14,12},{16,18},{18,... | collective-permute-start | bytes 1572872 | tf_op jit(solution)/shard_map/ppermute | solution.py:443
  52.5 8.7 %collective-permute-start.4 = (bf16[512,128]{1,0:T(8,128)(2,1)S(1)}, bf16[512,128]{1,0:T(8,128)(2,1)S(1)}, u32[]{:S(2)}, u32[]{:S(2)}) collective-permute-start(bf16[512,128]{1,0:T(8,128)(2,1)S(1)} %get-tuple-element.43), channel_id=1, source_target_pairs={{0,4},{2,6},{4,0},{6,2},{8,12},{10,14},{12,8},{14,10},{16,20},{18,... | collective-permute-start | bytes 393224 | tf_op jit(solution)/shard_map/ppermute | solution.py:355
  54.9 6.3 %collective-permute-start.5 = (bf16[512,128]{1,0:T(8,128)(2,1)S(1)}, bf16[512,128]{1,0:T(8,128)(2,1)S(1)}, u32[]{:S(2)}, u32[]{:S(2)}) collective-permute-start(bf16[512,128]{1,0:T(8,128)(2,1)S(1)} %get-tuple-element.42.refs_0_), channel_id=1, source_target_pairs={{0,1},{1,0},{2,3},{3,2},{4,5},{5,4},{6,7},{7,6},{8,9},{9,8},{10,11... | collective-permute-start | bytes 393224 | tf_op jit(solution)/shard_map/ppermute | solution.py:359
  61.2 1.3 %collective-permute-start.9 = (bf16[512,128]{1,0:T(8,128)(2,1)S(1)}, bf16[512,128]{1,0:T(8,128)(2,1)S(1)}, u32[]{:S(2)}, u32[]{:S(2)}) collective-permute-start(bf16[512,128]{1,0:T(8,128)(2,1)S(1)} %collective-permute-done.7.refs_5_), channel_id=1, source_target_pairs={{0,1},{1,0},{2,3},{3,2},{4,5},{5,4},{6,7},{7,6},{8,9},{9,8},{10,11... | collective-permute-start | bytes 393224 | tf_op jit(solution)/shard_map/ppermute | solution.py:359
  61.2 1.5 %collective-permute-start.6 = (bf16[512,128]{1,0:T(8,128)(2,1)S(1)}, bf16[512,128]{1,0:T(8,128)(2,1)S(1)}, u32[]{:S(2)}, u32[]{:S(2)}) collective-permute-start(bf16[512,128]{1,0:T(8,128)(2,1)S(1)} %collective-permute-done.4.refs_1_), channel_id=1, source_target_pairs={{0,1},{1,0},{2,3},{3,2},{4,5},{5,4},{6,7},{7,6},{8,9},{9,8},{10,11... | collective-permute-start | bytes 393224 | tf_op jit(solution)/shard_map/ppermute | solution.py:359
  64.0 22.7 %copy-start.2 = (s32[7]{0:T(128)S(1)}, s32[7]{0:T(128)}, u32[]{:S(2)}) copy-start(s32[7]{0:T(128)} %stack.28.meta_ref) | copy-start | bytes 88
  64.0 10.4 %collective-permute-start.13 = (bf16[128,512]{1,0:T(8,128)(2,1)S(1)}, bf16[128,512]{1,0:T(8,128)(2,1)S(1)}, u32[]{:S(2)}, u32[]{:S(2)}) collective-permute-start(bf16[128,512]{1,0:T(8,128)(2,1)S(1)} %get-tuple-element.47), channel_id=1, source_target_pairs={{0,8},{2,10},{4,12},{6,14},{8,0},{10,2},{12,4},{14,6},{16,24},{18,... | collective-permute-start | bytes 393224 | tf_op jit(solution)/shard_map/ppermute | solution.py:355
  68.4 12.9 %collective-permute-start.14 = (bf16[128,512]{1,0:T(8,128)(2,1)S(1)}, bf16[128,512]{1,0:T(8,128)(2,1)S(1)}, u32[]{:S(2)}, u32[]{:S(2)}) collective-permute-start(bf16[128,512]{1,0:T(8,128)(2,1)S(1)} %get-tuple-element.48), channel_id=1, source_target_pairs={{0,16},{2,18},{4,20},{6,22},{8,24},{10,26},{12,28},{14,30},{16,0},... | collective-permute-start | bytes 393224 | tf_op jit(solution)/shard_map/ppermute | solution.py:355
  71.1 10.3 %collective-permute-start.15 = (bf16[128,512]{1,0:T(8,128)(2,1)S(1)}, bf16[128,512]{1,0:T(8,128)(2,1)S(1)}, u32[]{:S(2)}, u32[]{:S(2)}) collective-permute-start(bf16[128,512]{1,0:T(8,128)(2,1)S(1)} %get-tuple-element.49), channel_id=1, source_target_pairs={{0,24},{2,26},{4,28},{6,30},{8,16},{10,18},{12,20},{14,22},{16,8},... | collective-permute-start | bytes 393224 | tf_op jit(solution)/shard_map/ppermute | solution.py:355
  82.0 7.2 %collective-permute-start.16 = (bf16[64,512]{1,0:T(8,128)(2,1)S(1)}, bf16[64,512]{1,0:T(8,128)(2,1)S(1)}, u32[]{:S(2)}, u32[]{:S(2)}) collective-permute-start(bf16[64,512]{1,0:T(8,128)(2,1)S(1)} %get-tuple-element.51), channel_id=1, source_target_pairs={{0,2},{2,0},{4,6},{6,4},{8,10},{10,8},{12,14},{14,12},{16,18},{18,... | collective-permute-start | bytes 196616 | tf_op jit(solution)/shard_map/ppermute | solution.py:355
  82.6 0.8 copy-start.3

commit v7 on v6

--- a/solution.py
+++ b/solution.py
@@ -54,8 +54,10 @@
         some = pl.ds(0, early) if group == 0 else pl.ds(early, pairs - early)
         these = pl.ds(0, len(kinds))
         found = [(thin_hbm.at[some, these, side], one_ref.at[some])]
-        for place, source in enumerate((rim_hbm.at[some], thick_hbm.at[some, :, side], thick_hbm.at[some, :, 1 - side])):
-            found.append((source, wide_ref.at[some, :, pl.ds(place * HALF, HALF)]))
+        sources = (rim_hbm.at[some] if second else None, thick_hbm.at[some, :, side], thick_hbm.at[some, :, 1 - side])
+        for place, source in enumerate(sources):
+            if source is not None:
+                found.append((source, wide_ref.at[some, :, pl.ds(place * HALF, HALF)]))
         return [pltpu.make_async_copy(a, b, in_sem.at[group, place]) for place, (a, b) in enumerate(found)]
 
     def stores(group):
@@ -67,6 +69,10 @@
         pair = pair_of(number)
         slot = number % 3
         first_head = lax.broadcasted_iota(jnp.int32, (HALF, PAIR), 1) < HEAD_DIM
+        if not second:
+            cols = pl.ds(pl.multiple_of(pair * PAIR, PAIR), PAIR)
+            for which in range(2):
+                wide_ref[pair, which, :HALF] = rim_hbm[which, :, cols]
         for which in kinds:
             one = one_ref[pair, which].astype(f32) * (1.0 if which else scale)
             two_ref[slot, which, :HALF] = jnp.where(first_head, one, 0.0).astype(bf16)
@@ -175,7 +181,7 @@
         ]
     return pl.pallas_call(
         functools.partial(half_kernel, second=second, front=front, back=back),
-        in_specs=[in_smem, in_hbm, in_hbm, pl.BlockSpec(memory_space=pl.ANY)],
+        in_specs=[in_smem, in_hbm, in_hbm, pl.BlockSpec(memory_space=pl.ANY) if second else in_vmem],
         out_specs=out_specs,
         out_shape=out_shape,
         scratch_shapes=scratch,
@@ -185,25 +191,25 @@
     )(meta, *held, rim)
 
 
-def rim_kernel(side_ref, k_ref, v_ref, out_ref):
-    for pair in range(out_ref.shape[0]):
-        cols = slice(pair * PAIR, (pair + 1) * PAIR)
-        out_ref[pair, 0] = k_ref[:, cols]
-        out_ref[pair, 1] = v_ref[:, cols]
+def rim_kernel(side_ref, k_hbm, v_hbm, out_ref, sems):
+    rows = pl.ds(pl.multiple_of(side_ref[0] * HALF, HALF), HALF)
+    copies = [pltpu.make_async_copy(ref.at[rows, :], out_ref.at[which], sems.at[which]) for which, ref in enumerate((k_hbm, v_hbm))]
+    for copy in copies:
+        copy.start()
+    for copy in copies:
+        copy.wait()
 
 
 def packed_rim(side, k, v):
-    width = k.shape[1]
-    block = pl.BlockSpec((HALF, width), lambda i, s: (s[0], 0))
-    shape = (width // PAIR, 2, HALF, PAIR)
+    in_hbm = pl.BlockSpec(memory_space=pltpu.HBM)
     return pl.pallas_call(
         rim_kernel,
-        grid_spec=pltpu.PrefetchScalarGridSpec(
-            num_scalar_prefetch=1, grid=(1,), in_specs=[block, block],
-            out_specs=pl.BlockSpec(shape, lambda i, s: (0, 0, 0, 0)),
-        ),
-        out_shape=jax.ShapeDtypeStruct(shape, bf16),
-    )(side, k, v)
+        in_specs=[in_smem, in_hbm, in_hbm],
+        out_specs=in_vmem,
+        out_shape=jax.ShapeDtypeStruct((2, HALF, k.shape[1]), bf16),
+        scratch_shapes=[pltpu.SemaphoreType.DMA((2,))],
+        compiler_params=pltpu.CompilerParams(vmem_limit_bytes=4 << 20),
+    )(side, *[pltpu.with_memory_space_constraint(array, pltpu.HBM) for array in (k, v)])
 
 
 def prepare_kernel(meta_ref, q_ref, k_ref, v_ref, g_ref, w_ref, thin_ref, thick_ref, rim_ref):

time: 90.5 us -> 90.5 us (level)
  transfers between devices with their start and end apart: 17 -> 17, of which waited for: 7 -> 7; matrix products, arithmetic and copies ran while one was open for 1% -> 1% of each run, Pallas kernels for 31% -> 30%
where the time goes in v7:
time: 90.5 us; the launch traced here: 89.9 us
  waiting for transfers between devices  38.2 us (42%)
  Pallas kernels  27.3 us (30%)
  starting transfers between devices  21.4 us (24%)
  local copies, waits for them, and re-layouts  1.49 us (2%)
    ppermute x7, waiting for transfers between devices, swapped(): return lax.ppermute(value, 'seq', [(i, i ^ stride) for i in range(count)])  20.1 us
    ppermute x1, waiting for transfers between devices, on_device(): second_rim = lax.ppermute(rim2, 'seq', near_pairs)  17.1 us
    pallas_call x3, Pallas kernels, half_attention(): pl.pallas_call(functools.partial(half_kernel, second=second, front=front,...  14 us
    ppermute x7, starting transfers between devices, swapped(): return lax.ppermute(value, 'seq', [(i, i ^ stride) for i in range(count)])  13.2 us
    ppermute x1, starting transfers between devices, on_device(): from_near = lax.ppermute(back2, 'seq', near_pairs)  4.67 us
    pallas_call x1, Pallas kernels, prepared(): pl.pallas_call(prepare_kernel, in_specs=[in_smem] + [in_vmem] * 5, out_sp...  4.62 us
    pallas_call x1, Pallas kernels, joined(): pl.pallas_call(join_kernel, in_specs=[in_smem] + [in_vmem] * 5, out_specs...  3.32 us
    pallas_call x1, Pallas kernels, finished(): pl.pallas_call(finish_kernel, in_specs=[in_smem, in_hbm, in_hbm, in_vmem]...  2.39 us
  transfers between devices with their start and end apart: 17, of which 7 were waited for; matrix products, arithmetic and copies ran while one was open for 1% of the time, Pallas kernels for 30%

profile of v7, /device:TPU:0, one launch (start us, length us, event | category | flops | bytes accessed | tf_op | source)
XLA Modules:
  0.0 89.9 jit_solution(14678713388427754328)
XLA Ops:
  0.6 3.1 %collective-permute-start.11 = (bf16[256,1024]{1,0:T(8,128)(2,1)}, bf16[256,1024]{1,0:T(8,128)(2,1)S(1)}, u32[]{:S(2)}, u32[]{:S(2)}) collective-permute-start(bf16[256,1024]{1,0:T(8,128)(2,1)} %bitcast.12), channel_id=1, source_target_pairs={{0,4},{2,6},{4,0},{6,2},{8,12},{10,14},{12,8},{14,10},{16,20},{18,... | collective-permute-start | bytes 1572872 | tf_op jit(solution)/shard_map/ppermute | solution.py:361
  3.7 0.7 stack.28.meta_ref
  4.4 0.0 copy-start
  4.4 0.0 copy-start.1
  4.4 4.6 %prepared.1 = (bf16[8,2,2,128,128]{4,3,2,1,0:T(8,128)(2,1)}, bf16[8,2,2,128,128]{4,3,2,1,0:T(8,128)(2,1)}, bf16[8,2,128,128]{3,2,1,0:T(8,128)(2,1)}) custom-call(s32[7]{0:T(128)} %stack.28.meta_ref, bf16[256,1024]{1,0:T(8,128)(2,1)} %bitcast.20, bf16[256,1024]{1,0:T(8,128)(2,1)} %bitcast.16, bf16[256,1024]{1,0:T(8,128)(2,1)} %bitcast.18, ...), custom_call_target="tpu_custom_call" | custom-call | flops 536870912 | bytes 5767168 | tf_op jit(solution)/shard_map/prepared/pallas_call | solution.py:239
  9.0 1.5 %collective-permute-start.1 = (bf16[8,2,128,128]{3,2,1,0:T(8,128)(2,1)}, bf16[8,2,128,128]{3,2,1,0:T(8,128)(2,1)S(1)}, u32[]{:S(2)}, u32[]{:S(2)}) collective-permute-start(bf16[8,2,128,128]{3,2,1,0:T(8,128)(2,1)} %get-tuple-element.32), channel_id=1, source_target_pairs={{0,2},{2,0},{4,6},{6,4},{8,10},{10,8},{12,14},{14,12},{16,18},{18,... | collective-permute-start | bytes 1572872 | tf_op jit(solution)/shard_map/ppermute | solution.py:431
  10.5 1.0 %shard_map.84 = bf16[2,128,1024]{2,1,0:T(8,128)(2,1)S(1)} custom-call(s32[1]{0:T(128)} %bitcast.side_ref, bf16[256,1024]{1,0:T(8,128)(2,1)} %bitcast.17, bf16[256,1024]{1,0:T(8,128)(2,1)} %bitcast.19), custom_call_target="tpu_custom_call" | custom-call | tf_op jit(solution)/shard_map/pallas_call | solution.py:205
  11.5 0.7 collective-permute-start
  12.2 0.0 copy-done
  12.2 0.1 collective-permute-start.10
  12.3 3.5 %collective-permute-done.11.refs_10_ = bf16[256,1024]{1,0:T(8,128)(2,1)S(1)} collective-permute-done((bf16[256,1024]{1,0:T(8,128)(2,1)}, bf16[256,1024]{1,0:T(8,128)(2,1)S(1)}, u32[]{:S(2)}, u32[]{:S(2)}) %collective-permute-start.11) | collective-permute-done | bytes 524320 | tf_op jit(solution)/shard_map/ppermute | solution.py:361
  15.8 0.0 collective-permute-start.12
  15.8 17.1 %collective-permute-done.1.rim_hbm = bf16[8,2,128,128]{3,2,1,0:T(8,128)(2,1)S(1)} collective-permute-done((bf16[8,2,128,128]{3,2,1,0:T(8,128)(2,1)}, bf16[8,2,128,128]{3,2,1,0:T(8,128)(2,1)S(1)}, u32[]{:S(2)}, u32[]{:S(2)}) %collective-permute-start.1) | collective-permute-done | bytes 524320 | tf_op jit(solution)/shard_map/ppermute | solution.py:431
  32.9 0.0 copy-done.1
  32.9 3.2 %shard_map.87 = (bf16[512,128]{1,0:T(8,128)(2,1)S(1)}, bf16[512,128]{1,0:T(8,128)(2,1)S(1)}) custom-call(s32[7]{0:T(128)S(1)} %copy-done.1, bf16[8,2,2,128,128]{4,3,2,1,0:T(8,128)(2,1)} %get-tuple-element.28.thin_hbm, bf16[8,2,2,128,128]{4,3,2,1,0:T(8,128)(2,1)} %get-tuple-element.29.thick_hbm, bf16[8,2,128,128]{3,2,1,0:T(8,128)(2,1)S(1)} %collective-permute-done.1.rim_hbm), custom_call_target="tpu_custom_call" | custom-call | flops 201326592 | bytes 4194304 | tf_op jit(solution)/shard_map/pallas_call | solution.py:182
  36.2 0.1 collective-permute-start.7
  36.3 0.1 collective-permute-start.8
  36.3 0.0 collective-permute-done.rim_hbm
  36.3 5.5 %shard_map.85 = (bf16[512,128]{1,0:T(8,128)(2,1)S(1)}, bf16[512,128]{1,0:T(8,128)(2,1)S(1)}, bf16[8,2,128,128]{3,2,1,0:T(8,128)(2,1)S(1)}, bf16[8,128,128]{2,1,0:T(8,128)(2,1)}, bf16[8,2,256,128]{3,2,1,0:T(8,128)(2,1)}) custom-call(s32[7]{0:T(128)S(1)} %copy-done.1, bf16[8,2,2,128,128]{4,3,2,1,0:T(8,128)(2,1)} %get-tuple-element.28.thin_hbm, ...), custom_call_target="tpu_custom_call" | custom-call | flops 603979776 | bytes 4194304 | tf_op jit(solution)/shard_map/pallas_call | solution.py:182
  41.9 0.7 collective-permute-start.2
  42.6 5.3 %shard_map.86 = (bf16[8,2,128,128]{3,2,1,0:T(8,128)(2,1)S(1)}, bf16[8,128,128]{2,1,0:T(8,128)(2,1)}, bf16[8,2,256,128]{3,2,1,0:T(8,128)(2,1)}) custom-call(s32[7]{0:T(128)S(1)} %copy-done.1, bf16[8,2,2,128,128]{4,3,2,1,0:T(8,128)(2,1)} %get-tuple-element.28.thin_hbm, bf16[8,2,2,128,128]{4,3,2,1,0:T(8,128)(2,1)} %get-tuple-element.29.thick_hbm, ...), custom_call_target="tpu_custom_call" | custom-call | flops 402653184 | bytes 4194304 | tf_op jit(solution)/shard_map/pallas_call | solution.py:182
  47.9 0.0 collective-permute-done.10.refs_9_
  47.9 4.7 %collective-permute-start.3 = (bf16[8,2,128,128]{3,2,1,0:T(8,128)(2,1)S(1)}, bf16[8,2,128,128]{3,2,1,0:T(8,128)(2,1)S(1)}, u32[]{:S(2)}, u32[]{:S(2)}) collective-permute-start(bf16[8,2,128,128]{3,2,1,0:T(8,128)(2,1)S(1)} %get-tuple-element.39), channel_id=1, source_target_pairs={{0,2},{2,0},{4,6},{6,4},{8,10},{10,8},{12,14},{14,12},{16,18},{18,... | collective-permute-start | bytes 1572872 | tf_op jit(solution)/shard_map/ppermute | solution.py:449
  52.6 0.0 collective-permute-done.7.refs_5_
  52.6 2.4 %collective-permute-start.4 = (bf16[512,128]{1,0:T(8,128)(2,1)S(1)}, bf16[512,128]{1,0:T(8,128)(2,1)S(1)}, u32[]{:S(2)}, u32[]{:S(2)}) collective-permute-start(bf16[512,128]{1,0:T(8,128)(2,1)S(1)} %get-tuple-element.43), channel_id=1, source_target_pairs={{0,4},{2,6},{4,0},{6,2},{8,12},{10,14},{12,8},{14,10},{16,20},{18,... | collective-permute-start | bytes 393224 | tf_op jit(solution)/shard_map/ppermute | solution.py:361
  55.0 0.0 collective-permute-done.8.refs_6_
  55.0 0.0 collective-permute-start.5
  55.0 6.3 %collective-permute-done.4.refs_1_ = bf16[512,128]{1,0:T(8,128)(2,1)S(1)} collective-permute-done((bf16[512,128]{1,0:T(8,128)(2,1)S(1)}, bf16[512,128]{1,0:T(8,128)(2,1)S(1)}, u32[]{:S(2)}, u32[]{:S(2)}) %collective-permute-start.4) | collective-permute-done | bytes 131104 | tf_op jit(solution)/shard_map/ppermute | solution.py:361
  61.3 0.0 collective-permute-start.9
  61.3 0.0 collective-permute-done.5.refs_2_
  61.3 0.5 collective-permute-start.6
  61.8 0.8 collective-permute-done.9.refs_7_
  62.6 0.2 collective-permute-done.6.refs_3_
  62.8 0.0 collective-permute-done.12.refs_11_
  62.8 1.3 %product.1 = (f32[128,512]{1,0:T(8,128)S(1)}, bf16[128,512]{1,0:T(8,128)(2,1)S(1)}, bf16[128,512]{1,0:T(8,128)(2,1)S(1)}, bf16[128,512]{1,0:T(8,128)(2,1)S(1)}) custom-call(s32[7]{0:T(128)S(1)} %copy-done.1, bf16[512,128]{1,0:T(8,128)(2,1)S(1)} %get-tuple-element.42.refs_0_, bf16[512,128]{1,0:T(8,128)(2,1)S(1)} %collective-permute-done.4.refs_1_, ...), custom_call_target="tpu_custom_call" | custom-call | tf_op jit(solution)/shard_map/product/pallas_call | solution.py:268
  64.1 0.0 copy-start.2
  64.1 4.4 %collective-permute-start.13 = (bf16[128,512]{1,0:T(8,128)(2,1)S(1)}, bf16[128,512]{1,0:T(8,128)(2,1)S(1)}, u32[]{:S(2)}, u32[]{:S(2)}) collective-permute-start(bf16[128,512]{1,0:T(8,128)(2,1)S(1)} %get-tuple-element.47), channel_id=1, source_target_pairs={{0,8},{2,10},{4,12},{6,14},{8,0},{10,2},{12,4},{14,6},{16,24},{18,... | collective-permute-start | bytes 393224 | tf_op jit(solution)/shard_map/ppermute | solution.py:361
  68.5 2.7 %collective-permute-start.14 = (bf16[128,512]{1,0:T(8,128)(2,1)S(1)}, bf16[128,512]{1,0:T(8,128)(2,1)S(1)}, u32[]{:S(2)}, u32[]{:S(2)}) collective-permute-start(bf16[128,512]{1,0:T(8,128)(2,1)S(1)} %get-tuple-element.48), channel_id=1, source_target_pairs={{0,16},{2,18},{4,20},{6,22},{8,24},{10,26},{12,28},{14,30},{16,0},... | collective-permute-start | bytes 393224 | tf_op jit(solution)/shard_map/ppermute | solution.py:361
  71.2 0.0 collective-permute-start.15
  71.2 3.4 %collective-permute-done.13.refs_0_ = bf16[128,512]{1,0:T(8,128)(2,1)S(1)} collective-permute-done((bf16[128,512]{1,0:T(8,128)(2,1)S(1)}, bf16[128,512]{1,0:T(8,128)(2,1)S(1)}, u32[]{:S(2)}, u32[]{:S(2)}) %collective-permute-start.13) | collective-permute-done | bytes 131104 | tf_op jit(solution)/shard_map/ppermute | solution.py:361
  74.6 6.9 %collective-permute-done.14.refs_1_ = bf16[128,512]{1,0:T(8,128)(2,1)S(1)} collective-permute-done((bf16[128,512]{1,0:T(8,128)(2,1)S(1)}, bf16[128,512]{1,0:T(8,128)(2,1)S(1)}, u32[]{:S(2)}, u32[]{:S(2)}) %collective-permute-start.14) | collective-permute-done | bytes 131104 | tf_op jit(solution)/shard_map/ppermute | solution.py:361
  81.4 0.0 collective-permute-done.15.refs_2_
  81.4 0.6 summed.1
  82.1 0.6 collective-permute-start.16
  82.7 0.0 collective-permute-done.2.rim_ref
  82.7 0.0 copy-start.3
  82.7 0.8 copy-done.3
  83.5 3.3 %joined.1 = (bf16[256,1024]{1,0:T(8,128)(2,1)}, bf16[256,1024]{1,0:T(8,128)(2,1)}, bf16[256,1024]{1,0:T(8,128)(2,1)}) custom-call(s32[7]{0:T(128)} %stack.28.meta_ref, bf16[8,128,128]{2,1,0:T(8,128)(2,1)} %get-tuple-element.30.dq1_ref, bf16[8,2,256,128]{3,2,1,0:T(8,128)(2,1)} %get-tuple-element.31.own1_ref, bf16[8,128,128]{2,1,0:T(8,128)(2,1)} %get-tuple-element.33.dq2_ref, ...), custom_call_target="tpu_custom_call" | custom-call | flops 1572864 | bytes 4194304 | tf_op jit(solution)/shard_map/joined/pallas_call | solution.py:317
  86.8 0.0 collective-permute-done.3.rim_ref
  86.8 0.0 copy-done.2
  86.8 2.4 %finished.1 = (bf16[256,1024]{1,0:T(8,128)(2,1)}, bf16[256,1024]{1,0:T(8,128)(2,1)}) custom-call(s32[7]{0:T(128)S(1)} %copy-done.2, bf16[256,1024]{1,0:T(8,128)(2,1)} %get-tuple-element.37.dk_hbm, bf16[256,1024]{1,0:T(8,128)(2,1)} %get-tuple-element.38.dv_hbm, ...), custom_call_target="tpu_custom_call", output_to_operand_aliasing={{0}: (1, {}), {1}: (2, {})} | custom-call | flops 262144 | bytes 1572864 | tf_op jit(solution)/shard_map/finished/pallas_call | solution.py:347
  89.2 0.0 collective-permute-done.16
  89.2 0.7 add_multiply_fusion
Async XLA Ops:
  0.6 15.2 %collective-permute-start.11 = (bf16[256,1024]{1,0:T(8,128)(2,1)}, bf16[256,1024]{1,0:T(8,128)(2,1)S(1)}, u32[]{:S(2)}, u32[]{:S(2)}) collective-permute-start(bf16[256,1024]{1,0:T(8,128)(2,1)} %bitcast.12), channel_id=1, source_target_pairs={{0,4},{2,6},{4,0},{6,2},{8,12},{10,14},{12,8},{14,10},{16,20},{18,... | collective-permute-start | bytes 1572872 | tf_op jit(solution)/shard_map/ppermute | solution.py:361
  4.4 7.9 %copy-start = (bf16[1,256,1024]{2,1,0:T(8,128)(2,1)S(1)}, bf16[1,256,1024]{2,1,0:T(8,128)(2,1)}, u32[]{:S(2)}) copy-start(bf16[1,256,1024]{2,1,0:T(8,128)(2,1)} %param.8) | copy-start | bytes 1572868
  4.4 28.6 %copy-start.1 = (s32[7]{0:T(128)S(1)}, s32[7]{0:T(128)}, u32[]{:S(2)}) copy-start(s32[7]{0:T(128)} %stack.28.meta_ref) | copy-start | bytes 88
  9.0 23.9 %collective-permute-start.1 = (bf16[8,2,128,128]{3,2,1,0:T(8,128)(2,1)}, bf16[8,2,128,128]{3,2,1,0:T(8,128)(2,1)S(1)}, u32[]{:S(2)}, u32[]{:S(2)}) collective-permute-start(bf16[8,2,128,128]{3,2,1,0:T(8,128)(2,1)} %get-tuple-element.32), channel_id=1, source_target_pairs={{0,2},{2,0},{4,6},{6,4},{8,10},{10,8},{12,14},{14,12},{16,18},{18,... | collective-permute-start | bytes 1572872 | tf_op jit(solution)/shard_map/ppermute | solution.py:431
  11.5 24.8 %collective-permute-start = (bf16[2,128,1024]{2,1,0:T(8,128)(2,1)S(1)}, bf16[2,128,1024]{2,1,0:T(8,128)(2,1)S(1)}, u32[]{:S(2)}, u32[]{:S(2)}) collective-permute-start(bf16[2,128,1024]{2,1,0:T(8,128)(2,1)S(1)} %shard_map.84), channel_id=1, source_target_pairs={{2,4},{4,2},{6,8},{8,6},{10,12},{12,10},{14,16},{16,14},{18,20},{2... | collective-permute-start | bytes 1572872 | tf_op jit(solution)/shard_map/ppermute | solution.py:427
  12.2 35.6 %collective-permute-start.10 = (bf16[256,1024]{1,0:T(8,128)(2,1)S(1)}, bf16[256,1024]{1,0:T(8,128)(2,1)S(1)}, u32[]{:S(2)}, u32[]{:S(2)}) collective-permute-start(bf16[256,1024]{1,0:T(8,128)(2,1)S(1)} %bitcast.14), channel_id=1, source_target_pairs={{0,1},{1,0},{2,3},{3,2},{4,5},{5,4},{6,7},{7,6},{8,9},{9,8},{10,11... | collective-permute-start | bytes 1572872 | tf_op jit(solution)/shard_map/ppermute | solution.py:365
  15.8 47.0 %collective-permute-start.12 = (bf16[256,1024]{1,0:T(8,128)(2,1)S(1)}, bf16[256,1024]{1,0:T(8,128)(2,1)S(1)}, u32[]{:S(2)}, u32[]{:S(2)}) collective-permute-start(bf16[256,1024]{1,0:T(8,128)(2,1)S(1)} %collective-permute-done.11.refs_10_), channel_id=1, source_target_pairs={{0,1},{1,0},{2,3},{3,2},{4,5},{5,4},{6,7},{7,6},{8,9},{9,8},{10,11... | collective-permute-start | bytes 1572872 | tf_op jit(solution)/shard_map/ppermute | solution.py:365
  36.2 16.4 %collective-permute-start.7 = (bf16[512,128]{1,0:T(8,128)(2,1)S(1)}, bf16[512,128]{1,0:T(8,128)(2,1)S(1)}, u32[]{:S(2)}, u32[]{:S(2)}) collective-permute-start(bf16[512,128]{1,0:T(8,128)(2,1)S(1)} %get-tuple-element.45), channel_id=1, source_target_pairs={{0,4},{2,6},{4,0},{6,2},{8,12},{10,14},{12,8},{14,10},{16,20},{18,... | collective-permute-start | bytes 393224 | tf_op jit(solution)/shard_map/ppermute | solution.py:361
  36.3 18.7 %collective-permute-start.8 = (bf16[512,128]{1,0:T(8,128)(2,1)S(1)}, bf16[512,128]{1,0:T(8,128)(2,1)S(1)}, u32[]{:S(2)}, u32[]{:S(2)}) collective-permute-start(bf16[512,128]{1,0:T(8,128)(2,1)S(1)} %get-tuple-element.44.refs_4_), channel_id=1, source_target_pairs={{0,1},{1,0},{2,3},{3,2},{4,5},{5,4},{6,7},{7,6},{8,9},{9,8},{10,11... | collective-permute-start | bytes 393224 | tf_op jit(solution)/shard_map/ppermute | solution.py:365
  41.9 40.8 %collective-permute-start.2 = (bf16[8,2,128,128]{3,2,1,0:T(8,128)(2,1)S(1)}, bf16[8,2,128,128]{3,2,1,0:T(8,128)(2,1)S(1)}, u32[]{:S(2)}, u32[]{:S(2)}) collective-permute-start(bf16[8,2,128,128]{3,2,1,0:T(8,128)(2,1)S(1)} %get-tuple-element.35), channel_id=1, source_target_pairs={{2,4},{4,2},{6,8},{8,6},{10,12},{12,10},{14,16},{16,14},{18,20},{2... | collective-permute-start | bytes 1572872 | tf_op jit(solution)/shard_map/ppermute | solution.py:438
  47.9 38.9 %collective-permute-start.3 = (bf16[8,2,128,128]{3,2,1,0:T(8,128)(2,1)S(1)}, bf16[8,2,128,128]{3,2,1,0:T(8,128)(2,1)S(1)}, u32[]{:S(2)}, u32[]{:S(2)}) collective-permute-start(bf16[8,2,128,128]{3,2,1,0:T(8,128)(2,1)S(1)} %get-tuple-element.39), channel_id=1, source_target_pairs={{0,2},{2,0},{4,6},{6,4},{8,10},{10,8},{12,14},{14,12},{16,18},{18,... | collective-permute-start | bytes 1572872 | tf_op jit(solution)/shard_map/ppermute | solution.py:449
  52.6 8.7 %collective-permute-start.4 = (bf16[512,128]{1,0:T(8,128)(2,1)S(1)}, bf16[512,128]{1,0:T(8,128)(2,1)S(1)}, u32[]{:S(2)}, u32[]{:S(2)}) collective-permute-start(bf16[512,128]{1,0:T(8,128)(2,1)S(1)} %get-tuple-element.43), channel_id=1, source_target_pairs={{0,4},{2,6},{4,0},{6,2},{8,12},{10,14},{12,8},{14,10},{16,20},{18,... | collective-permute-start | bytes 393224 | tf_op jit(solution)/shard_map/ppermute | solution.py:361
  55.0 6.3 %collective-permute-start.5 = (bf16[512,128]{1,0:T(8,128)(2,1)S(1)}, bf16[512,128]{1,0:T(8,128)(2,1)S(1)}, u32[]{:S(2)}, u32[]{:S(2)}) collective-permute-start(bf16[512,128]{1,0:T(8,128)(2,1)S(1)} %get-tuple-element.42.refs_0_), channel_id=1, source_target_pairs={{0,1},{1,0},{2,3},{3,2},{4,5},{5,4},{6,7},{7,6},{8,9},{9,8},{10,11... | collective-permute-start | bytes 393224 | tf_op jit(solution)/shard_map/ppermute | solution.py:365
  61.3 1.3 %collective-permute-start.9 = (bf16[512,128]{1,0:T(8,128)(2,1)S(1)}, bf16[512,128]{1,0:T(8,128)(2,1)S(1)}, u32[]{:S(2)}, u32[]{:S(2)}) collective-permute-start(bf16[512,128]{1,0:T(8,128)(2,1)S(1)} %collective-permute-done.7.refs_5_), channel_id=1, source_target_pairs={{0,1},{1,0},{2,3},{3,2},{4,5},{5,4},{6,7},{7,6},{8,9},{9,8},{10,11... | collective-permute-start | bytes 393224 | tf_op jit(solution)/shard_map/ppermute | solution.py:365
  61.3 1.5 %collective-permute-start.6 = (bf16[512,128]{1,0:T(8,128)(2,1)S(1)}, bf16[512,128]{1,0:T(8,128)(2,1)S(1)}, u32[]{:S(2)}, u32[]{:S(2)}) collective-permute-start(bf16[512,128]{1,0:T(8,128)(2,1)S(1)} %collective-permute-done.4.refs_1_), channel_id=1, source_target_pairs={{0,1},{1,0},{2,3},{3,2},{4,5},{5,4},{6,7},{7,6},{8,9},{9,8},{10,11... | collective-permute-start | bytes 393224 | tf_op jit(solution)/shard_map/ppermute | solution.py:365
  64.1 22.7 %copy-start.2 = (s32[7]{0:T(128)S(1)}, s32[7]{0:T(128)}, u32[]{:S(2)}) copy-start(s32[7]{0:T(128)} %stack.28.meta_ref) | copy-start | bytes 88
  64.1 10.5 %collective-permute-start.13 = (bf16[128,512]{1,0:T(8,128)(2,1)S(1)}, bf16[128,512]{1,0:T(8,128)(2,1)S(1)}, u32[]{:S(2)}, u32[]{:S(2)}) collective-permute-start(bf16[128,512]{1,0:T(8,128)(2,1)S(1)} %get-tuple-element.47), channel_id=1, source_target_pairs={{0,8},{2,10},{4,12},{6,14},{8,0},{10,2},{12,4},{14,6},{16,24},{18,... | collective-permute-start | bytes 393224 | tf_op jit(solution)/shard_map/ppermute | solution.py:361
  68.5 12.9 %collective-permute-start.14 = (bf16[128,512]{1,0:T(8,128)(2,1)S(1)}, bf16[128,512]{1,0:T(8,128)(2,1)S(1)}, u32[]{:S(2)}, u32[]{:S(2)}) collective-permute-start(bf16[128,512]{1,0:T(8,128)(2,1)S(1)} %get-tuple-element.48), channel_id=1, source_target_pairs={{0,16},{2,18},{4,20},{6,22},{8,24},{10,26},{12,28},{14,30},{16,0},... | collective-permute-start | bytes 393224 | tf_op jit(solution)/shard_map/ppermute | solution.py:361
  71.2 10.3 %collective-permute-start.15 = (bf16[128,512]{1,0:T(8,128)(2,1)S(1)}, bf16[128,512]{1,0:T(8,128)(2,1)S(1)}, u32[]{:S(2)}, u32[]{:S(2)}) collective-permute-start(bf16[128,512]{1,0:T(8,128)(2,1)S(1)} %get-tuple-element.49), channel_id=1, source_target_pairs={{0,24},{2,26},{4,28},{6,30},{8,16},{10,18},{12,20},{14,22},{16,8},... | collective-permute-start | bytes 393224 | tf_op jit(solution)/shard_map/ppermute | solution.py:361
  82.1 7.2 %collective-permute-start.16 = (bf16[64,512]{1,0:T(8,128)(2,1)S(1)}, bf16[64,512]{1,0:T(8,128)(2,1)S(1)}, u32[]{:S(2)}, u32[]{:S(2)}) collective-permute-start(bf16[64,512]{1,0:T(8,128)(2,1)S(1)} %get-tuple-element.51), channel_id=1, source_target_pairs={{0,2},{2,0},{4,6},{6,4},{8,10},{10,8},{12,14},{14,12},{16,18},{18,... | collective-permute-start | bytes 196616 | tf_op jit(solution)/shard_map/ppermute | solution.py:361
  82.7 0.8 copy-start.3
